TPU v7x, 32 devices: a whole 2x2x4 slice. The times are simulated.
32 devices in a mesh: gx: 8 (over y, x, core), gy: 4 (over z).
Axes of the slice: x: 2, y: 2, z: 4, core: 2. Of those that a mesh axis runs over, the one named last changes fastest.
Arguments:
- image_tokens: bfloat16 [16, 32, 32, 1152], P('gx', None, 'gy'), may hold values from -6 to 6
- text_tokens: bfloat16 [16, 80, 1152], P('gx', 'gy'), may hold values from -6 to 6
- image_skip: bfloat16 [16, 32, 32, 1152], P('gx', None, 'gy'), may hold values from -6 to 6
- text_skip: bfloat16 [16, 80, 1152], P('gx', 'gy'), may hold values from -6 to 6
- time_steps: int32 [16], P('gx'), may hold values from 0 to 999
- caption_len: int32 [16], P('gx'), may hold values from 1 to 77, as said below
- pred_grad: float32 [16, 4, 64, 64], P('gx', None, None, 'gy'), may hold values from -6 to 6
- text_grad: float32 [16, 80, 1152], P('gx', 'gy'), may hold values from -6 to 6
- w_skip: bfloat16 [2304, 1152], replicated, may hold values from -0.125 to 0.125
- b_skip: float32 [1152], replicated, may hold values from -1.8 to 1.8
- gain_attn: float32 [1152], replicated, may hold values from 0.5 to 1.5
- bias_attn: float32 [1152], replicated, may hold values from -1.8 to 1.8
- w_qkv: bfloat16 [1152, 3456], replicated, may hold values from -0.25 to 0.25
- w_proj: bfloat16 [1152, 1152], replicated, may hold values from -1 to 1
- b_proj: float32 [1152], replicated, may hold values from -1.8 to 1.8
- gain_mlp: float32 [1152], replicated, may hold values from 0.5 to 1.5
- bias_mlp: float32 [1152], replicated, may hold values from -1.8 to 1.8
- w_up: bfloat16 [1152, 4608], replicated, may hold values from -0.1875 to 0.1875
- b_up: float32 [4608], replicated, may hold values from -1.8 to 1.8
- w_down: bfloat16 [4608, 1152], replicated, may hold values from -0.09375 to 0.09375
- b_down: float32 [1152], replicated, may hold values from -1.8 to 1.8
- gain_head: float32 [1152], replicated, may hold values from 0.5 to 1.5
- bias_head: float32 [1152], replicated, may hold values from -1.8 to 1.8
- w_head: bfloat16 [1152, 16], replicated, may hold values from -0.1875 to 0.1875
- b_head: float32 [16], replicated, may hold values from -1.8 to 1.8
- w_conv: float32 [4, 4, 3, 3], replicated, may hold values from -1 to 1
- b_conv: float32 [4], replicated, may hold values from -1.8 to 1.8
Outputs:
- prediction: float32 [16, 4, 64, 64], P('gx', None, None, 'gy')
- text_out: bfloat16 [16, 80, 1152], P('gx', 'gy')
- grad_image: float32 [16, 32, 32, 1152], P('gx', None, 'gy')
- grad_text: float32 [16, 80, 1152], P('gx', 'gy')
- grad_image_skip: float32 [16, 32, 32, 1152], P('gx', None, 'gy')
- grad_text_skip: float32 [16, 80, 1152], P('gx', 'gy')
- grad_w_skip: float32 [2304, 1152], P(('gx', 'gy'))
- grad_b_skip: float32 [1152], P(('gx', 'gy'))
- grad_gain_attn: float32 [1152], P(('gx', 'gy'))
- grad_bias_attn: float32 [1152], P(('gx', 'gy'))
- grad_w_qkv: float32 [1152, 3456], P(('gx', 'gy'))
- grad_w_proj: float32 [1152, 1152], P(('gx', 'gy'))
- grad_b_proj: float32 [1152], P(('gx', 'gy'))
- grad_gain_mlp: float32 [1152], P(('gx', 'gy'))
- grad_bias_mlp: float32 [1152], P(('gx', 'gy'))
- grad_w_up: float32 [1152, 4608], P(('gx', 'gy'))
- grad_b_up: float32 [4608], P(('gx', 'gy'))
- grad_w_down: float32 [4608, 1152], P(('gx', 'gy'))
- grad_b_down: float32 [1152], P(('gx', 'gy'))
- grad_gain_head: float32 [1152], P(('gx', 'gy'))
- grad_bias_head: float32 [1152], P(('gx', 'gy'))
- grad_w_head: float32 [1152, 16], P(('gx', 'gy'))
- grad_b_head: float32 [16], replicated
- grad_w_conv: float32 [4, 4, 3, 3], replicated
- grad_b_conv: float32 [4], replicated
Inputs may be any that keep to these rules, and one draw needn't show every extreme that they name: `caption_len`: caption tokens of each item that are attended to; some item has all 77.
All inputs are finite; a program needn't handle non-finite values.
Results may differ from a plain program's by a relative error of at most 0.017.
Values may be sent and summed in bfloat16 or wider, within the bound.
No kernel may reach another device: no remote copies, remote signals or barrier semaphores. Data moves between devices by JAX's collectives and lax.ppermute only.
A program may use at most 320 MiB of HBM per device.

v0:
```python
from functools import partial
import math

import jax
import jax.numpy as jnp
from jax import lax
from jax.sharding import PartitionSpec as P

HEADS = 16
HEAD_DIM = 72
LAT_CH = 4
PATCH = 2


EPSILON = 1e-05
HIGHEST = lax.Precision.HIGHEST


def with_halo(block, sides, width):
    for axis, dim in sides:
        count = lax.axis_size(axis)
        forward = [(i, i + 1) for i in range(count - 1)]
        backward = [(target, source) for source, target in forward]
        low = lax.ppermute(
            lax.slice_in_dim(block, block.shape[dim] - width, None, axis=dim), axis, forward
        )
        high = lax.ppermute(lax.slice_in_dim(block, 0, width, axis=dim), axis, backward)
        block = jnp.concatenate([low, block, high], axis=dim)
    return block


def layer_norm(values, gain, bias):
    centre = jnp.mean(values, axis=-1, keepdims=True)
    centred = values - centre
    variance = jnp.mean(centred * centred, axis=-1, keepdims=True)
    return centred * lax.rsqrt(variance + EPSILON) * gain + bias


def time_embedding(time_steps, model_width):
    half_width = model_width // 2
    freqs = jnp.exp(-math.log(10000.0) * jnp.arange(half_width, dtype=jnp.float32) / half_width)
    angles = time_steps.astype(jnp.float32)[:, None] * freqs[None, :]
    return jnp.concatenate([jnp.cos(angles), jnp.sin(angles)], axis=1)


def project(rows, weight):
    return jnp.einsum("rbd,de->rbe", rows, weight, preferred_element_type=jnp.float32)


def weight_grad(rows, grads):
    return jnp.einsum("rbd,rbe->de", rows, grads, preferred_element_type=jnp.float32)


def back_project(grads, weight):
    return jnp.einsum("rbe,de->rbd", grads, weight, preferred_element_type=jnp.float32)


def per_device(
    image_tokens,
    text_tokens,
    image_skip,
    text_skip,
    time_steps,
    caption_len,
    pred_grad,
    text_grad,
    w_skip,
    b_skip,
    gain_attn,
    bias_attn,
    w_qkv,
    w_proj,
    b_proj,
    gain_mlp,
    bias_mlp,
    w_up,
    b_up,
    w_down,
    b_down,
    gain_head,
    bias_head,
    w_head,
    b_head,
    w_conv,
    b_conv,
):
    item_count, text_dev, model_width = text_tokens.shape
    grid_rows, grid_cols = (image_tokens.shape[1], image_tokens.shape[2])
    image_dev = grid_rows * grid_cols
    local_rows = text_dev + image_dev
    devices = lax.axis_size("gy")
    device = lax.axis_index("gy")
    key_rows = devices * local_rows
    scale = HEAD_DIM ** (-0.5)
    slots = device * text_dev + jnp.arange(text_dev, dtype=jnp.int32)
    first_row = (slots == 0).astype(jnp.float32)
    embed = time_embedding(time_steps, model_width)
    text_rows = (
        jnp.transpose(text_tokens, (1, 0, 2)).astype(jnp.float32)
        + first_row[:, None, None] * embed[None]
    )
    image_rows = jnp.transpose(image_tokens, (1, 2, 0, 3)).reshape(
        image_dev, item_count, model_width
    )
    tokens = jnp.concatenate([text_rows, image_rows.astype(jnp.float32)], axis=0)
    skips = jnp.concatenate(
        [
            jnp.transpose(text_skip, (1, 0, 2)),
            jnp.transpose(image_skip, (1, 2, 0, 3)).reshape(image_dev, item_count, model_width),
        ],
        axis=0,
    )
    joined = jnp.concatenate([tokens.astype(jnp.bfloat16), skips], axis=2)
    resid = project(joined, w_skip) + b_skip
    normed_attn, attn_norm_back = jax.vjp(layer_norm, resid, gain_attn, bias_attn)
    normed = normed_attn.astype(jnp.bfloat16)
    queries = project(normed, w_qkv[:, :model_width]).astype(jnp.bfloat16)
    key_weight = w_qkv[:, model_width:]
    key_values = project(lax.all_gather(normed, "gy", axis=0, tiled=True), key_weight).astype(
        jnp.bfloat16
    )
    key_index = jnp.arange(key_rows, dtype=jnp.int32)
    owner = key_index // local_rows
    within = key_index - owner * local_rows
    key_slot = owner * text_dev + within
    allowed = (within[None, :] >= text_dev) | (key_slot[None, :] <= caption_len[:, None])

    def scores_of(query_part, key_part, mask):
        raw = (
            jnp.einsum("ibhe,jbhe->bhij", query_part, key_part, preferred_element_type=jnp.float32)
            * scale
        )
        return jnp.where(mask[:, None, None, :], raw, -1e30)

    query_heads = queries.reshape(local_rows, item_count, HEADS, HEAD_DIM)
    key_heads = key_values[..., :model_width].reshape(key_rows, item_count, HEADS, HEAD_DIM)
    value_heads = key_values[..., model_width:].reshape(key_rows, item_count, HEADS, HEAD_DIM)
    scores = scores_of(query_heads, key_heads, allowed)
    largest = jnp.max(scores, axis=3, keepdims=True)
    expo = jnp.exp(scores - largest)
    totals = jnp.sum(expo, axis=3, keepdims=True)
    probs = expo / totals
    log_total = largest + jnp.log(totals)
    mixed = jnp.einsum(
        "bhij,jbhe->ibhe",
        probs.astype(jnp.bfloat16),
        value_heads,
        preferred_element_type=jnp.float32,
    )
    mixed = mixed.reshape(local_rows, item_count, model_width).astype(jnp.bfloat16)
    resid_two = resid + project(mixed, w_proj) + b_proj
    normed_mlp, mlp_norm_back = jax.vjp(layer_norm, resid_two, gain_mlp, bias_mlp)
    normed_two = normed_mlp.astype(jnp.bfloat16)
    pre_act = project(normed_two, w_up) + b_up
    activated, gelu_back = jax.vjp(partial(jax.nn.gelu, approximate=False), pre_act)
    hidden = activated.astype(jnp.bfloat16)
    resid_three = resid_two + project(hidden, w_down) + b_down
    text_out = jnp.transpose(resid_three[:text_dev], (1, 0, 2)).astype(jnp.bfloat16)
    normed_head, head_norm_back = jax.vjp(layer_norm, resid_three[text_dev:], gain_head, bias_head)
    head_in = normed_head.astype(jnp.bfloat16)
    patches = project(head_in, w_head) + b_head
    patch_grid = patches.reshape(grid_rows, grid_cols, item_count, PATCH, PATCH, LAT_CH)
    latent = jnp.transpose(patch_grid, (2, 5, 0, 3, 1, 4)).reshape(
        item_count, LAT_CH, PATCH * grid_rows, PATCH * grid_cols
    )
    lat_rows, lat_cols = (latent.shape[2], latent.shape[3])
    side_pad = with_halo(latent, (("gy", 3),), 1)
    padded = jnp.pad(side_pad, ((0, 0), (0, 0), (1, 1), (0, 0)))
    prediction = jnp.zeros(latent.shape, jnp.float32) + b_conv[None, :, None, None]
    for row_off in range(3):
        for col_off in range(3):
            prediction = prediction + jnp.einsum(
                "oi,bihw->bohw",
                w_conv[:, :, row_off, col_off],
                padded[:, :, row_off : row_off + lat_rows, col_off : col_off + lat_cols],
                precision=HIGHEST,
            )
    grad_side = with_halo(pred_grad, (("gy", 3),), 1)
    grad_pad = jnp.pad(grad_side, ((0, 0), (0, 0), (1, 1), (0, 0)))
    grad_latent = jnp.zeros(latent.shape, jnp.float32)
    conv_taps = []
    for row_off in range(3):
        for col_off in range(3):
            grad_latent = grad_latent + jnp.einsum(
                "oi,bohw->bihw",
                w_conv[:, :, row_off, col_off],
                grad_pad[
                    :, :, 2 - row_off : 2 - row_off + lat_rows, 2 - col_off : 2 - col_off + lat_cols
                ],
                precision=HIGHEST,
            )
            conv_taps.append(
                jnp.einsum(
                    "bohw,bihw->oi",
                    pred_grad,
                    padded[:, :, row_off : row_off + lat_rows, col_off : col_off + lat_cols],
                    precision=HIGHEST,
                )
            )
    grad_w_conv = jnp.stack(conv_taps, axis=-1).reshape(LAT_CH, LAT_CH, 3, 3)
    grad_b_conv = jnp.sum(pred_grad, axis=(0, 2, 3))
    grad_patches = jnp.transpose(
        grad_latent.reshape(item_count, LAT_CH, grid_rows, PATCH, grid_cols, PATCH),
        (2, 4, 0, 3, 5, 1),
    ).reshape(image_dev, item_count, LAT_CH * PATCH * PATCH)
    grad_w_head = jnp.einsum(
        "rbd,rbo->do", head_in.astype(jnp.float32), grad_patches, precision=HIGHEST
    )
    grad_b_head = jnp.sum(grad_patches, axis=(0, 1))
    grad_normed_head = jnp.einsum(
        "rbo,do->rbd", grad_patches, w_head.astype(jnp.float32), precision=HIGHEST
    )
    grad_image_out, grad_gain_head, grad_bias_head = head_norm_back(grad_normed_head)
    grad_three = jnp.concatenate([jnp.transpose(text_grad, (1, 0, 2)), grad_image_out], axis=0)
    grad_b_down = jnp.sum(grad_three, axis=(0, 1))
    down_in = grad_three.astype(jnp.bfloat16)
    grad_w_down = weight_grad(hidden, down_in)
    (grad_pre,) = gelu_back(back_project(down_in, w_down))
    pre_low = grad_pre.astype(jnp.bfloat16)
    grad_b_up = jnp.sum(pre_low.astype(jnp.float32), axis=(0, 1))
    grad_w_up = weight_grad(normed_two, pre_low)
    grad_two, grad_gain_mlp, grad_bias_mlp = mlp_norm_back(back_project(pre_low, w_up))
    grad_two = grad_two + grad_three
    grad_b_proj = jnp.sum(grad_two, axis=(0, 1))
    proj_in = grad_two.astype(jnp.bfloat16)
    grad_w_proj = weight_grad(mixed, proj_in)
    grad_mixed = back_project(proj_in, w_proj).astype(jnp.bfloat16)
    grad_mixed_heads = grad_mixed.reshape(local_rows, item_count, HEADS, HEAD_DIM)
    grad_dots = jnp.einsum(
        "ibhe,jbhe->bhij", grad_mixed_heads, value_heads, preferred_element_type=jnp.float32
    )
    probs_again = jnp.exp(scores_of(query_heads, key_heads, allowed) - log_total)
    row_delta = jnp.sum(probs_again * grad_dots, axis=3, keepdims=True)
    grad_scores = (probs_again * (grad_dots - row_delta)).astype(jnp.bfloat16)
    grad_queries = (
        jnp.einsum("bhij,jbhe->ibhe", grad_scores, key_heads, preferred_element_type=jnp.float32)
        * scale
    )
    probs_low = probs_again.astype(jnp.bfloat16)
    key_grad = (
        jnp.einsum("bhij,ibhe->jbhe", grad_scores, query_heads, preferred_element_type=jnp.float32)
        * scale
    )
    value_grad = jnp.einsum(
        "bhij,ibhe->jbhe", probs_low, grad_mixed_heads, preferred_element_type=jnp.float32
    )
    grad_kv = lax.psum_scatter(
        jnp.concatenate(
            [
                key_grad.reshape(local_rows * lax.axis_size("gy"), item_count, model_width),
                value_grad.reshape(local_rows * lax.axis_size("gy"), item_count, model_width),
            ],
            axis=2,
        ).astype(jnp.bfloat16),
        "gy",
        scatter_dimension=0,
        tiled=True,
    ).astype(jnp.float32)
    grad_qkv = jnp.concatenate(
        [grad_queries.reshape(local_rows, item_count, model_width), grad_kv], axis=2
    ).astype(jnp.bfloat16)
    grad_w_qkv = weight_grad(normed, grad_qkv)
    grad_one, grad_gain_attn, grad_bias_attn = attn_norm_back(back_project(grad_qkv, w_qkv))
    grad_one = grad_one + grad_two
    grad_b_skip = jnp.sum(grad_one, axis=(0, 1))
    skip_in = grad_one.astype(jnp.bfloat16)
    grad_w_skip = weight_grad(joined, skip_in)
    grad_joined = back_project(skip_in, w_skip)
    grad_tokens = grad_joined[..., :model_width]
    grad_skips = grad_joined[..., model_width:]
    grad_text = jnp.transpose(grad_tokens[:text_dev], (1, 0, 2))
    grad_image = jnp.transpose(
        grad_tokens[text_dev:].reshape(grid_rows, grid_cols, item_count, model_width), (2, 0, 1, 3)
    )
    grad_text_skip = jnp.transpose(grad_skips[:text_dev], (1, 0, 2))
    grad_image_skip = jnp.transpose(
        grad_skips[text_dev:].reshape(grid_rows, grid_cols, item_count, model_width), (2, 0, 1, 3)
    )
    summed = (
        lax.psum_scatter(grad_w_skip, ("gx", "gy"), scatter_dimension=0, tiled=True),
        lax.psum_scatter(grad_b_skip, ("gx", "gy"), scatter_dimension=0, tiled=True),
        lax.psum_scatter(grad_gain_attn, ("gx", "gy"), scatter_dimension=0, tiled=True),
        lax.psum_scatter(grad_bias_attn, ("gx", "gy"), scatter_dimension=0, tiled=True),
        lax.psum_scatter(grad_w_qkv, ("gx", "gy"), scatter_dimension=0, tiled=True),
        lax.psum_scatter(grad_w_proj, ("gx", "gy"), scatter_dimension=0, tiled=True),
        lax.psum_scatter(grad_b_proj, ("gx", "gy"), scatter_dimension=0, tiled=True),
        lax.psum_scatter(grad_gain_mlp, ("gx", "gy"), scatter_dimension=0, tiled=True),
        lax.psum_scatter(grad_bias_mlp, ("gx", "gy"), scatter_dimension=0, tiled=True),
        lax.psum_scatter(grad_w_up, ("gx", "gy"), scatter_dimension=0, tiled=True),
        lax.psum_scatter(grad_b_up, ("gx", "gy"), scatter_dimension=0, tiled=True),
        lax.psum_scatter(grad_w_down, ("gx", "gy"), scatter_dimension=0, tiled=True),
        lax.psum_scatter(grad_b_down, ("gx", "gy"), scatter_dimension=0, tiled=True),
        lax.psum_scatter(grad_gain_head, ("gx", "gy"), scatter_dimension=0, tiled=True),
        lax.psum_scatter(grad_bias_head, ("gx", "gy"), scatter_dimension=0, tiled=True),
        lax.psum_scatter(grad_w_head, ("gx", "gy"), scatter_dimension=0, tiled=True),
    )
    head_small = lax.psum((grad_b_head, grad_w_conv, grad_b_conv), ("gx", "gy"))
    return (
        prediction,
        text_out,
        grad_image,
        grad_text,
        grad_image_skip,
        grad_text_skip,
        summed[0],
        summed[1],
        summed[2],
        summed[3],
        summed[4],
        summed[5],
        summed[6],
        summed[7],
        summed[8],
        summed[9],
        summed[10],
        summed[11],
        summed[12],
        summed[13],
        summed[14],
        summed[15],
        head_small[0],
        head_small[1],
        head_small[2],
    )


def solution(mesh):
    return jax.shard_map(
        per_device,
        mesh=mesh,
        in_specs=(
            P("gx", None, "gy", None),
            P("gx", "gy", None),
            P("gx", None, "gy", None),
            P("gx", "gy", None),
            P("gx"),
            P("gx"),
            P("gx", None, None, "gy"),
            P("gx", "gy", None),
            P(),
            P(),
            P(),
            P(),
            P(),
            P(),
            P(),
            P(),
            P(),
            P(),
            P(),
            P(),
            P(),
            P(),
            P(),
            P(),
            P(),
            P(),
            P(),
        ),
        out_specs=(
            P("gx", None, None, "gy"),
            P("gx", "gy", None),
            P("gx", None, "gy", None),
            P("gx", "gy", None),
            P("gx", None, "gy", None),
            P("gx", "gy", None),
            P(("gx", "gy"), None),
            P(("gx", "gy")),
            P(("gx", "gy")),
            P(("gx", "gy")),
            P(("gx", "gy"), None),
            P(("gx", "gy"), None),
            P(("gx", "gy")),
            P(("gx", "gy")),
            P(("gx", "gy")),
            P(("gx", "gy"), None),
            P(("gx", "gy")),
            P(("gx", "gy"), None),
            P(("gx", "gy")),
            P(("gx", "gy")),
            P(("gx", "gy")),
            P(("gx", "gy"), None),
            P(),
            P(),
            P(),
        ),
        check_vma=False,
    )
```

profile of v0, /device:TPU:0, one launch (start us, length us, event | category | flops | bytes accessed | tf_op | source)
XLA Modules:
  0.0 2492.8 jit_solution(3032355318105495868)
XLA Ops:
  10.3 6.9 fusion.168
  23.8 5.9 collective-permute-start.2
  29.9 5.4 convolution_convert_fusion.2
  47.2 73.6 %all-gather.2.cloned.1.call-done = bf16[1104,2,1152]{2,1,0:T(2,128)(2,1)} async-done(((bf16[276,2,1152]{2,1,0:T(2,128)(2,1)}), bf16[1104,2,1152]{2,1,0:T(2,128)(2,1)}) %all-gather.2.cloned.1.call-update) | async-done | bytes 5087248 | tf_op jit(solution)/shard_map/all_gather | solution.py:119
  120.8 20.0 convolution_convert_fusion
  140.8 8.7 fusion.165
  149.5 8.5 copy.314
  158.0 8.5 copy.316
  166.5 19.2 fusion.169
  185.7 19.7 fusion.3
  206.1 16.9 fusion.54
  227.3 16.1 fusion.52
  243.4 26.1 %multiply_convert_fusion.2 = (bf16[276,2,4608]{2,0,1:T(8,128)(2,1)S(1)}, f32[276,2,4608]{2,0,1:T(8,128)}) fusion(f32[276,2,4608]{2,0,1:T(8,128)} %get-tuple-element.212, f32[4608]{0:T(1024)S(1)} %copy-done.71, u8[276,4608]{1,0:T(8,128)(4,1)S(1)} %get-tuple-element.151, u8[276,4608]{1,0:T(8,128)(4,1)S(1)} %get-tuple-element.150), kind=kLoop, calls=%fused_computation.34 | loop fusion | flops 180596736 | bytes 27998208 | tf_op jit(solution)/shard_map/convert_element_type | solution.py:156
  269.5 12.0 fusion.44
  289.0 18.3 convert_reduce_fusion
  307.3 13.3 fusion.159
  330.4 17.5 fusion.25
  347.9 28.1 %multiply_reduce_fusion = (f32[2,16,276]{2,1,0:T(8,128)S(1)}, f32[2,16,276,1104]{3,2,1,0:T(8,128)}) fusion(f32[2,16,276,1104]{3,2,1,0:T(8,128)} %get-tuple-element.209, f32[2,16,276]{2,1,0:T(8,128)S(1)} %copy-done.24, bf16[276,2,16,72]{0,3,2,1:T(8,128)(2,1)S(1)} %bitcast.301, bf16[1104,2,16,72]{0,3,2,1:T(8,128)(2,1)} %bitcast.295), kind=kOutput, calls=%fused_computation.1 | convolution fusion | flops 1433318784 | bytes 84433920 | tf_op jit(solution)/shard_map/ibhe,jbhe->bhij/dot_general | solution.py:229
  376.0 16.6 copy.345
  392.6 33.6 %multiply_convert_fusion = bf16[2,16,276,1104]{3,2,1,0:T(8,128)(2,1)} fusion(f32[2,16,276,1104]{3,2,1,0:T(8,128)} %get-tuple-element.216, f32[2,16,276,1104]{3,2,1,0:T(8,128)} %get-tuple-element.209, f32[2,16,276]{2,1,0:T(8,128)S(1)} %get-tuple-element.215, f32[2,16,276]{2,1,0:T(8,128)S(1)} %copy-done.24), kind=kLoop, calls=%fused_computation | loop fusion | flops 39002112 | bytes 97575936 | tf_op jit(solution)/shard_map/convert_element_type | solution.py:234
  426.2 11.3 multiply_convert_fusion.1
  437.5 16.5 copy.344
  454.0 14.6 pad_maximum_fusion
  470.6 14.1 multiply_convert_fusion.3
  489.0 327.1 %all-reduce.26.cloned.1.call-done = bf16[1104,2,2304]{2,1,0:T(2,128)(2,1)} async-done(((bf16[1104,2,2304]{2,1,0:T(2,128)(2,1)}), bf16[1104,2,2304]{2,1,0:T(2,128)(2,1)}) %all-reduce.26.cloned.1.call-update) | async-done | bytes 10174480
  821.7 10.0 multiply_reduce_fusion.2
  834.5 8.0 convolution_bitcast_fusion.3
  844.1 15.0 convolution_bitcast_fusion
  868.6 5.0 collective-permute-start
  873.9 7.2 convolution_bitcast_fusion.4
  881.1 14.7 convolution_bitcast_fusion.1
  903.7 11.5 convolution_bitcast_fusion.2
  915.2 1245.9 %fusion.161 = (f32[48,3456]{1,0:T(8,128)S(1)}, f32[48,1152]{1,0:T(8,128)S(1)}, f32[40,4608]{1,0:T(8,128)S(1)}) fusion(f32[1152,3456]{1,0:T(8,128)} %convolution_bitcast_fusion.2, f32[1152,1152]{1,0:T(8,128)} %convolution_bitcast_fusion.4, f32[1152,4608]{1,0:T(8,128)} %convolution_bitcast_fusion.1), kind=kCustom, calls=%all-reduce-scatter.3 | all-reduce-scatter fusion | flops 12976130 | bytes 44089344
  2164.5 6.0 collective-permute-start.16
  2170.5 4.1 collective-permute-start.19
  2176.6 4.7 collective-permute-start.15
  2193.2 4.8 collective-permute-start.11
  2198.1 6.0 fusion.29
  2204.2 4.9 collective-permute-start.10
  2216.7 13.2 collective-permute-done.11
  2233.8 16.7 collective-permute-start.5
  2250.5 6.5 collective-permute-start.4
  2259.6 44.1 %collective-permute-start.21 = (f32[40,4608]{1,0:T(8,128)S(1)}, f32[40,4608]{1,0:T(8,128)}, u32[]{:S(2)}, u32[]{:S(2)}) collective-permute-start(f32[40,4608]{1,0:T(8,128)S(1)} %get-tuple-element.184), channel_id=1, source_target_pairs={{0,2},{1,3},{2,4},{3,5},{4,6},{5,7},{6,8},{7,9},{8,10},{9,11},{10,... | collective-permute-start | bytes 2211848
  2303.7 4.1 collective-permute-start.20
  2309.4 100.9 %all-reduce.21 = (f32[1152]{0:T(1024)S(1)}, f32[1152]{0:T(1024)S(1)}, f32[1152]{0:T(1024)S(1)}, f32[1152]{0:T(1024)S(1)}, f32[1152]{0:T(1024)S(1)}, /*index=5*/f...) all-reduce(f32[1152]{0:T(1024)S(1)} %get-tuple-element.163, ...), channel_id=4, replica_groups=mesh['gx'=8,'gy'=4] {'gx','gy'}, use_global_device_ids=true, to_apply=%region_18.19.clone | all-reduce | flops 15140 | bytes 121120
  2416.2 9.2 concatenate.56
  2427.5 36.8 %concatenate.55 = f32[420,3456]{1,0:T(8,128)} concatenate(f32[36,3456]{1,0:T(8,128)} %copy-done.37, f32[48,3456]{1,0:T(8,128)} %copy-done.32, f32[48,3456]{1,0:T(8,128)} %copy-done.33, f32[48,3456]{1,0:T(8,128)} %copy-done.34, f32[48,3456]{1,0:T(8,128)} %copy-done.35, f32[48,3456]{1,0:T(8,128)} %copy-done.36, f32[48,3456]{1,0:T(8,128)} %collective-permute-done.5, ...), dimensions={0} | concatenate | bytes 11612160
  2466.4 17.6 concatenate.57
  (363 shorter events, 121.2 us)
Async XLA Ops:
  7.2 215.8 %copy-start = (bf16[1152,1152]{1,0:T(8,128)(2,1)S(1)}, bf16[1152,1152]{1,0:T(8,128)(2,1)}, u32[]{:S(2)}) copy-start(bf16[1152,1152]{1,0:T(8,128)(2,1)} %param.40) | copy-start | bytes 7962628
  7.2 113.6 %all-gather.2.cloned.1.call-start = ((), (), s32[]{:S(2)}) async-start(), calls=%async_computation.2 | async-start | bytes 6359040 | tf_op jit(solution)/shard_map/all_gather | solution.py:119
  22.4 793.7 %all-reduce.26.cloned.1.call-start = ((), (), s32[]{:S(2)}) async-start(), calls=%async_computation.4 | async-start | bytes 20348928
  22.5 16.4 collective-permute-start.3
  23.8 15.1 collective-permute-start.2
  226.8 42.7 %copy-start.2 = (f32[276,2,1152]{2,0,1:T(8,128)}, f32[276,2,1152]{2,0,1:T(8,128)S(1)}, u32[]{:S(2)}) copy-start(f32[276,2,1152]{2,0,1:T(8,128)S(1)} %get-tuple-element.211) | copy-start | bytes 7630852
  226.8 95.5 %copy-start.50 = (f32[276,2]{0,1:T(2,128)}, f32[276,2]{0,1:T(2,128)S(1)}, u32[]{:S(2)}) copy-start(f32[276,2]{0,1:T(2,128)S(1)} %broadcast_multiply_fusion) | copy-start | bytes 6628
  227.3 95.0 %copy-start.65 = (f32[276,2]{0,1:T(2,128)}, f32[276,2]{0,1:T(2,128)S(1)}, u32[]{:S(2)}) copy-start(f32[276,2]{0,1:T(2,128)S(1)} %fusion.135) | copy-start | bytes 6628
  243.3 26.1 %copy-start.86 = (f32[1152]{0:T(1024)S(1)}, f32[1152]{0:T(1024)}, u32[]{:S(2)}) copy-start(f32[1152]{0:T(1024)} %param.47) | copy-start | bytes 13828
  392.6 33.6 %copy-start.9 = (bf16[276,2,1152]{0,2,1:T(8,128)(2,1)S(1)}, bf16[276,2,1152]{0,2,1:T(8,128)(2,1)}, u32[]{:S(2)}) copy-start(bf16[276,2,1152]{0,2,1:T(8,128)(2,1)} %copy.315) | copy-start | bytes 3815428
  468.7 1706.6 %all-reduce.28.cloned.1.call-start = ((), (), s32[]{:S(2)}) async-start(), calls=%async_computation.5 | async-start | bytes 147456
  488.9 1997.2 %reduce-scatter.14.cloned.1.call-start = ((), (), s32[]{:S(2)}) async-start(), calls=%async_computation.6 | async-start | bytes 10948608
  842.5 1643.6 %reduce-scatter.12.cloned.1.call-start = ((), (), s32[]{:S(2)}) async-start(), calls=%async_computation.3 | async-start | bytes 21897216 | tf_op jit(solution)/shard_map/reduce_scatter | solution.py:291
  867.3 29.7 %collective-permute-start.1 = (f32[2,4,64,1]{2,1,3,0:T(4,128)S(1)}, f32[2,4,64,1]{2,1,3,0:T(4,128)S(1)}, u32[]{:S(2)}, u32[]{:S(2)}) collective-permute-start(f32[2,4,64,1]{2,1,3,0:T(4,128)S(1)} %get-tuple-element.199), channel_id=1, source_target_pairs={{1,0},{2,1},{3,2},{5,4},{6,5},{7,6},{9,8},{10,9},{11,10},{13,12},{... | collective-permute-start | bytes 6152 | tf_op jit(solution)/shard_map/ppermute | solution.py:27
  868.6 28.4 %collective-permute-start = (f32[2,4,64,1]{2,1,3,0:T(4,128)S(1)}, f32[2,4,64,1]{2,1,3,0:T(4,128)S(1)}, u32[]{:S(2)}, u32[]{:S(2)}) collective-permute-start(f32[2,4,64,1]{2,1,3,0:T(4,128)S(1)} %get-tuple-element.198), channel_id=1, source_target_pairs={{0,1},{1,2},{2,3},{4,5},{5,6},{6,7},{8,9},{9,10},{10,11},{12,13},{... | collective-permute-start | bytes 6152 | tf_op jit(solution)/shard_map/ppermute | solution.py:24
  915.2 1282.8 %copy-start.27 = (bf16[276,2,1152]{2,0,1:T(8,128)(2,1)S(1)}, bf16[276,2,1152]{2,0,1:T(8,128)(2,1)}, u32[]{:S(2)}) copy-start(bf16[276,2,1152]{2,0,1:T(8,128)(2,1)} %copy-done.26) | copy-start | bytes 3815428
  2161.2 42.9 %copy-start.25 = (f32[48,1152]{1,0:T(8,128)}, f32[48,1152]{1,0:T(8,128)S(1)}, u32[]{:S(2)}) copy-start(f32[48,1152]{1,0:T(8,128)S(1)} %get-tuple-element.183) | copy-start | bytes 663556
  2161.2 26.0 %collective-permute-start.18 = (f32[48,1152]{1,0:T(8,128)S(1)}, f32[48,1152]{1,0:T(8,128)S(1)}, u32[]{:S(2)}, u32[]{:S(2)}) collective-permute-start(f32[48,1152]{1,0:T(8,128)S(1)} %get-tuple-element.183), channel_id=1, source_target_pairs={{0,7},{1,8},{2,9},{3,10},{4,11},{5,12},{6,13},{7,14},{8,15},{9,16}... | collective-permute-start | bytes 663560
  2162.5 26.8 %collective-permute-start.17 = (f32[48,1152]{1,0:T(8,128)S(1)}, f32[48,1152]{1,0:T(8,128)}, u32[]{:S(2)}, u32[]{:S(2)}) collective-permute-start(f32[48,1152]{1,0:T(8,128)S(1)} %get-tuple-element.183), channel_id=1, source_target_pairs={{0,6},{1,7},{2,8},{3,9},{4,10},{5,11},{6,12},{7,13},{8,14},{9,15},... | collective-permute-start | bytes 663560
  2164.5 28.7 %collective-permute-start.16 = (f32[48,1152]{1,0:T(8,128)S(1)}, f32[48,1152]{1,0:T(8,128)}, u32[]{:S(2)}, u32[]{:S(2)}) collective-permute-start(f32[48,1152]{1,0:T(8,128)S(1)} %get-tuple-element.183), channel_id=1, source_target_pairs={{0,5},{1,6},{2,7},{3,8},{4,9},{5,10},{6,11},{7,12},{8,13},{9,14},{... | collective-permute-start | bytes 663560
  2170.5 14.4 collective-permute-start.19
  2176.6 27.5 %collective-permute-start.15 = (f32[48,1152]{1,0:T(8,128)S(1)}, f32[48,1152]{1,0:T(8,128)S(1)}, u32[]{:S(2)}, u32[]{:S(2)}) collective-permute-start(f32[48,1152]{1,0:T(8,128)S(1)} %get-tuple-element.183), channel_id=1, source_target_pairs={{0,4},{1,5},{2,6},{3,7},{4,8},{5,9},{6,10},{7,11},{8,12},{9,13},{1... | collective-permute-start | bytes 663560
  2184.9 24.2 collective-permute-start.14
  2187.2 24.1 collective-permute-start.13
  2189.4 25.9 %collective-permute-start.12 = (f32[48,1152]{1,0:T(8,128)S(1)}, f32[48,1152]{1,0:T(8,128)S(1)}, u32[]{:S(2)}, u32[]{:S(2)}) collective-permute-start(f32[48,1152]{1,0:T(8,128)S(1)} %get-tuple-element.183), channel_id=1, source_target_pairs={{0,1},{1,2},{2,3},{3,4},{4,5},{5,6},{6,7},{7,8},{8,9},{9,10},{10,1... | collective-permute-start | bytes 663560
  2193.2 36.7 %collective-permute-start.11 = (f32[36,3456]{1,0:T(8,128)S(1)}, f32[36,3456]{1,0:T(8,128)S(1)}, u32[]{:S(2)}, u32[]{:S(2)}) collective-permute-start(f32[36,3456]{1,0:T(8,128)S(1)} %slice.217), channel_id=1, source_target_pairs={{0,8},{1,9},{2,10},{3,11},{4,12},{5,13},{6,14},{7,15},{8,16},{9,17... | collective-permute-start | bytes 1493000
  2204.1 105.2 %copy-start.56 = (f32[1152]{0:T(1024)S(1)}, f32[1152]{0:T(1024)}, u32[]{:S(2)}) copy-start(f32[1152]{0:T(1024)} %get-tuple-element.156) | copy-start | bytes 13828
  2204.1 105.2 %copy-start.57 = (f32[1152]{0:T(1024)S(1)}, f32[1152]{0:T(1024)}, u32[]{:S(2)}) copy-start(f32[1152]{0:T(1024)} %get-tuple-element.152) | copy-start | bytes 13828
  2204.2 105.2 %copy-start.72 = (f32[4608]{0:T(1024)S(1)}, f32[4608]{0:T(1024)}, u32[]{:S(2)}) copy-start(f32[4608]{0:T(1024)} %get-tuple-element.218) | copy-start | bytes 55300
  2204.2 105.2 %copy-start.78 = (f32[1152]{0:T(1024)S(1)}, f32[1152]{0:T(1024)}, u32[]{:S(2)}) copy-start(f32[1152]{0:T(1024)} %get-tuple-element.165) | copy-start | bytes 13828
  2204.2 105.2 %copy-start.79 = (f32[1152]{0:T(1024)S(1)}, f32[1152]{0:T(1024)}, u32[]{:S(2)}) copy-start(f32[1152]{0:T(1024)} %get-tuple-element.160) | copy-start | bytes 13828
  2204.2 29.5 %copy-start.40 = (f32[48,1152]{1,0:T(8,128)}, f32[48,1152]{1,0:T(8,128)S(1)}, u32[]{:S(2)}) copy-start(f32[48,1152]{1,0:T(8,128)S(1)} %collective-permute-done.15) | copy-start | bytes 663556
  2204.2 29.5 %collective-permute-start.10 = (f32[48,3456]{1,0:T(8,128)S(1)}, f32[48,3456]{1,0:T(8,128)S(1)}, u32[]{:S(2)}, u32[]{:S(2)}) collective-permute-start(f32[48,3456]{1,0:T(8,128)S(1)} %get-tuple-element.182), channel_id=1, source_target_pairs={{0,7},{1,8},{2,9},{3,10},{4,11},{5,12},{6,13},{7,14},{8,15},{9,16}... | collective-permute-start | bytes 1990664
  2209.2 24.6 copy-start.41
  2209.2 41.3 %collective-permute-start.9 = (f32[48,3456]{1,0:T(8,128)S(1)}, f32[48,3456]{1,0:T(8,128)S(1)}, u32[]{:S(2)}, u32[]{:S(2)}) collective-permute-start(f32[48,3456]{1,0:T(8,128)S(1)} %get-tuple-element.182), channel_id=1, source_target_pairs={{0,6},{1,7},{2,8},{3,9},{4,10},{5,11},{6,12},{7,13},{8,14},{9,15},... | collective-permute-start | bytes 1990664
  2211.4 45.6 %collective-permute-start.8 = (f32[48,3456]{1,0:T(8,128)S(1)}, f32[48,3456]{1,0:T(8,128)S(1)}, u32[]{:S(2)}, u32[]{:S(2)}) collective-permute-start(f32[48,3456]{1,0:T(8,128)S(1)} %get-tuple-element.182), channel_id=1, source_target_pairs={{0,5},{1,6},{2,7},{3,8},{4,9},{5,10},{6,11},{7,12},{8,13},{9,14},{... | collective-permute-start | bytes 1990664
  2215.3 44.3 %collective-permute-start.7 = (f32[48,3456]{1,0:T(8,128)S(1)}, f32[48,3456]{1,0:T(8,128)S(1)}, u32[]{:S(2)}, u32[]{:S(2)}) collective-permute-start(f32[48,3456]{1,0:T(8,128)S(1)} %get-tuple-element.182), channel_id=1, source_target_pairs={{0,4},{1,5},{2,6},{3,7},{4,8},{5,9},{6,10},{7,11},{8,12},{9,13},{1... | collective-permute-start | bytes 1990664
  2229.9 73.8 %collective-permute-start.6 = (f32[48,3456]{1,0:T(8,128)S(1)}, f32[48,3456]{1,0:T(8,128)S(1)}, u32[]{:S(2)}, u32[]{:S(2)}) collective-permute-start(f32[48,3456]{1,0:T(8,128)S(1)} %get-tuple-element.182), channel_id=1, source_target_pairs={{0,3},{1,4},{2,5},{3,6},{4,7},{5,8},{6,9},{7,10},{8,11},{9,12},{10... | collective-permute-start | bytes 1990664
  2233.8 69.9 %copy-start.32 = (f32[48,3456]{1,0:T(8,128)}, f32[48,3456]{1,0:T(8,128)S(1)}, u32[]{:S(2)}) copy-start(f32[48,3456]{1,0:T(8,128)S(1)} %collective-permute-done.10) | copy-start | bytes 1990660
  2233.8 192.4 %collective-permute-start.5 = (f32[48,3456]{1,0:T(8,128)S(1)}, f32[48,3456]{1,0:T(8,128)}, u32[]{:S(2)}, u32[]{:S(2)}) collective-permute-start(f32[48,3456]{1,0:T(8,128)S(1)} %get-tuple-element.182), channel_id=1, source_target_pairs={{0,2},{1,3},{2,4},{3,5},{4,6},{5,7},{6,8},{7,9},{8,10},{9,11},{10,... | collective-permute-start | bytes 1990664
  2250.5 165.1 %copy-start.33 = (f32[48,3456]{1,0:T(8,128)}, f32[48,3456]{1,0:T(8,128)S(1)}, u32[]{:S(2)}) copy-start(f32[48,3456]{1,0:T(8,128)S(1)} %collective-permute-done.9) | copy-start | bytes 1990660
  2250.5 177.0 %collective-permute-start.4 = (f32[48,3456]{1,0:T(8,128)S(1)}, f32[48,3456]{1,0:T(8,128)}, u32[]{:S(2)}, u32[]{:S(2)}) collective-permute-start(f32[48,3456]{1,0:T(8,128)S(1)} %get-tuple-element.182), channel_id=1, source_target_pairs={{0,1},{1,2},{2,3},{3,4},{4,5},{5,6},{6,7},{7,8},{8,9},{9,10},{10,1... | collective-permute-start | bytes 1990664
  2257.0 52.4 %copy-start.34 = (f32[48,3456]{1,0:T(8,128)}, f32[48,3456]{1,0:T(8,128)S(1)}, u32[]{:S(2)}) copy-start(f32[48,3456]{1,0:T(8,128)S(1)} %collective-permute-done.8) | copy-start | bytes 1990660
  2257.0 209.4 %collective-permute-start.22 = (f32[40,4608]{1,0:T(8,128)S(1)}, f32[40,4608]{1,0:T(8,128)}, u32[]{:S(2)}, u32[]{:S(2)}) collective-permute-start(f32[40,4608]{1,0:T(8,128)S(1)} %get-tuple-element.184), channel_id=1, source_target_pairs={{0,3},{1,4},{2,5},{3,6},{4,7},{5,8},{6,9},{7,10},{8,11},{9,12},{10... | collective-permute-start | bytes 2211848
  2259.6 49.8 %copy-start.35 = (f32[48,3456]{1,0:T(8,128)}, f32[48,3456]{1,0:T(8,128)S(1)}, u32[]{:S(2)}) copy-start(f32[48,3456]{1,0:T(8,128)S(1)} %collective-permute-done.7) | copy-start | bytes 1990660
  2259.6 206.7 %collective-permute-start.21 = (f32[40,4608]{1,0:T(8,128)S(1)}, f32[40,4608]{1,0:T(8,128)}, u32[]{:S(2)}, u32[]{:S(2)}) collective-permute-start(f32[40,4608]{1,0:T(8,128)S(1)} %get-tuple-element.184), channel_id=1, source_target_pairs={{0,2},{1,3},{2,4},{3,5},{4,6},{5,7},{6,8},{7,9},{8,10},{9,11},{10,... | collective-permute-start | bytes 2211848
  2303.7 162.7 %collective-permute-start.20 = (f32[40,4608]{1,0:T(8,128)S(1)}, f32[40,4608]{1,0:T(8,128)}, u32[]{:S(2)}, u32[]{:S(2)}) collective-permute-start(f32[40,4608]{1,0:T(8,128)S(1)} %get-tuple-element.184), channel_id=1, source_target_pairs={{0,1},{1,2},{2,3},{3,4},{4,5},{5,6},{6,7},{7,8},{8,9},{9,10},{10,1... | collective-permute-start | bytes 2211848
  2426.2 40.2 %collective-permute-start.23 = (f32[4,4608]{1,0:T(4,128)S(1)}, f32[4,4608]{1,0:T(4,128)S(1)}, u32[]{:S(2)}, u32[]{:S(2)}) collective-permute-start(f32[4,4608]{1,0:T(4,128)S(1)} %slice.219), channel_id=1, source_target_pairs={{0,4},{1,5},{2,6},{3,7},{4,8},{5,9},{6,10},{7,11},{8,12},{9,13},{1... | collective-permute-start | bytes 221192
  (73 other events, 565.5 us)
Sparse Core Ops, SparseCore 0:
  22.6 98.1 all-gather.1
  468.8 347.2 all-reduce.25
  822.3 120.4 all-reduce.27
  949.3 190.1 reduce-scatter.13
  1146.3 325.4 reduce-scatter.11
where the time goes:
time: 2500 us; the launch traced here: 2490 us
  blocking collectives  1350 us (54%)
  waiting for transfers between devices  418 us (17%)
  matrix products  292 us (12%)
  local copies, waits for them, and re-layouts  176 us (7%)
  starting transfers between devices  134 us (5%)
  other arithmetic  110 us (4%)
    unnamed x2, blocking collectives  1350 us
    unnamed x28, waiting for transfers between devices  344 us
    unnamed x23, starting transfers between devices  120 us
    unnamed x221, local copies, waits for them, and re-layouts  94.8 us
    all_gather x1, waiting for transfers between devices, per_device(): lax.all_gather(normed, 'gy', axis=0, tiled=True)  73.6 us
    dot_general x7, matrix products, project(): jnp.einsum('rbd,de->rbe', rows, weight, preferred_element_type=jnp.float32)  64.9 us
    dot_general x5, matrix products, weight_grad(): jnp.einsum('rbd,rbe->de', rows, grads, preferred_element_type=jnp.float32)  56.3 us
    dot_general x5, matrix products, back_project(): jnp.einsum('rbe,de->rbd', grads, weight, preferred_element_type=jnp.float32)  50.7 us
  transfers between devices with their start and end apart: 29, of which 4 were waited for; matrix products, arithmetic and copies ran while one was open for 58% of the time, Pallas kernels for 0%

commit v1 on v0

v1 whole, which is shorter than its diff:
```python
from functools import partial
import math

import jax
import jax.numpy as jnp
from jax import lax
from jax.sharding import PartitionSpec as P

HEADS = 16
HEAD_DIM = 72
LAT_CH = 4
PATCH = 2

EPSILON = 1e-05
HIGHEST = lax.Precision.HIGHEST
F32 = jnp.float32
BF16 = jnp.bfloat16


def bits_of(count):
    bits = count.bit_length() - 1
    assert 1 << bits == count
    return bits


def with_halo(block, axis, dim, width):
    count = lax.axis_size(axis)
    forward = [(i, i + 1) for i in range(count - 1)]
    backward = [(target, source) for source, target in forward]
    low = lax.ppermute(
        lax.slice_in_dim(block, block.shape[dim] - width, None, axis=dim), axis, forward
    )
    high = lax.ppermute(lax.slice_in_dim(block, 0, width, axis=dim), axis, backward)
    return jnp.concatenate([low, block, high], axis=dim)


def layer_norm(values, gain, bias):
    centre = jnp.mean(values, axis=-1, keepdims=True)
    centred = values - centre
    variance = jnp.mean(centred * centred, axis=-1, keepdims=True)
    return centred * lax.rsqrt(variance + EPSILON) * gain + bias


def time_embedding(time_steps, model_width):
    half_width = model_width // 2
    freqs = jnp.exp(-math.log(10000.0) * jnp.arange(half_width, dtype=F32) / half_width)
    angles = time_steps.astype(F32)[:, None] * freqs[None, :]
    return jnp.concatenate([jnp.cos(angles), jnp.sin(angles)], axis=1)


def project(rows, weight):
    return jnp.einsum("rd,de->re", rows, weight, preferred_element_type=F32)


def weight_grad(rows, grads):
    return jnp.einsum("rd,re->de", rows, grads, preferred_element_type=F32)


def back_project(grads, weight):
    return jnp.einsum("re,de->rd", grads, weight, preferred_element_type=F32)


class Regroup:
    def __init__(self):
        self.gx, self.gy = lax.axis_size("gx"), lax.axis_size("gy")
        self.ratio = self.gy // 4
        assert self.ratio * 4 == self.gy and self.gx % 2 == 0
        core, z = lax.axis_index("gx") % 2, lax.axis_index("gy")
        self.parity = z % 2
        self.item = z // self.ratio
        self.slot = (z % self.ratio) * 2 + core
        self.holders = 2 * self.ratio
        self.perms = []
        for turn in range(2):
            pairs = []
            for gx in range(self.gx):
                pair, c = gx // 2, gx % 2
                for z in range(self.gy):
                    f = (z & 1) ^ turn
                    item, d = 2 * c + f, z // 2
                    to_z, to_c = item * self.ratio + d // 2, d % 2
                    pairs.append((gx * self.gy + z, (2 * pair + to_c) * self.gy + to_z))
            self.perms.append(pairs)

    def there(self, blocks):
        out = []
        for turn in range(2):
            send = lax.dynamic_index_in_dim(blocks, self.parity ^ turn, 0, keepdims=False)
            out.append(lax.ppermute(send, ("gx", "gy"), self.perms[turn]))
        return out

    def back(self, first, second):
        got = [
            lax.ppermute(part, ("gx", "gy"), [(b, a) for a, b in self.perms[turn]])
            for turn, part in enumerate((first, second))
        ]
        even = self.parity == 0
        return jnp.stack([jnp.where(even, got[0], got[1]), jnp.where(even, got[1], got[0])])

    def share(self, rows, step):
        pairs = []
        for gx in range(self.gx):
            pair, c = gx // 2, gx % 2
            for z in range(self.gy):
                base, d = z // self.ratio * self.ratio, (z % self.ratio) * 2 + c
                to = (d + step) % self.holders
                pairs.append(
                    (gx * self.gy + z, (2 * pair + to % 2) * self.gy + base + to // 2)
                )
        return lax.ppermute(rows, ("gx", "gy"), pairs)

    def block_z(self, step, turn):
        d = (self.slot - step) % self.holders
        return 2 * d + ((self.item % 2) ^ turn)


def scatter_sum(part, order, wire):
    sizes = {axis: lax.axis_size(axis) for axis in ("gx", "gy")}
    dims = [(axis, bit) for axis in ("gx", "gy") for bit in reversed(range(bits_of(sizes[axis])))]
    rows, rest = part.shape[0] >> len(dims), part.shape[1:]
    for axis, bit in order:
        place = dims.index((axis, bit))
        before, after = 1 << place, 1 << (len(dims) - place - 1)
        part = part.reshape((before, 2, after * rows) + rest)
        mine = (lax.axis_index(axis) >> bit) & 1
        send = lax.dynamic_index_in_dim(part, 1 - mine, 1, keepdims=False)
        keep = lax.dynamic_index_in_dim(part, mine, 1, keepdims=False)
        got = lax.ppermute(send, axis, [(i, i ^ (1 << bit)) for i in range(sizes[axis])])
        part = (keep.astype(F32) + got.astype(F32)).astype(wire)
        part = part.reshape((before * after * rows,) + rest)
        dims.pop(place)
    return part


def orders():
    gx = list(range(bits_of(lax.axis_size("gx"))))
    gy = list(range(bits_of(lax.axis_size("gy"))))
    first = [("gx", b) for b in gx] + [("gy", b) for b in gy]
    second = [("gx", 0)] + [("gx", b) for b in reversed(gx[1:])] + [("gy", b) for b in gy]
    return first, second


def matrix_grad(rows, grads, cut, order_pair):
    pieces = []
    for part, order in zip((grads[:, :cut], grads[:, cut:]), order_pair):
        pieces.append(scatter_sum(weight_grad(rows, part).astype(BF16), order, BF16))
    return jnp.concatenate(pieces, axis=1).astype(F32)


def per_device(
    image_tokens,
    text_tokens,
    image_skip,
    text_skip,
    time_steps,
    caption_len,
    pred_grad,
    text_grad,
    w_skip,
    b_skip,
    gain_attn,
    bias_attn,
    w_qkv,
    w_proj,
    b_proj,
    gain_mlp,
    bias_mlp,
    w_up,
    b_up,
    w_down,
    b_down,
    gain_head,
    bias_head,
    w_head,
    b_head,
    w_conv,
    b_conv,
):
    item_count, text_dev, width = text_tokens.shape
    grid_rows, grid_cols = (image_tokens.shape[1], image_tokens.shape[2])
    image_dev = grid_rows * grid_cols
    assert item_count == 2
    block = -(-(image_dev + text_dev) // 16) * 16
    text_pad = block - image_dev
    rows = 2 * block
    go = Regroup()
    scale = HEAD_DIM ** (-0.5)
    order_pair = orders()
    devices = go.gx * go.gy

    lat_shape = pred_grad.shape
    lat_rows, lat_cols = (lat_shape[2], lat_shape[3])
    grad_pad = jnp.pad(with_halo(pred_grad, "gy", 3, 1), ((0, 0), (0, 0), (1, 1), (0, 0)))
    grad_latent = jnp.zeros(lat_shape, F32)
    for row_off in range(3):
        for col_off in range(3):
            grad_latent = grad_latent + jnp.einsum(
                "oi,bohw->bihw",
                w_conv[:, :, row_off, col_off],
                grad_pad[
                    :, :, 2 - row_off : 2 - row_off + lat_rows, 2 - col_off : 2 - col_off + lat_cols
                ],
                precision=HIGHEST,
            )
    grad_patches = jnp.transpose(
        grad_latent.reshape(item_count, LAT_CH, grid_rows, PATCH, grid_cols, PATCH),
        (0, 2, 4, 3, 5, 1),
    ).reshape(item_count, image_dev, LAT_CH * PATCH * PATCH)
    grad_b_head = jnp.sum(grad_patches, axis=(0, 1))
    grad_b_conv = jnp.sum(pred_grad, axis=(0, 2, 3))

    slots = lax.axis_index("gy") * text_dev + jnp.arange(text_dev, dtype=jnp.int32)
    first_row = (slots == 0).astype(F32)
    embed = time_embedding(time_steps, width)
    text_in = (text_tokens.astype(F32) + first_row[None, :, None] * embed[:, None, :]).astype(BF16)

    def rows_of(image, text):
        return jnp.concatenate(
            [
                image.reshape(item_count, image_dev, width),
                jnp.pad(text, ((0, 0), (0, text_pad - text_dev), (0, 0))),
            ],
            axis=1,
        )

    joined_here = jnp.concatenate(
        [rows_of(image_tokens, text_in), rows_of(image_skip, text_skip)], axis=2
    )
    resid_here = (
        project(joined_here.reshape(rows, 2 * width), w_skip) + b_skip
    ).astype(BF16)
    resid = jnp.concatenate(go.there(resid_here.reshape(2, block, width)), axis=0).astype(F32)
    gate, joined_late, text_grad, grad_patches, caption = lax.optimization_barrier(
        (resid, joined_here, text_grad, grad_patches, caption_len.astype(F32))
    )
    resid = gate
    joined = jnp.concatenate(go.there(joined_late), axis=0)
    patch_rows = -(-grad_patches.shape[1] * grad_patches.shape[2] // width)
    flat = grad_patches.reshape(2, -1)
    flat = jnp.pad(flat, ((0, 0), (0, patch_rows * width - flat.shape[1])))
    message = jnp.concatenate(
        [
            text_grad,
            flat.reshape(2, patch_rows, width),
            jnp.broadcast_to(caption[:, None, None], (2, 1, width)),
        ],
        axis=1,
    )
    message = go.there(message)
    text_grad_rows = [part[:text_dev] for part in message]
    grad_patches = jnp.concatenate(
        [
            part[text_dev : text_dev + patch_rows].reshape(-1)[: image_dev * 16].reshape(-1, 16)
            for part in message
        ],
        axis=0,
    )
    caption = message[0][-1, 0].astype(jnp.int32)

    normed_attn, attn_norm_back = jax.vjp(layer_norm, resid, gain_attn, bias_attn)
    normed = normed_attn.astype(BF16)
    qkv = project(normed, w_qkv).astype(BF16)
    queries, key_values = qkv[:, :width], qkv[:, width:]
    shared = [key_values] + [go.share(key_values, step) for step in range(1, go.holders)]
    allowed = []
    for step in range(go.holders):
        for turn in range(2):
            slot = go.block_z(step, turn) * text_dev + jnp.arange(text_pad)
            inside = (jnp.arange(text_pad) < text_dev) & (slot <= caption)
            allowed += [jnp.ones((image_dev,), jnp.bool_), inside]
    allowed = jnp.concatenate(allowed)
    key_values = jnp.concatenate(shared, axis=0)
    key_rows = rows * go.holders

    query_heads = queries.reshape(rows, HEADS, HEAD_DIM)
    key_heads = key_values[:, :width].reshape(key_rows, HEADS, HEAD_DIM)
    value_heads = key_values[:, width:].reshape(key_rows, HEADS, HEAD_DIM)

    def scores_of():
        raw = jnp.einsum("ihe,jhe->hij", query_heads, key_heads, preferred_element_type=F32) * scale
        return jnp.where(allowed[None, None, :], raw, -1e30)

    scores = scores_of()
    largest = jnp.max(scores, axis=2, keepdims=True)
    expo = jnp.exp(scores - largest)
    totals = jnp.sum(expo, axis=2, keepdims=True)
    probs = expo / totals
    log_total = largest + jnp.log(totals)
    mixed = jnp.einsum("hij,jhe->ihe", probs.astype(BF16), value_heads, preferred_element_type=F32)
    mixed = mixed.reshape(rows, width).astype(BF16)

    resid_two = resid + project(mixed, w_proj) + b_proj
    normed_mlp, mlp_norm_back = jax.vjp(layer_norm, resid_two, gain_mlp, bias_mlp)
    normed_two = normed_mlp.astype(BF16)
    pre_act = project(normed_two, w_up) + b_up
    activated, gelu_back = jax.vjp(partial(jax.nn.gelu, approximate=False), pre_act)
    hidden = activated.astype(BF16)
    resid_three = resid_two + project(hidden, w_down) + b_down

    def image_of(values):
        return jnp.concatenate([values[:image_dev], values[block : block + image_dev]], axis=0)

    def text_of(values):
        return [values[image_dev : image_dev + text_dev], values[block + image_dev : block + image_dev + text_dev]]

    text_out = go.back(*[part.astype(BF16) for part in text_of(resid_three)])
    normed_head, head_norm_back = jax.vjp(layer_norm, image_of(resid_three), gain_head, bias_head)
    head_in = normed_head.astype(BF16)
    patches = project(head_in, w_head) + b_head
    patches = go.back(patches[:image_dev], patches[image_dev:])

    patch_grid = patches.reshape(item_count, grid_rows, grid_cols, PATCH, PATCH, LAT_CH)
    latent = jnp.transpose(patch_grid, (0, 5, 1, 3, 2, 4)).reshape(lat_shape)
    padded = jnp.pad(with_halo(latent, "gy", 3, 1), ((0, 0), (0, 0), (1, 1), (0, 0)))
    prediction = jnp.zeros(lat_shape, F32) + b_conv[None, :, None, None]
    conv_taps = []
    for row_off in range(3):
        for col_off in range(3):
            window = padded[:, :, row_off : row_off + lat_rows, col_off : col_off + lat_cols]
            prediction = prediction + jnp.einsum(
                "oi,bihw->bohw", w_conv[:, :, row_off, col_off], window, precision=HIGHEST
            )
            conv_taps.append(jnp.einsum("bohw,bihw->oi", pred_grad, window, precision=HIGHEST))
    grad_w_conv = jnp.stack(conv_taps, axis=-1)

    grad_w_head = jnp.einsum("rd,ro->do", head_in.astype(F32), grad_patches, precision=HIGHEST)
    grad_normed_head = jnp.einsum("ro,do->rd", grad_patches, w_head.astype(F32), precision=HIGHEST)
    grad_image_out, grad_gain_head, grad_bias_head = head_norm_back(grad_normed_head)
    text_padding = ((0, text_pad - text_dev), (0, 0))
    grad_three = jnp.concatenate(
        [
            grad_image_out[:image_dev],
            jnp.pad(text_grad_rows[0], text_padding),
            grad_image_out[image_dev:],
            jnp.pad(text_grad_rows[1], text_padding),
        ],
        axis=0,
    )
    grad_b_down = jnp.sum(grad_three, axis=0)
    down_in = grad_three.astype(BF16)
    grad_w_down = matrix_grad(hidden, down_in, 640, order_pair)
    (grad_pre,) = gelu_back(back_project(down_in, w_down))
    pre_low = grad_pre.astype(BF16)
    grad_b_up = jnp.sum(pre_low.astype(F32), axis=0)
    grad_w_up = matrix_grad(normed_two, pre_low, 2304, order_pair)
    grad_two, grad_gain_mlp, grad_bias_mlp = mlp_norm_back(back_project(pre_low, w_up))
    grad_two = grad_two + grad_three
    grad_b_proj = jnp.sum(grad_two, axis=0)
    proj_in = grad_two.astype(BF16)
    grad_w_proj = matrix_grad(mixed, proj_in, 640, order_pair)
    grad_mixed = back_project(proj_in, w_proj).astype(BF16)
    grad_mixed_heads = grad_mixed.reshape(rows, HEADS, HEAD_DIM)
    grad_dots = jnp.einsum("ihe,jhe->hij", grad_mixed_heads, value_heads, preferred_element_type=F32)
    probs_again = jnp.exp(scores_of() - log_total)
    row_delta = jnp.sum(probs_again * grad_dots, axis=2, keepdims=True)
    grad_scores = (probs_again * (grad_dots - row_delta)).astype(BF16)
    grad_queries = (
        jnp.einsum("hij,jhe->ihe", grad_scores, key_heads, preferred_element_type=F32) * scale
    ).reshape(rows, width)
    probs_low = probs_again.astype(BF16)
    key_grad = (
        jnp.einsum("hij,ihe->jhe", grad_scores, query_heads, preferred_element_type=F32) * scale
    )
    value_grad = jnp.einsum("hij,ihe->jhe", probs_low, grad_mixed_heads, preferred_element_type=F32)
    grad_kv = jnp.concatenate(
        [key_grad.reshape(key_rows, width), value_grad.reshape(key_rows, width)], axis=1
    ).astype(BF16)
    grad_kv_sum = grad_kv[:rows].astype(F32)
    for step in range(1, go.holders):
        part = go.share(grad_kv[step * rows : (step + 1) * rows], go.holders - step)
        grad_kv_sum = grad_kv_sum + part.astype(F32)
    grad_qkv = jnp.concatenate([grad_queries, grad_kv_sum], axis=1).astype(BF16)
    grad_w_qkv = matrix_grad(normed, grad_qkv, 1792, order_pair)
    grad_one, grad_gain_attn, grad_bias_attn = attn_norm_back(back_project(grad_qkv, w_qkv))
    grad_one = grad_one + grad_two
    grad_b_skip = jnp.sum(grad_one, axis=0)
    skip_in = grad_one.astype(BF16)
    grad_w_skip = matrix_grad(joined, skip_in, 640, order_pair)
    skip_here = go.back(skip_in[:block], skip_in[block:])
    grad_joined = back_project(skip_here.reshape(rows, width), w_skip).reshape(2, block, 2 * width)
    image_shape = image_tokens.shape
    grad_image = grad_joined[:, :image_dev, :width].reshape(image_shape)
    grad_image_skip = grad_joined[:, :image_dev, width:].reshape(image_shape)
    grad_text = grad_joined[:, image_dev : image_dev + text_dev, :width]
    grad_text_skip = grad_joined[:, image_dev : image_dev + text_dev, width:]

    vectors = (
        grad_b_skip,
        grad_gain_attn,
        grad_bias_attn,
        grad_b_proj,
        grad_gain_mlp,
        grad_bias_mlp,
        grad_b_up,
        grad_b_down,
        grad_gain_head,
        grad_bias_head,
        grad_w_head,
    )
    whole = jnp.concatenate([grad_b_head, grad_w_conv.reshape(-1), grad_b_conv])
    packed = [v.reshape(devices, -1) for v in vectors]
    packed.append(jnp.broadcast_to(whole[None], (devices, whole.shape[0])))
    packed = jnp.concatenate(packed, axis=1)
    packed = jnp.pad(packed, ((0, 0), (0, -packed.shape[1] % 128)))
    packed = scatter_sum(packed, order_pair[0], F32)[0]
    small = []
    start = 0
    for v in vectors:
        size = v.size // devices
        small.append(packed[start : start + size])
        start += size
    small[-1] = small[-1].reshape(-1, grad_w_head.shape[1])
    whole = packed[start : start + whole.shape[0]]
    patch_size = grad_b_head.shape[0]
    taps = grad_w_conv.size
    return (
        prediction,
        text_out,
        grad_image,
        grad_text,
        grad_image_skip,
        grad_text_skip,
        grad_w_skip,
        small[0],
        small[1],
        small[2],
        grad_w_qkv,
        grad_w_proj,
        small[3],
        small[4],
        small[5],
        grad_w_up,
        small[6],
        grad_w_down,
        small[7],
        small[8],
        small[9],
        small[10],
        whole[:patch_size],
        whole[patch_size : patch_size + taps].reshape(LAT_CH, LAT_CH, 3, 3),
        whole[patch_size + taps :],
    )


def solution(mesh):
    rows = P(("gx", "gy"))
    image = P("gx", None, "gy", None)
    text = P("gx", "gy", None)
    latent = P("gx", None, None, "gy")
    return jax.shard_map(
        per_device,
        mesh=mesh,
        in_specs=(image, text, image, text, P("gx"), P("gx"), latent, text) + (P(),) * 19,
        out_specs=(latent, text, image, text, image, text) + (rows,) * 16 + (P(),) * 3,
        check_vma=False,
    )
```

time: 2500 us -> 901 us (0.36)
  blocking collectives: 1350 us -> 0 us
  waiting for transfers between devices: 418 us -> 244 us
  local copies, waits for them, and re-layouts: 176 us -> 113 us
  starting transfers between devices: 134 us -> 106 us
    unnamed x2 -> x0, blocking collectives: 1350 us -> none
    unnamed x28 -> x0, waiting for transfers between devices: 344 us -> none
    ppermute x0 -> x69, waiting for transfers between devices: none -> 240 us  [the longest x55 184 us: scatter_sum(): lax.ppermute(send, axis, [(i, i ^ 1 << bit) for i in range(sizes[axis])])]
    unnamed x23 -> x0, starting transfers between devices: 120 us -> none
    ppermute x0 -> x69, starting transfers between devices: none -> 96.3 us  [the longest x55 59.6 us: scatter_sum(): lax.ppermute(send, axis, [(i, i ^ 1 << bit) for i in range(sizes[axis])])]
    unnamed x221 -> x258, local copies, waits for them, and re-layouts: 94.8 us -> 20.4 us
    all_gather x1 -> x0, waiting for transfers between devices: 73.6 us -> none  [per_device(): lax.all_gather(normed, 'gy', axis=0, tiled=True)]
    squeeze x0 -> x58, local copies, waits for them, and re-layouts: none -> 34 us  [the longest x55 31.1 us: scatter_sum(): send = lax.dynamic_index_in_dim(part, 1 - mine, 1, keepdims=False)]
  transfers between devices with their start and end apart: 29 -> 73, of which waited for: 4 -> 33; matrix products, arithmetic and copies ran while one was open for 58% -> 22% of each run, Pallas kernels for 0% -> 0%
where the time goes in v1:
time: 901 us; the launch traced here: 889 us
  matrix products  288 us (32%)
  waiting for transfers between devices  244 us (27%)
  other arithmetic  134 us (15%)
  local copies, waits for them, and re-layouts  113 us (13%)
  starting transfers between devices  106 us (12%)
    ppermute x55, waiting for transfers between devices, scatter_sum(): lax.ppermute(send, axis, [(i, i ^ 1 << bit) for i in range(sizes[axis])])  184 us
    dot_general x6, matrix products, project(): return jnp.einsum('rd,de->re', rows, weight, preferred_element_type=F32)  62.7 us
    ppermute x55, starting transfers between devices, scatter_sum(): lax.ppermute(send, axis, [(i, i ^ 1 << bit) for i in range(sizes[axis])])  59.6 us
    dot_general x5, matrix products, back_project(): return jnp.einsum('re,de->rd', grads, weight, preferred_element_type=F32)  53.6 us
    dot_general x10, matrix products, weight_grad(): return jnp.einsum('rd,re->de', rows, grads, preferred_element_type=F32)  51 us
    ppermute x6, waiting for transfers between devices, there(): out.append(lax.ppermute(send, ('gx', 'gy'), self.perms[turn]))  50.3 us
    convert_element_type x40, other arithmetic, scatter_sum(): part = (keep.astype(F32) + got.astype(F32)).astype(wire)  35.9 us
    convert_element_type x1, other arithmetic, per_device(): grad_scores = (probs_again * (grad_dots - row_delta)).astype(BF16)  34.2 us
  transfers between devices with their start and end apart: 73, of which 33 were waited for; matrix products, arithmetic and copies ran while one was open for 22% of the time, Pallas kernels for 0%

profile of v1, /device:TPU:0, one launch (start us, length us, event | category | flops | bytes accessed | tf_op | source)
XLA Modules:
  0.0 889.4 jit_solution(17941211790162423465)
XLA Ops:
  12.7 7.1 fusion.35
  21.0 6.7 collective-permute-start
  38.2 14.2 %collective-permute-done.1 = bf16[288,1152]{1,0:T(8,128)(2,1)} collective-permute-done((bf16[288,1152]{1,0:T(8,128)(2,1)}, bf16[288,1152]{1,0:T(8,128)(2,1)}, u32[]{:S(2)}, u32[]{:S(2)}) %collective-permute-start.1) | collective-permute-done | bytes 663584 | tf_op jit(solution)/shard_map/ppermute | solution.py:89
  60.5 9.5 %convolution_convert_fusion.6 = bf16[576,3456]{1,0:T(8,128)(2,1)S(1)} fusion(bf16[576,1152]{1,0:T(8,128)(2,1)S(1)} %add_convert_fusion.3, bf16[1152,3456]{1,0:T(8,128)(2,1)} %param.39), kind=kOutput, calls=%fused_computation.35 | convolution fusion | flops 4588462080 | bytes 13271040 | tf_op jit(solution)/shard_map/rd,de->re/dot_general | solution.py:52
  75.4 11.7 %collective-permute-start.16 = (bf16[288,2304]{1,0:T(8,128)(2,1)}, bf16[288,2304]{1,0:T(8,128)(2,1)}, u32[]{:S(2)}, u32[]{:S(2)}) collective-permute-start(bf16[288,2304]{1,0:T(8,128)(2,1)} %get-tuple-element.168), channel_id=1, source_target_pairs={{0,0},{1,1},{2,4},{3,5},{4,2},{5,3},{6,6},{7,7},{8,8},{9,9},{10,12... | collective-permute-start | bytes 3981320 | tf_op jit(solution)/shard_map/ppermute | solution.py:89
  101.8 36.1 %collective-permute-done.12 = f32[25,1152]{1,0:T(8,128)S(1)} collective-permute-done((f32[25,1152]{1,0:T(8,128)S(1)}, f32[25,1152]{1,0:T(8,128)S(1)}, u32[]{:S(2)}, u32[]{:S(2)}) %collective-permute-start.12) | collective-permute-done | bytes 115232 | tf_op jit(solution)/shard_map/ppermute | solution.py:89
  146.5 5.2 pad_maximum_fusion.1
  151.8 5.2 copy.256
  157.0 5.2 copy.252
  162.2 18.8 %fusion.207 = (f32[16,576]{1,0:T(8,128)S(1)}, f32[16,576,1152]{2,1,0:T(8,128)}) fusion(bf16[576,16,72]{0,2,1:T(8,128)(2,1)} %bitcast.527, bf16[1152,16,72]{0,2,1:T(8,128)(2,1)} %bitcast.523, pred[1152]{0:T(1024)(128)(4,1)S(1)} %concatenate.94), kind=kOutput, calls=%fused_computation.474 | convolution fusion | flops 1560665088 | bytes 46486656 | tf_op jit(solution)/shard_map/ihe,jhe->hij/dot_general | solution.py:280
  181.0 19.4 %fusion = f32[16,576]{1,0:T(8,128)S(1)} fusion(f32[16,576,1152]{2,1,0:T(8,128)} %get-tuple-element.215, f32[16,576]{1,0:T(8,128)S(1)} %get-tuple-element.214), kind=kLoop, calls=%fused_computation.6 | loop fusion | flops 21224448 | bytes 42541056 | tf_op jit(solution)/shard_map/reduce_sum | solution.py:286
  201.0 16.3 %fusion.57 = bf16[16,72,576]{2,1,0:T(8,128)(2,1)S(1)} fusion(bf16[1152,16,72]{0,2,1:T(8,128)(2,1)S(1)} %bitcast.531, f32[16,576,1152]{2,1,0:T(8,128)} %get-tuple-element.215, f32[16,576]{1,0:T(8,128)S(1)} %fusion, f32[16,576]{1,0:T(8,128)S(1)} %get-tuple-element.214), kind=kOutput, calls=%fused_computation.140 | convolution fusion | flops 1561337856 | bytes 46522368 | tf_op jit(solution)/shard_map/hij,jhe->ihe/dot_general | solution.py:289
  220.5 35.1 %multiply_convert_fusion.1 = (bf16[576,4608]{1,0:T(8,128)(2,1)S(1)}, f32[576,4608]{1,0:T(8,128)}, f32[576,4608]{1,0:T(8,128)}) fusion(f32[4608]{0:T(1024)S(1)} %copy-done.107, bf16[1152,4608]{1,0:T(8,128)(2,1)} %param.44, f32[576,1152]{1,0:T(8,128)S(1)} %get-tuple-element.217, f32[1152]{0:T(1024)S(1)} %copy-done.110, f32[1152]{0:T(1024)S(1)} %copy-done.99, ...), kind=kOutput, calls=%fused_computation.17 | convolution fusion | flops 6293790720 | bytes 39845376 | tf_op jit(solution)/shard_map/rd,de->re/dot_general | solution.py:52
  255.7 8.2 fusion.209
  273.7 19.9 %convert_reduce_fusion = (f32[4608]{0:T(1024)}, bf16[576,4608]{1,0:T(8,128)(2,1)}) fusion(f32[576,4608]{1,0:T(8,128)} %get-tuple-element.159, f32[576,4608]{1,0:T(8,128)} %get-tuple-element.218, f32[4608]{0:T(1024)S(1)} %copy-done.107, bf16[576,1152]{1,0:T(8,128)(2,1)} %fusion.58, bf16[4608,1152]{1,0:T(8,128)(2,1)} %param.46), kind=kOutput, calls=%fused_computation.15 | convolution fusion | flops 6160412160 | bytes 38522880 | tf_op jit(solution)/shard_map/re,de->rd/dot_general | solution.py:60
  293.7 14.4 %multiply_reduce_fusion.1 = (f32[1152]{0:T(1024)}, f32[576]{0:T(1024)S(1)}, f32[1152]{0:T(1024)}, f32[576,1152]{1,0:T(8,128)S(1)}) fusion(f32[576,1152]{1,0:T(8,128)} %copy-done.6, f32[576]{0:T(1024)S(1)} %fusion.151, f32[576]{0:T(1024)S(1)} %broadcast_multiply_fusion, f32[1152]{0:T(1024)S(1)} %copy-done.99, bf16[576,4608]{1,0:T(8,128)(2,1)} %get-tuple-element.151, ...), kind=kOutput, calls=%fused_computation.106 | convolution fusion | flops 6120601088 | bytes 21254400 | tf_op jit(solution)/shard_map/re,de->rd/dot_general | solution.py:60
  319.4 5.5 convolution_convert_fusion.5
  325.0 7.6 convolution_convert_fusion.2
  332.6 7.0 convolution_convert_fusion.1
  339.6 6.9 convolution_convert_fusion
  348.6 18.0 %fusion.29 = bf16[16,72,1152]{2,1,0:T(8,128)(2,1)} fusion(bf16[576,16,72]{0,2,1:T(8,128)(2,1)S(1)} %bitcast.525, f32[16,576,1152]{2,1,0:T(8,128)} %get-tuple-element.215, f32[16,576]{1,0:T(8,128)S(1)} %copy-done.47), kind=kOutput, calls=%fused_computation.71 | convolution fusion | flops 1551384576 | bytes 46485504 | tf_op jit(solution)/shard_map/hij,ihe->jhe/dot_general | solution.py:364
  366.6 30.6 %multiply_reduce_fusion = (f32[16,576]{1,0:T(8,128)S(1)}, f32[16,576,1152]{2,1,0:T(8,128)}) fusion(f32[16,576,1152]{2,1,0:T(8,128)} %get-tuple-element.215, f32[16,576]{1,0:T(8,128)S(1)} %copy-done.47, bf16[576,16,72]{0,2,1:T(8,128)(2,1)S(1)} %bitcast.526, bf16[1152,16,72]{0,2,1:T(8,128)(2,1)} %bitcast.530), kind=kOutput, calls=%fused_computation.1 | convolution fusion | flops 1560665088 | bytes 88989696 | tf_op jit(solution)/shard_map/ihe,jhe->hij/dot_general | solution.py:353
  397.1 34.2 %multiply_convert_fusion = bf16[16,576,1152]{2,1,0:T(8,128)(2,1)} fusion(f32[16,576,1152]{2,1,0:T(8,128)} %get-tuple-element.224, f32[16,576,1152]{2,1,0:T(8,128)} %get-tuple-element.215, f32[16,576]{1,0:T(8,128)S(1)} %get-tuple-element.223, f32[16,576]{1,0:T(8,128)S(1)} %copy-done.47), kind=kLoop, calls=%fused_computation | loop fusion | flops 42467328 | bytes 106242048 | tf_op jit(solution)/shard_map/convert_element_type | solution.py:356
  431.3 12.0 %multiply_convert_fusion.3 = bf16[16,72,576]{2,1,0:T(8,128)(2,1)} fusion(bf16[1152,16,72]{0,2,1:T(8,128)(2,1)S(1)} %bitcast.524, bf16[16,576,1152]{2,1,0:T(8,128)(2,1)} %multiply_convert_fusion), kind=kOutput, calls=%fused_computation.89 | convolution fusion | flops 1530150912 | bytes 25214976 | tf_op jit(solution)/shard_map/hij,jhe->ihe/dot_general | solution.py:358
  443.4 12.6 %multiply_convert_fusion.2 = bf16[16,72,1152]{2,1,0:T(8,128)(2,1)} fusion(bf16[576,16,72]{0,2,1:T(8,128)(2,1)S(1)} %bitcast.528, bf16[16,576,1152]{2,1,0:T(8,128)(2,1)} %multiply_convert_fusion), kind=kOutput, calls=%fused_computation.56 | convolution fusion | flops 1531478016 | bytes 25214976 | tf_op jit(solution)/shard_map/hij,ihe->jhe/dot_general | solution.py:362
  465.1 15.8 %collective-permute-start.48 = (bf16[4,144,512]{2,1,0:T(8,128)(2,1)}, bf16[4,144,512]{2,1,0:T(8,128)(2,1)}, u32[]{:S(2)}, u32[]{:S(2)}) collective-permute-start(bf16[4,144,512]{2,1,0:T(8,128)(2,1)} %dynamic-slice_bitcast_fusion.22), channel_id=1, source_target_pairs={{0,4},{4,0},{8,12},{12,8},{16,20},{20,16},{24,28},{28,24},{1,5},{5... | collective-permute-start | bytes 1769480 | tf_op jit(solution)/shard_map/ppermute | solution.py:128
  498.5 5.2 copy.269
  556.1 5.7 collective-permute-done.45
  593.2 10.1 %multiply_reduce_fusion.2 = (f32[1152]{0:T(1024)S(1)}, f32[576]{0:T(1024)S(1)}, f32[1152]{0:T(1024)S(1)}, f32[576,1152]{1,0:T(8,128)S(1)}) fusion(f32[576,1152]{1,0:T(8,128)S(1)} %copy-done.4, f32[576]{0:T(1024)S(1)} %copy-done.87, f32[576]{0:T(1024)S(1)} %copy-done.81, f32[1152]{0:T(1024)S(1)} %copy-done.90, bf16[1152,3456]{1,0:T(8,128)(2,1)} %param.39, ...), kind=kOutput, calls=%fused_computation.107 | convolution fusion | flops 4599739904 | bytes 17273088 | tf_op jit(solution)/shard_map/re,de->rd/dot_general | solution.py:60
  606.3 5.2 convolution_convert_fusion.8
  611.5 6.3 convolution_convert_fusion.7
  632.7 6.8 collective-permute-start.14
  668.1 6.2 collective-permute-done.15
  675.4 6.1 fusion.19
  696.2 41.4 %collective-permute-done.70 = bf16[1,576,512]{2,1,0:T(8,128)(2,1)S(1)} collective-permute-done((bf16[1,576,512]{2,1,0:T(8,128)(2,1)S(1)}, bf16[1,576,512]{2,1,0:T(8,128)(2,1)S(1)}, u32[]{:S(2)}, u32[]{:S(2)}) %collective-permute-start.70) | collective-permute-done | bytes 589856 | tf_op jit(solution)/shard_map/ppermute | solution.py:128
  740.3 7.3 collective-permute-done.71
  756.3 5.1 collective-permute-done.72
  773.7 12.4 %collective-permute-done.25 = bf16[1,288,512]{2,1,0:T(8,128)(2,1)} collective-permute-done((bf16[1,288,512]{2,1,0:T(8,128)(2,1)}, bf16[1,288,512]{2,1,0:T(8,128)(2,1)}, u32[]{:S(2)}, u32[]{:S(2)}) %collective-permute-start.25) | collective-permute-done | bytes 294944 | tf_op jit(solution)/shard_map/ppermute | solution.py:128
  792.3 6.3 collective-permute-done.26
  800.4 6.4 collective-permute-done.27
  813.1 8.8 collective-permute-done.62
  821.9 7.1 collective-permute-done.57
  831.6 7.0 collective-permute-done.21
  840.9 6.3 collective-permute-done.22
  852.0 5.5 collective-permute-done.67
  863.9 5.0 collective-permute-done.35
  875.9 5.7 collective-permute-done.36
  881.9 6.4 collective-permute-done.37
  (677 shorter events, 319.5 us)
Async XLA Ops:
  1.7 29.0 %collective-permute-start.2 = (f32[2,4,64,1]{2,1,3,0:T(4,128)S(1)}, f32[2,4,64,1]{2,1,3,0:T(4,128)S(1)}, u32[]{:S(2)}, u32[]{:S(2)}) collective-permute-start(f32[2,4,64,1]{2,1,3,0:T(4,128)S(1)} %get-tuple-element.193), channel_id=1, source_target_pairs={{0,1},{1,2},{2,3},{4,5},{5,6},{6,7},{8,9},{9,10},{10,11},{12,13},{... | collective-permute-start | bytes 6152 | tf_op jit(solution)/shard_map/ppermute | solution.py:30
  6.7 24.0 %collective-permute-start.3 = (f32[2,4,64,1]{2,1,3,0:T(4,128)S(1)}, f32[2,4,64,1]{2,1,3,0:T(4,128)S(1)}, u32[]{:S(2)}, u32[]{:S(2)}) collective-permute-start(f32[2,4,64,1]{2,1,3,0:T(4,128)S(1)} %get-tuple-element.194), channel_id=1, source_target_pairs={{1,0},{2,1},{3,2},{5,4},{6,5},{7,6},{9,8},{10,9},{11,10},{13,12},{... | collective-permute-start | bytes 6152 | tf_op jit(solution)/shard_map/ppermute | solution.py:33
  21.0 17.2 %collective-permute-start = (bf16[288,1152]{1,0:T(8,128)(2,1)}, bf16[288,1152]{1,0:T(8,128)(2,1)}, u32[]{:S(2)}, u32[]{:S(2)}) collective-permute-start(bf16[288,1152]{1,0:T(8,128)(2,1)} %get-tuple-element.181), channel_id=1, source_target_pairs={{0,0},{1,1},{2,4},{3,5},{4,2},{5,3},{6,6},{7,7},{8,8},{9,9},{10,12... | collective-permute-start | bytes 1990664 | tf_op jit(solution)/shard_map/ppermute | solution.py:89
  27.7 24.7 %collective-permute-start.1 = (bf16[288,1152]{1,0:T(8,128)(2,1)}, bf16[288,1152]{1,0:T(8,128)(2,1)}, u32[]{:S(2)}, u32[]{:S(2)}) collective-permute-start(bf16[288,1152]{1,0:T(8,128)(2,1)} %get-tuple-element.182), channel_id=1, source_target_pairs={{0,1},{1,0},{2,5},{3,4},{4,3},{5,2},{6,7},{7,6},{8,9},{9,8},{10,13... | collective-permute-start | bytes 1990664 | tf_op jit(solution)/shard_map/ppermute | solution.py:89
  71.8 74.7 %collective-permute-start.4 = (bf16[576,2304]{1,0:T(8,128)(2,1)}, bf16[576,2304]{1,0:T(8,128)(2,1)}, u32[]{:S(2)}, u32[]{:S(2)}) collective-permute-start(bf16[576,2304]{1,0:T(8,128)(2,1)} %slice.415), channel_id=1, source_target_pairs={{0,4},{1,5},{2,6},{3,7},{4,0},{5,1},{6,2},{7,3},{8,12},{9,13},{10,... | collective-permute-start | bytes 7962632 | tf_op jit(solution)/shard_map/ppermute | solution.py:110
  75.4 66.0 %collective-permute-start.16 = (bf16[288,2304]{1,0:T(8,128)(2,1)}, bf16[288,2304]{1,0:T(8,128)(2,1)}, u32[]{:S(2)}, u32[]{:S(2)}) collective-permute-start(bf16[288,2304]{1,0:T(8,128)(2,1)} %get-tuple-element.168), channel_id=1, source_target_pairs={{0,0},{1,1},{2,4},{3,5},{4,2},{5,3},{6,6},{7,7},{8,8},{9,9},{10,12... | collective-permute-start | bytes 3981320 | tf_op jit(solution)/shard_map/ppermute | solution.py:89
  87.5 56.5 %collective-permute-start.17 = (bf16[288,2304]{1,0:T(8,128)(2,1)}, bf16[288,2304]{1,0:T(8,128)(2,1)}, u32[]{:S(2)}, u32[]{:S(2)}) collective-permute-start(bf16[288,2304]{1,0:T(8,128)(2,1)} %get-tuple-element.167), channel_id=1, source_target_pairs={{0,1},{1,0},{2,5},{3,4},{4,3},{5,2},{6,7},{7,6},{8,9},{9,8},{10,13... | collective-permute-start | bytes 3981320 | tf_op jit(solution)/shard_map/ppermute | solution.py:89
  91.6 46.3 %collective-permute-start.12 = (f32[25,1152]{1,0:T(8,128)S(1)}, f32[25,1152]{1,0:T(8,128)S(1)}, u32[]{:S(2)}, u32[]{:S(2)}) collective-permute-start(f32[25,1152]{1,0:T(8,128)S(1)} %get-tuple-element.184), channel_id=1, source_target_pairs={{0,1},{1,0},{2,5},{3,4},{4,3},{5,2},{6,7},{7,6},{8,9},{9,8},{10,13... | collective-permute-start | bytes 345608 | tf_op jit(solution)/shard_map/ppermute | solution.py:89
  457.6 73.4 %collective-permute-start.10 = (bf16[20,1152]{1,0:T(8,128)(2,1)}, bf16[20,1152]{1,0:T(8,128)(2,1)}, u32[]{:S(2)}, u32[]{:S(2)}) collective-permute-start(bf16[20,1152]{1,0:T(8,128)(2,1)} %get-tuple-element.179), channel_id=1, source_target_pairs={{0,0},{1,1},{4,2},{5,3},{2,4},{3,5},{6,6},{7,7},{8,8},{9,9},{12,10... | collective-permute-start | bytes 138248 | tf_op jit(solution)/shard_map/ppermute | solution.py:94
  459.7 71.8 %collective-permute-start.11 = (bf16[20,1152]{1,0:T(8,128)(2,1)}, bf16[20,1152]{1,0:T(8,128)(2,1)}, u32[]{:S(2)}, u32[]{:S(2)}) collective-permute-start(bf16[20,1152]{1,0:T(8,128)(2,1)} %get-tuple-element.180), channel_id=1, source_target_pairs={{1,0},{0,1},{5,2},{4,3},{3,4},{2,5},{7,6},{6,7},{9,8},{8,9},{13,10... | collective-permute-start | bytes 138248 | tf_op jit(solution)/shard_map/ppermute | solution.py:94
  461.5 51.5 %collective-permute-start.6 = (f32[256,16]{0,1:T(8,128)S(1)}, f32[256,16]{0,1:T(8,128)S(1)}, u32[]{:S(2)}, u32[]{:S(2)}) collective-permute-start(f32[256,16]{0,1:T(8,128)S(1)} %get-tuple-element.197), channel_id=1, source_target_pairs={{0,0},{1,1},{4,2},{5,3},{2,4},{3,5},{6,6},{7,7},{8,8},{9,9},{12,10... | collective-permute-start | bytes 49160 | tf_op jit(solution)/shard_map/ppermute | solution.py:94
  462.2 50.8 %collective-permute-start.7 = (f32[256,16]{0,1:T(8,128)S(1)}, f32[256,16]{0,1:T(8,128)S(1)}, u32[]{:S(2)}, u32[]{:S(2)}) collective-permute-start(f32[256,16]{0,1:T(8,128)S(1)} %get-tuple-element.198), channel_id=1, source_target_pairs={{1,0},{0,1},{5,2},{4,3},{3,4},{2,5},{7,6},{6,7},{9,8},{8,9},{13,10... | collective-permute-start | bytes 49160 | tf_op jit(solution)/shard_map/ppermute | solution.py:94
  465.1 67.4 %collective-permute-start.48 = (bf16[4,144,512]{2,1,0:T(8,128)(2,1)}, bf16[4,144,512]{2,1,0:T(8,128)(2,1)}, u32[]{:S(2)}, u32[]{:S(2)}) collective-permute-start(bf16[4,144,512]{2,1,0:T(8,128)(2,1)} %dynamic-slice_bitcast_fusion.22), channel_id=1, source_target_pairs={{0,4},{4,0},{8,12},{12,8},{16,20},{20,16},{24,28},{28,24},{1,5},{5... | collective-permute-start | bytes 1769480 | tf_op jit(solution)/shard_map/ppermute | solution.py:128
  519.7 15.7 %collective-permute-start.43 = (bf16[4,144,640]{2,1,0:T(8,128)(2,1)}, bf16[4,144,640]{2,1,0:T(8,128)(2,1)S(1)}, u32[]{:S(2)}, u32[]{:S(2)}) collective-permute-start(bf16[4,144,640]{2,1,0:T(8,128)(2,1)} %dynamic-slice_bitcast_fusion.16), channel_id=1, source_target_pairs={{0,4},{4,0},{8,12},{12,8},{16,20},{20,16},{24,28},{28,24},{1,5},{5... | collective-permute-start | bytes 2211848 | tf_op jit(solution)/shard_map/ppermute | solution.py:128
  523.4 55.0 %collective-permute-start.68 = (bf16[4,576,512]{2,1,0:T(8,128)(2,1)}, bf16[4,576,512]{2,1,0:T(8,128)(2,1)}, u32[]{:S(2)}, u32[]{:S(2)}) collective-permute-start(bf16[4,576,512]{2,1,0:T(8,128)(2,1)} %dynamic-slice_bitcast_fusion.3), channel_id=1, source_target_pairs={{0,4},{4,0},{8,12},{12,8},{16,20},{20,16},{24,28},{28,24},{1,5},{5... | collective-permute-start | bytes 7077896 | tf_op jit(solution)/shard_map/ppermute | solution.py:128
  531.0 130.2 %collective-permute-start.63 = (bf16[4,576,640]{2,1,0:T(8,128)(2,1)}, bf16[4,576,640]{2,1,0:T(8,128)(2,1)}, u32[]{:S(2)}, u32[]{:S(2)}) collective-permute-start(bf16[4,576,640]{2,1,0:T(8,128)(2,1)} %dynamic-slice_bitcast_fusion), channel_id=1, source_target_pairs={{0,4},{4,0},{8,12},{12,8},{16,20},{20,16},{24,28},{28,24},{1,5},{5... | collective-permute-start | bytes 8847368 | tf_op jit(solution)/shard_map/ppermute | solution.py:128
  531.5 51.8 %collective-permute-start.58 = (bf16[4,144,2304]{2,1,0:T(8,128)(2,1)}, bf16[4,144,2304]{2,1,0:T(8,128)(2,1)}, u32[]{:S(2)}, u32[]{:S(2)}) collective-permute-start(bf16[4,144,2304]{2,1,0:T(8,128)(2,1)} %dynamic-slice_bitcast_fusion.1), channel_id=1, source_target_pairs={{0,4},{4,0},{8,12},{12,8},{16,20},{20,16},{24,28},{28,24},{1,5},{5... | collective-permute-start | bytes 7962632 | tf_op jit(solution)/shard_map/ppermute | solution.py:128
  536.7 14.0 %collective-permute-start.44 = (bf16[2,144,640]{2,1,0:T(8,128)(2,1)S(1)}, bf16[2,144,640]{2,1,0:T(8,128)(2,1)S(1)}, u32[]{:S(2)}, u32[]{:S(2)}) collective-permute-start(bf16[2,144,640]{2,1,0:T(8,128)(2,1)S(1)} %dynamic-slice_bitcast_fusion.28), channel_id=1, source_target_pairs={{0,8},{4,12},{8,0},{12,4},{16,24},{20,28},{24,16},{28,20},{1,9},{5... | collective-permute-start | bytes 1105928 | tf_op jit(solution)/shard_map/ppermute | solution.py:128
  550.6 40.3 %collective-permute-start.13 = (bf16[576,2304]{1,0:T(8,128)(2,1)}, bf16[576,2304]{1,0:T(8,128)(2,1)}, u32[]{:S(2)}, u32[]{:S(2)}) collective-permute-start(bf16[576,2304]{1,0:T(8,128)(2,1)} %pad_maximum_fusion), channel_id=1, source_target_pairs={{0,4},{1,5},{2,6},{3,7},{4,0},{5,1},{6,2},{7,3},{8,12},{9,13},{10,... | collective-permute-start | bytes 7962632 | tf_op jit(solution)/shard_map/ppermute | solution.py:110
  577.7 49.9 %collective-permute-start.53 = (bf16[4,144,2304]{2,1,0:T(8,128)(2,1)}, bf16[4,144,2304]{2,1,0:T(8,128)(2,1)}, u32[]{:S(2)}, u32[]{:S(2)}) collective-permute-start(bf16[4,144,2304]{2,1,0:T(8,128)(2,1)} %dynamic-slice_bitcast_fusion.2), channel_id=1, source_target_pairs={{0,4},{4,0},{8,12},{12,8},{16,20},{20,16},{24,28},{28,24},{1,5},{5... | collective-permute-start | bytes 7962632 | tf_op jit(solution)/shard_map/ppermute | solution.py:128
  582.7 103.2 %collective-permute-start.69 = (bf16[1,1152,512]{2,1,0:T(8,128)(2,1)}, bf16[1,1152,512]{2,1,0:T(8,128)(2,1)}, u32[]{:S(2)}, u32[]{:S(2)}) collective-permute-start(bf16[1,1152,512]{2,1,0:T(8,128)(2,1)} %dynamic-slice_bitcast_fusion.12), channel_id=1, source_target_pairs={{0,16},{4,20},{8,24},{12,28},{16,0},{20,4},{24,8},{28,12},{1,17},{... | collective-permute-start | bytes 3538952 | tf_op jit(solution)/shard_map/ppermute | solution.py:128
  589.3 99.3 %collective-permute-start.59 = (bf16[1,288,2304]{2,1,0:T(8,128)(2,1)}, bf16[1,288,2304]{2,1,0:T(8,128)(2,1)}, u32[]{:S(2)}, u32[]{:S(2)}) collective-permute-start(bf16[1,288,2304]{2,1,0:T(8,128)(2,1)} %dynamic-slice_bitcast_fusion.8), channel_id=1, source_target_pairs={{0,16},{4,20},{8,24},{12,28},{16,0},{20,4},{24,8},{28,12},{1,17},{... | collective-permute-start | bytes 3981320 | tf_op jit(solution)/shard_map/ppermute | solution.py:128
  606.3 33.3 %collective-permute-start.28 = (f32[4,4,1280]{2,1,0:T(4,128)S(1)}, f32[4,4,1280]{2,1,0:T(4,128)S(1)}, u32[]{:S(2)}, u32[]{:S(2)}) collective-permute-start(f32[4,4,1280]{2,1,0:T(4,128)S(1)} %dynamic-slice_bitcast_fusion.41), channel_id=1, source_target_pairs={{0,4},{4,0},{8,12},{12,8},{16,20},{20,16},{24,28},{28,24},{1,5},{5... | collective-permute-start | bytes 245768 | tf_op jit(solution)/shard_map/ppermute | solution.py:128
  632.7 33.6 %collective-permute-start.14 = (bf16[288,1152]{1,0:T(8,128)(2,1)}, bf16[288,1152]{1,0:T(8,128)(2,1)}, u32[]{:S(2)}, u32[]{:S(2)}) collective-permute-start(bf16[288,1152]{1,0:T(8,128)(2,1)} %get-tuple-element.177), channel_id=1, source_target_pairs={{0,0},{1,1},{4,2},{5,3},{2,4},{3,5},{6,6},{7,7},{8,8},{9,9},{12,10... | collective-permute-start | bytes 1990664 | tf_op jit(solution)/shard_map/ppermute | solution.py:94
  657.0 17.2 %collective-permute-start.15 = (bf16[288,1152]{1,0:T(8,128)(2,1)S(1)}, bf16[288,1152]{1,0:T(8,128)(2,1)S(1)}, u32[]{:S(2)}, u32[]{:S(2)}) collective-permute-start(bf16[288,1152]{1,0:T(8,128)(2,1)S(1)} %get-tuple-element.178), channel_id=1, source_target_pairs={{1,0},{0,1},{5,2},{4,3},{3,4},{2,5},{7,6},{6,7},{9,8},{8,9},{13,10... | collective-permute-start | bytes 1990664 | tf_op jit(solution)/shard_map/ppermute | solution.py:94
  661.2 32.2 %collective-permute-start.54 = (bf16[2,144,2304]{2,1,0:T(8,128)(2,1)}, bf16[2,144,2304]{2,1,0:T(8,128)(2,1)S(1)}, u32[]{:S(2)}, u32[]{:S(2)}) collective-permute-start(bf16[2,144,2304]{2,1,0:T(8,128)(2,1)} %dynamic-slice_bitcast_fusion.9), channel_id=1, source_target_pairs={{0,8},{4,12},{8,0},{12,4},{16,24},{20,28},{24,16},{28,20},{1,9},{5... | collective-permute-start | bytes 3981320 | tf_op jit(solution)/shard_map/ppermute | solution.py:128
  667.4 20.7 %collective-permute-start.23 = (bf16[4,288,512]{2,1,0:T(8,128)(2,1)S(1)}, bf16[4,288,512]{2,1,0:T(8,128)(2,1)S(1)}, u32[]{:S(2)}, u32[]{:S(2)}) collective-permute-start(bf16[4,288,512]{2,1,0:T(8,128)(2,1)S(1)} %copy-done.65), channel_id=1, source_target_pairs={{0,4},{4,0},{8,12},{12,8},{16,20},{20,16},{24,28},{28,24},{1,5},{5... | collective-permute-start | bytes 3538952 | tf_op jit(solution)/shard_map/ppermute | solution.py:128
  674.2 64.6 %collective-permute-start.18 = (bf16[4,288,640]{2,1,0:T(8,128)(2,1)S(1)}, bf16[4,288,640]{2,1,0:T(8,128)(2,1)S(1)}, u32[]{:S(2)}, u32[]{:S(2)}) collective-permute-start(bf16[4,288,640]{2,1,0:T(8,128)(2,1)S(1)} %copy-done.54), channel_id=1, source_target_pairs={{0,4},{4,0},{8,12},{12,8},{16,20},{20,16},{24,28},{28,24},{1,5},{5... | collective-permute-start | bytes 4423688 | tf_op jit(solution)/shard_map/ppermute | solution.py:128
  685.9 77.0 %collective-permute-start.38 = (bf16[4,144,1664]{2,1,0:T(8,128)(2,1)S(1)}, bf16[4,144,1664]{2,1,0:T(8,128)(2,1)S(1)}, u32[]{:S(2)}, u32[]{:S(2)}) collective-permute-start(bf16[4,144,1664]{2,1,0:T(8,128)(2,1)S(1)} %copy-done.53), channel_id=1, source_target_pairs={{0,4},{4,0},{8,12},{12,8},{16,20},{20,16},{24,28},{28,24},{1,5},{5... | collective-permute-start | bytes 5750792 | tf_op jit(solution)/shard_map/ppermute | solution.py:128
  688.1 99.2 %collective-permute-start.33 = (bf16[4,144,1792]{2,1,0:T(8,128)(2,1)}, bf16[4,144,1792]{2,1,0:T(8,128)(2,1)}, u32[]{:S(2)}, u32[]{:S(2)}) collective-permute-start(bf16[4,144,1792]{2,1,0:T(8,128)(2,1)} %dynamic-slice_bitcast_fusion.4), channel_id=1, source_target_pairs={{0,4},{4,0},{8,12},{12,8},{16,20},{20,16},{24,28},{28,24},{1,5},{5... | collective-permute-start | bytes 6193160 | tf_op jit(solution)/shard_map/ppermute | solution.py:128
  688.6 65.5 %collective-permute-start.64 = (bf16[2,576,640]{2,1,0:T(8,128)(2,1)S(1)}, bf16[2,576,640]{2,1,0:T(8,128)(2,1)S(1)}, u32[]{:S(2)}, u32[]{:S(2)}) collective-permute-start(bf16[2,576,640]{2,1,0:T(8,128)(2,1)S(1)} %dynamic-slice_bitcast_fusion.6), channel_id=1, source_target_pairs={{0,8},{4,12},{8,0},{12,4},{16,24},{20,28},{24,16},{28,20},{1,9},{5... | collective-permute-start | bytes 4423688 | tf_op jit(solution)/shard_map/ppermute | solution.py:128
  693.4 44.2 %collective-permute-start.70 = (bf16[1,576,512]{2,1,0:T(8,128)(2,1)S(1)}, bf16[1,576,512]{2,1,0:T(8,128)(2,1)S(1)}, u32[]{:S(2)}, u32[]{:S(2)}) collective-permute-start(bf16[1,576,512]{2,1,0:T(8,128)(2,1)S(1)} %dynamic-slice_bitcast_fusion.21), channel_id=1, source_target_pairs={{0,8},{4,12},{8,0},{12,4},{16,24},{20,28},{24,16},{28,20},{1,9},{5... | collective-permute-start | bytes 1769480 | tf_op jit(solution)/shard_map/ppermute | solution.py:128
  737.6 15.3 %collective-permute-start.24 = (bf16[1,576,512]{2,1,0:T(8,128)(2,1)S(1)}, bf16[1,576,512]{2,1,0:T(8,128)(2,1)S(1)}, u32[]{:S(2)}, u32[]{:S(2)}) collective-permute-start(bf16[1,576,512]{2,1,0:T(8,128)(2,1)S(1)} %dynamic-slice_bitcast_fusion.23), channel_id=1, source_target_pairs={{0,16},{4,20},{8,24},{12,28},{16,0},{20,4},{24,8},{28,12},{1,17},{... | collective-permute-start | bytes 1769480 | tf_op jit(solution)/shard_map/ppermute | solution.py:128
  747.6 18.1 %collective-permute-start.60 = (bf16[1,144,2304]{2,1,0:T(8,128)(2,1)S(1)}, bf16[1,144,2304]{2,1,0:T(8,128)(2,1)S(1)}, u32[]{:S(2)}, u32[]{:S(2)}) collective-permute-start(bf16[1,144,2304]{2,1,0:T(8,128)(2,1)S(1)} %dynamic-slice_bitcast_fusion.18), channel_id=1, source_target_pairs={{0,8},{4,12},{8,0},{12,4},{16,24},{20,28},{24,16},{28,20},{1,9},{5... | collective-permute-start | bytes 1990664 | tf_op jit(solution)/shard_map/ppermute | solution.py:128
  752.9 18.1 %collective-permute-start.55 = (bf16[1,144,2304]{2,1,0:T(8,128)(2,1)}, bf16[1,144,2304]{2,1,0:T(8,128)(2,1)}, u32[]{:S(2)}, u32[]{:S(2)}) collective-permute-start(bf16[1,144,2304]{2,1,0:T(8,128)(2,1)} %constant_dynamic-slice_fusion.5), channel_id=1, source_target_pairs={{0,16},{4,20},{8,24},{12,28},{16,0},{20,4},{24,8},{28,12},{1,17},{... | collective-permute-start | bytes 1990664 | tf_op jit(solution)/shard_map/ppermute | solution.py:128
  761.4 37.6 %collective-permute-start.19 = (bf16[2,288,640]{2,1,0:T(8,128)(2,1)}, bf16[2,288,640]{2,1,0:T(8,128)(2,1)}, u32[]{:S(2)}, u32[]{:S(2)}) collective-permute-start(bf16[2,288,640]{2,1,0:T(8,128)(2,1)} %dynamic-slice_bitcast_fusion.17), channel_id=1, source_target_pairs={{0,8},{4,12},{8,0},{12,4},{16,24},{20,28},{24,16},{28,20},{1,9},{5... | collective-permute-start | bytes 2211848 | tf_op jit(solution)/shard_map/ppermute | solution.py:128
  763.0 67.2 %collective-permute-start.65 = (bf16[1,576,640]{2,1,0:T(8,128)(2,1)}, bf16[1,576,640]{2,1,0:T(8,128)(2,1)}, u32[]{:S(2)}, u32[]{:S(2)}) collective-permute-start(bf16[1,576,640]{2,1,0:T(8,128)(2,1)} %constant_dynamic-slice_fusion.2), channel_id=1, source_target_pairs={{0,16},{4,20},{8,24},{12,28},{16,0},{20,4},{24,8},{28,12},{1,17},{... | collective-permute-start | bytes 2211848 | tf_op jit(solution)/shard_map/ppermute | solution.py:128
  765.7 20.4 %collective-permute-start.25 = (bf16[1,288,512]{2,1,0:T(8,128)(2,1)}, bf16[1,288,512]{2,1,0:T(8,128)(2,1)}, u32[]{:S(2)}, u32[]{:S(2)}) collective-permute-start(bf16[1,288,512]{2,1,0:T(8,128)(2,1)} %dynamic-slice_bitcast_fusion.31), channel_id=1, source_target_pairs={{0,8},{4,12},{8,0},{12,4},{16,24},{20,28},{24,16},{28,20},{1,9},{5... | collective-permute-start | bytes 884744 | tf_op jit(solution)/shard_map/ppermute | solution.py:128
  771.0 79.0 %collective-permute-start.39 = (bf16[1,288,1664]{2,1,0:T(8,128)(2,1)}, bf16[1,288,1664]{2,1,0:T(8,128)(2,1)}, u32[]{:S(2)}, u32[]{:S(2)}) collective-permute-start(bf16[1,288,1664]{2,1,0:T(8,128)(2,1)} %dynamic-slice_bitcast_fusion.15), channel_id=1, source_target_pairs={{0,16},{4,20},{8,24},{12,28},{16,0},{20,4},{24,8},{28,12},{1,17},{... | collective-permute-start | bytes 2875400 | tf_op jit(solution)/shard_map/ppermute | solution.py:128
  786.1 22.2 %collective-permute-start.61 = (bf16[2,36,2304]{2,1,0:T(8,128)(2,1)S(1)}, bf16[2,36,2304]{2,1,0:T(8,128)(2,1)S(1)}, u32[]{:S(2)}, u32[]{:S(2)}) collective-permute-start(bf16[2,36,2304]{2,1,0:T(8,128)(2,1)S(1)} %dynamic-slice_bitcast_fusion.26), channel_id=1, source_target_pairs={{0,1},{1,0},{2,3},{3,2},{4,5},{5,4},{6,7},{7,6},{8,9},{9,8},{10,11... | collective-permute-start | bytes 995336 | tf_op jit(solution)/shard_map/ppermute | solution.py:128
  787.3 11.4 %collective-permute-start.26 = (bf16[2,72,512]{2,1,0:T(8,128)(2,1)S(1)}, bf16[2,72,512]{2,1,0:T(8,128)(2,1)S(1)}, u32[]{:S(2)}, u32[]{:S(2)}) collective-permute-start(bf16[2,72,512]{2,1,0:T(8,128)(2,1)S(1)} %dynamic-slice_bitcast_fusion.36), channel_id=1, source_target_pairs={{0,1},{1,0},{2,3},{3,2},{4,5},{5,4},{6,7},{7,6},{8,9},{9,8},{10,11... | collective-permute-start | bytes 442376 | tf_op jit(solution)/shard_map/ppermute | solution.py:128
  798.6 10.8 %collective-permute-start.56 = (bf16[2,36,2304]{2,1,0:T(8,128)(2,1)S(1)}, bf16[2,36,2304]{2,1,0:T(8,128)(2,1)S(1)}, u32[]{:S(2)}, u32[]{:S(2)}) collective-permute-start(bf16[2,36,2304]{2,1,0:T(8,128)(2,1)S(1)} %dynamic-slice_bitcast_fusion.27), channel_id=1, source_target_pairs={{0,1},{1,0},{2,3},{3,2},{4,5},{5,4},{6,7},{7,6},{8,9},{9,8},{10,11... | collective-permute-start | bytes 995336 | tf_op jit(solution)/shard_map/ppermute | solution.py:128
  806.8 51.6 %collective-permute-start.34 = (bf16[2,144,1792]{2,1,0:T(8,128)(2,1)S(1)}, bf16[2,144,1792]{2,1,0:T(8,128)(2,1)S(1)}, u32[]{:S(2)}, u32[]{:S(2)}) collective-permute-start(bf16[2,144,1792]{2,1,0:T(8,128)(2,1)S(1)} %dynamic-slice_bitcast_fusion.14), channel_id=1, source_target_pairs={{0,8},{4,12},{8,0},{12,4},{16,24},{20,28},{24,16},{28,20},{1,9},{5... | collective-permute-start | bytes 3096584 | tf_op jit(solution)/shard_map/ppermute | solution.py:128
  808.4 21.6 %collective-permute-start.20 = (bf16[1,288,640]{2,1,0:T(8,128)(2,1)S(1)}, bf16[1,288,640]{2,1,0:T(8,128)(2,1)S(1)}, u32[]{:S(2)}, u32[]{:S(2)}) collective-permute-start(bf16[1,288,640]{2,1,0:T(8,128)(2,1)S(1)} %constant_dynamic-slice_fusion.20), channel_id=1, source_target_pairs={{0,16},{4,20},{8,24},{12,28},{16,0},{20,4},{24,8},{28,12},{1,17},{... | collective-permute-start | bytes 1105928 | tf_op jit(solution)/shard_map/ppermute | solution.py:128
  809.4 12.5 %collective-permute-start.62 = (bf16[1,36,2304]{2,1,0:T(8,128)(2,1)S(1)}, bf16[1,36,2304]{2,1,0:T(8,128)(2,1)S(1)}, u32[]{:S(2)}, u32[]{:S(2)}) collective-permute-start(bf16[1,36,2304]{2,1,0:T(8,128)(2,1)S(1)} %constant_dynamic-slice_fusion.3), channel_id=1, source_target_pairs={{0,2},{1,3},{2,0},{3,1},{4,6},{5,7},{6,4},{7,5},{8,10},{9,11},{10,... | collective-permute-start | bytes 497672 | tf_op jit(solution)/shard_map/ppermute | solution.py:128
  838.8 10.5 %collective-permute-start.66 = (bf16[2,144,640]{2,1,0:T(8,128)(2,1)S(1)}, bf16[2,144,640]{2,1,0:T(8,128)(2,1)S(1)}, u32[]{:S(2)}, u32[]{:S(2)}) collective-permute-start(bf16[2,144,640]{2,1,0:T(8,128)(2,1)S(1)} %dynamic-slice_bitcast_fusion.25), channel_id=1, source_target_pairs={{0,1},{1,0},{2,3},{3,2},{4,5},{5,4},{6,7},{7,6},{8,9},{9,8},{10,11... | collective-permute-start | bytes 1105928 | tf_op jit(solution)/shard_map/ppermute | solution.py:128
  851.5 9.6 %collective-permute-start.40 = (bf16[1,144,1664]{2,1,0:T(8,128)(2,1)S(1)}, bf16[1,144,1664]{2,1,0:T(8,128)(2,1)S(1)}, u32[]{:S(2)}, u32[]{:S(2)}) collective-permute-start(bf16[1,144,1664]{2,1,0:T(8,128)(2,1)S(1)} %dynamic-slice_bitcast_fusion.24), channel_id=1, source_target_pairs={{0,8},{4,12},{8,0},{12,4},{16,24},{20,28},{24,16},{28,20},{1,9},{5... | collective-permute-start | bytes 1437704 | tf_op jit(solution)/shard_map/ppermute | solution.py:128
  862.2 10.1 %collective-permute-start.41 = (bf16[2,36,1664]{2,1,0:T(8,128)(2,1)S(1)}, bf16[2,36,1664]{2,1,0:T(8,128)(2,1)}, u32[]{:S(2)}, u32[]{:S(2)}) collective-permute-start(bf16[2,36,1664]{2,1,0:T(8,128)(2,1)S(1)} %dynamic-slice_bitcast_fusion.33), channel_id=1, source_target_pairs={{0,1},{1,0},{2,3},{3,2},{4,5},{5,4},{6,7},{7,6},{8,9},{9,8},{10,11... | collective-permute-start | bytes 718856 | tf_op jit(solution)/shard_map/ppermute | solution.py:128
  (149 other events, 1536.9 us)

commit v2 on v1

--- a/solution.py
+++ b/solution.py
@@ -4,6 +4,8 @@
 import jax
 import jax.numpy as jnp
 from jax import lax
+from jax.experimental import pallas as pl
+from jax.experimental.pallas import tpu as pltpu
 from jax.sharding import PartitionSpec as P
 
 HEADS = 16
@@ -114,37 +116,257 @@
         return 2 * d + ((self.item % 2) ^ turn)
 
 
-def scatter_sum(part, order, wire):
-    sizes = {axis: lax.axis_size(axis) for axis in ("gx", "gy")}
-    dims = [(axis, bit) for axis in ("gx", "gy") for bit in reversed(range(bits_of(sizes[axis])))]
-    rows, rest = part.shape[0] >> len(dims), part.shape[1:]
-    for axis, bit in order:
-        place = dims.index((axis, bit))
-        before, after = 1 << place, 1 << (len(dims) - place - 1)
-        part = part.reshape((before, 2, after * rows) + rest)
-        mine = (lax.axis_index(axis) >> bit) & 1
-        send = lax.dynamic_index_in_dim(part, 1 - mine, 1, keepdims=False)
-        keep = lax.dynamic_index_in_dim(part, mine, 1, keepdims=False)
-        got = lax.ppermute(send, axis, [(i, i ^ (1 << bit)) for i in range(sizes[axis])])
-        part = (keep.astype(F32) + got.astype(F32)).astype(wire)
-        part = part.reshape((before * after * rows,) + rest)
-        dims.pop(place)
-    return part
-
-
-def orders():
-    gx = list(range(bits_of(lax.axis_size("gx"))))
-    gy = list(range(bits_of(lax.axis_size("gy"))))
-    first = [("gx", b) for b in gx] + [("gy", b) for b in gy]
-    second = [("gx", 0)] + [("gx", b) for b in reversed(gx[1:])] + [("gy", b) for b in gy]
-    return first, second
-
-
-def matrix_grad(rows, grads, cut, order_pair):
-    pieces = []
-    for part, order in zip((grads[:, :cut], grads[:, cut:]), order_pair):
-        pieces.append(scatter_sum(weight_grad(rows, part).astype(BF16), order, BF16))
-    return jnp.concatenate(pieces, axis=1).astype(F32)
+class Halving:
+    def __init__(self, part, columns=None, wire=BF16):
+        self.sizes = {axis: lax.axis_size(axis) for axis in ("gx", "gy")}
+        gx, gy = bits_of(self.sizes["gx"]), bits_of(self.sizes["gy"])
+        dims = [("gx", b) for b in reversed(range(gx))] + [("gy", b) for b in reversed(range(gy))]
+        self.rows = part.shape[0] >> len(dims)
+        self.pieces = [([part], dims)]
+        rising = [("gx", b) for b in range(1, gx)]
+        self.orders = [[("gx", 0)]] + [list(pair) for pair in zip(rising, reversed(rising))]
+        self.orders += [[("gy", b)] for b in range(gy)]
+        self.columns, self.wire = columns, wire
+        if columns is None:
+            self.orders = [order[:1] for order in self.orders]
+
+    def cut(self):
+        steps = self.orders.pop(0)
+        if len(steps) > len(self.pieces):
+            (parts, dims), c = self.pieces[0], self.columns
+            self.pieces = [([p[:, :c] for p in parts], dims), ([p[:, c:] for p in parts], dims)]
+        self.kept, sends = [], []
+        together = len(steps) < len(self.pieces)
+        for i, (parts, dims) in enumerate(self.pieces):
+            axis, bit = steps[0 if together else i]
+            place = dims.index((axis, bit))
+            before, after = 1 << place, 1 << (len(dims) - place - 1)
+            mine = (lax.axis_index(axis) >> bit) & 1
+
+            def half(which):
+                total = 0.0
+                for p in parts:
+                    p = p.reshape((before, 2, after * self.rows) + p.shape[1:])
+                    p = lax.dynamic_index_in_dim(p, which, 1, keepdims=False)
+                    p = p.reshape((before * after * self.rows,) + p.shape[2:])
+                    total = p if len(parts) == 1 else total + p.astype(F32)
+                return total.astype(self.wire)
+
+            sends.append(half(1 - mine))
+            self.kept.append((half(mine), [d for d in dims if d != (axis, bit)]))
+        if together:
+            sends = [jnp.concatenate(sends, axis=1)]
+            self.kept = [(jnp.concatenate([k for k, _ in self.kept], axis=1), self.kept[0][1])]
+        self.steps = steps
+        return sends
+
+    def send(self, sends):
+        self.pieces = []
+        for value, (kept, dims), (axis, bit) in zip(sends, self.kept, self.steps):
+            got = lax.ppermute(value, axis, [(i, i ^ (1 << bit)) for i in range(self.sizes[axis])])
+            self.pieces.append(([kept, got], dims))
+
+    def advance(self, *others):
+        sends = self.cut()
+        out = lax.optimization_barrier((*sends, *others))
+        self.send(out[: len(sends)])
+        return out[len(sends) :] if len(others) != 1 else out[-1]
+
+    def finish(self):
+        while self.orders:
+            self.send(self.cut())
+        (kept, got), _ = self.pieces[0]
+        return kept.astype(F32) + got.astype(F32)
+
+
+LANES = 128
+NT = (((1,), (1,)), ((), ()))
+TN = (((0,), (0,)), ((), ()))
+NN = (((1,), (0,)), ((), ()))
+IN_VMEM = pl.BlockSpec(memory_space=pltpu.VMEM)
+
+
+def dot(left, right, dims):
+    return lax.dot_general(left, right, dims, preferred_element_type=F32)
+
+
+def head_of(ref, head, base=0):
+    start = base + head * HEAD_DIM
+    return ref[:, start : start + HEAD_DIM].astype(F32)
+
+
+def widen(value, extras=()):
+    rows = value.shape[0]
+    out = jnp.concatenate([value, jnp.zeros((rows, LANES - HEAD_DIM), F32)], axis=1)
+    lane = lax.broadcasted_iota(jnp.int32, (rows, LANES), 1)
+    for i, extra in enumerate(extras):
+        out = jnp.where(lane == HEAD_DIM + i, extra, out)
+    return out
+
+
+def thirds(value):
+    high = value.astype(BF16).astype(F32)
+    rest = value - high
+    middle = rest.astype(BF16).astype(F32)
+    return high, middle, rest - middle
+
+
+def attend_kernel(holders, width, chunk, *refs):
+    qkv, others, bias, mixed, lse = refs[0], refs[1:holders], refs[holders], *refs[holders + 1 : holders + 3]
+    q_s, k_s, v_s, o_s = refs[holders + 3 :]
+    rows = qkv.shape[0]
+    factor = HEAD_DIM**-0.5 * math.log2(math.e)
+    for head in range(HEADS):
+        q_s[head] = widen(head_of(qkv, head), (1.0,)).astype(BF16)
+        for s in range(holders):
+            source, base = (qkv, width) if s == 0 else (others[s - 1], 0)
+            part = slice(s * rows, (s + 1) * rows)
+            k_s[head, part, :] = widen(head_of(source, head, base), (bias[part, 0:1],)).astype(BF16)
+            v_s[head, part, :] = widen(head_of(source, head, base + width), (1.0,)).astype(BF16)
+    lane = lax.broadcasted_iota(jnp.int32, (chunk, LANES), 1)
+
+    def one_head(head, carry):
+        k, v = k_s[head], v_s[head]
+        for r in range(0, rows, chunk):
+            scores = dot(q_s[head, r : r + chunk, :], k, NT)
+            largest = jnp.max(scores, axis=1, keepdims=True)
+            expo = jnp.exp2((scores - largest) * factor).astype(BF16)
+            out = dot(expo, v, NN)
+            total = out[:, HEAD_DIM : HEAD_DIM + 1]
+            o_s[head, r : r + chunk, :] = jnp.where(
+                lane == HEAD_DIM, largest * factor + jnp.log2(total), out / total
+            )
+        return carry
+
+    lax.fori_loop(0, HEADS, one_head, 0)
+    lane = lax.broadcasted_iota(jnp.int32, (rows, LANES), 1)
+    logs = jnp.zeros((rows, LANES), F32)
+    for head in range(HEADS):
+        out = o_s[head]
+        mixed[:, head * HEAD_DIM : (head + 1) * HEAD_DIM] = out[:, :HEAD_DIM].astype(mixed.dtype)
+        logs = jnp.where(lane == head, out[:, HEAD_DIM : HEAD_DIM + 1], logs)
+    lse[...] = logs
+
+
+def attend(qkv, others, bias):
+    rows, width, holders = qkv.shape[0], qkv.shape[1] // 3, len(others) + 1
+    keys = rows * holders
+    return pl.pallas_call(
+        partial(attend_kernel, holders, width, 288),
+        out_shape=(
+            jax.ShapeDtypeStruct((rows, width), BF16),
+            jax.ShapeDtypeStruct((rows, LANES), F32),
+        ),
+        in_specs=[IN_VMEM] * (holders + 1),
+        out_specs=(IN_VMEM,) * 2,
+        scratch_shapes=[
+            pltpu.VMEM((HEADS, rows, LANES), BF16),
+            pltpu.VMEM((HEADS, keys, LANES), BF16),
+            pltpu.VMEM((HEADS, keys, LANES), BF16),
+            pltpu.VMEM((HEADS, rows, LANES), F32),
+        ],
+        cost_estimate=pl.CostEstimate(
+            flops=4 * rows * keys * 512 * HEADS,
+            transcendentals=rows * keys * HEADS,
+            bytes_accessed=2 * width * (rows * 4 + keys * 2),
+        ),
+        compiler_params=pltpu.CompilerParams(vmem_limit_bytes=56 << 20),
+        name="attend",
+    )(qkv, *others, bias)
+
+
+def attend_back_kernel(holders, width, chunk, first, heads, *refs):
+    refs = list(refs)
+    qkv, others, bias, mixed, lse, grad = refs[0], refs[1:holders], *refs[holders : holders + 4]
+    refs = refs[holders + 4 :]
+    last = first + heads == HEADS
+    earlier, refs = (refs[:2], refs[2:]) if last and first else ((), refs)
+    outs, refs = (refs[: holders + 1], refs[holders + 1 :]) if last else (refs[:2], refs[2:])
+    q_s, k_s, v_s, g_s = refs[:4]
+    dq_s, dkv_s = refs[4:] if last else outs
+    rows = qkv.shape[0]
+    keys = rows * holders
+    scale = HEAD_DIM**-0.5
+    factor = scale * math.log2(math.e)
+    for i in range(heads):
+        head = first + i
+        g = head_of(grad, head)
+        delta = jnp.sum(g * head_of(mixed, head), axis=1, keepdims=True)
+        shift = thirds(lse[:, head : head + 1] * (-1.0 / factor))
+        q_s[i] = widen(head_of(qkv, head), (1.0,) + shift).astype(BF16)
+        g_s[i] = widen(g, thirds(-delta)).astype(BF16)
+        for s in range(holders):
+            source, base = (qkv, width) if s == 0 else (others[s - 1], 0)
+            part = slice(s * rows, (s + 1) * rows)
+            k = widen(head_of(source, head, base), (bias[part, 0:1], 1.0, 1.0, 1.0))
+            k_s[i, part, :] = k.astype(BF16)
+            v_s[i, part, :] = widen(head_of(source, head, base + width), (1.0,) * 3).astype(BF16)
+
+    def one_head(i, carry):
+        q, g = q_s[i], g_s[i]
+        dq = jnp.zeros((LANES, rows), F32)
+        for r in range(0, keys, chunk):
+            k, v = k_s[i, r : r + chunk, :], v_s[i, r : r + chunk, :]
+            probs = jnp.exp2(dot(k, q, NT) * factor)
+            ds = (probs * dot(v, g, NT)).astype(BF16)
+            dkv_s[0, i, r : r + chunk, :] = (dot(ds, q, NN) * scale).astype(dkv_s.dtype)
+            dkv_s[1, i, r : r + chunk, :] = dot(probs.astype(BF16), g, NN).astype(dkv_s.dtype)
+            dq = dq + dot(k, ds, TN)
+        dq_s[i] = (jnp.transpose(dq) * scale).astype(dq_s.dtype)
+        return carry
+
+    lax.fori_loop(0, heads, one_head, 0)
+    if not last:
+        return
+    for head in range(HEADS):
+        dq, dkv, i = (dq_s, dkv_s, head - first) if head >= first else (*earlier, head)
+        cols = slice(head * HEAD_DIM, (head + 1) * HEAD_DIM)
+        outs[0][:, cols] = dq[i][:, :HEAD_DIM].astype(F32).astype(BF16)
+        for s in range(holders):
+            for which in range(2):
+                value = dkv[which, i, s * rows : (s + 1) * rows, :][:, :HEAD_DIM]
+                cols = slice(which * width + head * HEAD_DIM, which * width + (head + 1) * HEAD_DIM)
+                outs[1 + s][:, cols] = value.astype(F32).astype(BF16)
+
+
+def attend_back(qkv, others, bias, mixed, lse, grad, first, heads, earlier):
+    rows, width, holders = qkv.shape[0], qkv.shape[1] // 3, len(others) + 1
+    keys = rows * holders
+    last = first + heads == HEADS
+    if last:
+        out_shape = (jax.ShapeDtypeStruct((rows, width), BF16),) + (
+            jax.ShapeDtypeStruct((rows, 2 * width), BF16),
+        ) * holders
+    else:
+        out_shape = (
+            jax.ShapeDtypeStruct((heads, rows, LANES), BF16),
+            jax.ShapeDtypeStruct((2, heads, keys, LANES), BF16),
+        )
+    scratch = [
+        pltpu.VMEM((heads, rows, LANES), BF16),
+        pltpu.VMEM((heads, keys, LANES), BF16),
+        pltpu.VMEM((heads, keys, LANES), BF16),
+        pltpu.VMEM((heads, rows, LANES), BF16),
+    ]
+    if last:
+        scratch += [
+            pltpu.VMEM((heads, rows, LANES), BF16),
+            pltpu.VMEM((2, heads, keys, LANES), BF16),
+        ]
+    return pl.pallas_call(
+        partial(attend_back_kernel, holders, width, keys // 2, first, heads),
+        out_shape=out_shape,
+        in_specs=[IN_VMEM] * (holders + 4 + len(earlier)),
+        out_specs=(IN_VMEM,) * len(out_shape),
+        scratch_shapes=scratch,
+        cost_estimate=pl.CostEstimate(
+            flops=10 * rows * keys * 512 * heads,
+            transcendentals=rows * keys * heads,
+            bytes_accessed=2 * width * (rows * 8 + keys * 4),
+        ),
+        compiler_params=pltpu.CompilerParams(vmem_limit_bytes=58 << 20),
+        name="attend_back",
+    )(qkv, *others, bias, mixed, lse, grad, *earlier)
 
 
 def per_device(
@@ -184,8 +406,6 @@
     text_pad = block - image_dev
     rows = 2 * block
     go = Regroup()
-    scale = HEAD_DIM ** (-0.5)
-    order_pair = orders()
     devices = go.gx * go.gy
 
     lat_shape = pred_grad.shape
@@ -234,7 +454,6 @@
         (resid, joined_here, text_grad, grad_patches, caption_len.astype(F32))
     )
     resid = gate
-    joined = jnp.concatenate(go.there(joined_late), axis=0)
     patch_rows = -(-grad_patches.shape[1] * grad_patches.shape[2] // width)
     flat = grad_patches.reshape(2, -1)
     flat = jnp.pad(flat, ((0, 0), (0, patch_rows * width - flat.shape[1])))
@@ -247,6 +466,8 @@
         axis=1,
     )
     message = go.there(message)
+    joined_late, *message = lax.optimization_barrier((joined_late, *message))
+    joined = jnp.concatenate(go.there(joined_late), axis=0)
     text_grad_rows = [part[:text_dev] for part in message]
     grad_patches = jnp.concatenate(
         [
@@ -260,34 +481,17 @@
     normed_attn, attn_norm_back = jax.vjp(layer_norm, resid, gain_attn, bias_attn)
     normed = normed_attn.astype(BF16)
     qkv = project(normed, w_qkv).astype(BF16)
-    queries, key_values = qkv[:, :width], qkv[:, width:]
-    shared = [key_values] + [go.share(key_values, step) for step in range(1, go.holders)]
-    allowed = []
+    key_values = qkv[:, width:]
+    others = [go.share(key_values, step) for step in range(1, go.holders)]
+    inside = jnp.arange(text_pad, dtype=jnp.int32)
+    bias = []
     for step in range(go.holders):
         for turn in range(2):
-            slot = go.block_z(step, turn) * text_dev + jnp.arange(text_pad)
-            inside = (jnp.arange(text_pad) < text_dev) & (slot <= caption)
-            allowed += [jnp.ones((image_dev,), jnp.bool_), inside]
-    allowed = jnp.concatenate(allowed)
-    key_values = jnp.concatenate(shared, axis=0)
-    key_rows = rows * go.holders
-
-    query_heads = queries.reshape(rows, HEADS, HEAD_DIM)
-    key_heads = key_values[:, :width].reshape(key_rows, HEADS, HEAD_DIM)
-    value_heads = key_values[:, width:].reshape(key_rows, HEADS, HEAD_DIM)
-
-    def scores_of():
-        raw = jnp.einsum("ihe,jhe->hij", query_heads, key_heads, preferred_element_type=F32) * scale
-        return jnp.where(allowed[None, None, :], raw, -1e30)
-
-    scores = scores_of()
-    largest = jnp.max(scores, axis=2, keepdims=True)
-    expo = jnp.exp(scores - largest)
-    totals = jnp.sum(expo, axis=2, keepdims=True)
-    probs = expo / totals
-    log_total = largest + jnp.log(totals)
-    mixed = jnp.einsum("hij,jhe->ihe", probs.astype(BF16), value_heads, preferred_element_type=F32)
-    mixed = mixed.reshape(rows, width).astype(BF16)
+            slot = go.block_z(step, turn) * text_dev + inside
+            allowed = (inside < text_dev) & (slot <= caption)
+            bias += [jnp.zeros((image_dev,), F32), jnp.where(allowed, 0.0, -1e30)]
+    bias = jnp.broadcast_to(jnp.concatenate(bias)[:, None], (rows * go.holders, LANES))
+    mixed, lse = attend(qkv, others, bias)
 
     resid_two = resid + project(mixed, w_proj) + b_proj
     normed_mlp, mlp_norm_back = jax.vjp(layer_norm, resid_two, gain_mlp, bias_mlp)
@@ -338,44 +542,44 @@
     )
     grad_b_down = jnp.sum(grad_three, axis=0)
     down_in = grad_three.astype(BF16)
-    grad_w_down = matrix_grad(hidden, down_in, 640, order_pair)
+    sum_down = Halving(weight_grad(hidden, down_in).astype(BF16), 640)
+    down_in = sum_down.advance(down_in)
     (grad_pre,) = gelu_back(back_project(down_in, w_down))
     pre_low = grad_pre.astype(BF16)
     grad_b_up = jnp.sum(pre_low.astype(F32), axis=0)
-    grad_w_up = matrix_grad(normed_two, pre_low, 2304, order_pair)
+    pre_low = sum_down.advance(pre_low)
+    sum_up = Halving(weight_grad(normed_two, pre_low).astype(BF16), 2304)
+    pre_low = sum_up.advance(pre_low)
     grad_two, grad_gain_mlp, grad_bias_mlp = mlp_norm_back(back_project(pre_low, w_up))
     grad_two = grad_two + grad_three
     grad_b_proj = jnp.sum(grad_two, axis=0)
     proj_in = grad_two.astype(BF16)
-    grad_w_proj = matrix_grad(mixed, proj_in, 640, order_pair)
+    proj_in = sum_up.advance(proj_in)
+    sum_proj = Halving(weight_grad(mixed, proj_in).astype(BF16), 640)
+    proj_in = sum_proj.advance(proj_in)
     grad_mixed = back_project(proj_in, w_proj).astype(BF16)
-    grad_mixed_heads = grad_mixed.reshape(rows, HEADS, HEAD_DIM)
-    grad_dots = jnp.einsum("ihe,jhe->hij", grad_mixed_heads, value_heads, preferred_element_type=F32)
-    probs_again = jnp.exp(scores_of() - log_total)
-    row_delta = jnp.sum(probs_again * grad_dots, axis=2, keepdims=True)
-    grad_scores = (probs_again * (grad_dots - row_delta)).astype(BF16)
-    grad_queries = (
-        jnp.einsum("hij,jhe->ihe", grad_scores, key_heads, preferred_element_type=F32) * scale
-    ).reshape(rows, width)
-    probs_low = probs_again.astype(BF16)
-    key_grad = (
-        jnp.einsum("hij,ihe->jhe", grad_scores, query_heads, preferred_element_type=F32) * scale
-    )
-    value_grad = jnp.einsum("hij,ihe->jhe", probs_low, grad_mixed_heads, preferred_element_type=F32)
-    grad_kv = jnp.concatenate(
-        [key_grad.reshape(key_rows, width), value_grad.reshape(key_rows, width)], axis=1
-    ).astype(BF16)
-    grad_kv_sum = grad_kv[:rows].astype(F32)
+    grad_mixed = sum_down.advance(grad_mixed)
+    parts = attend_back(qkv, others, bias, mixed, lse, grad_mixed, 0, HEADS // 2, ())
+    parts = sum_proj.advance(*parts)
+    parts = sum_up.advance(*parts)
+    parts = sum_down.advance(*parts)
+    grads = attend_back(qkv, others, bias, mixed, lse, grad_mixed, HEADS // 2, HEADS // 2, parts)
+    grads = sum_down.advance(*grads)
+    grads = sum_proj.advance(*grads)
+    grads = sum_up.advance(*grads)
+    grad_kv = grads[1].astype(F32)
     for step in range(1, go.holders):
-        part = go.share(grad_kv[step * rows : (step + 1) * rows], go.holders - step)
-        grad_kv_sum = grad_kv_sum + part.astype(F32)
-    grad_qkv = jnp.concatenate([grad_queries, grad_kv_sum], axis=1).astype(BF16)
-    grad_w_qkv = matrix_grad(normed, grad_qkv, 1792, order_pair)
+        grad_kv = grad_kv + go.share(grads[1 + step], go.holders - step).astype(F32)
+    grad_qkv = jnp.concatenate([grads[0], grad_kv.astype(BF16)], axis=1)
+    sum_qkv = Halving(weight_grad(normed, grad_qkv).astype(BF16), 1792)
+    grad_qkv = sum_qkv.advance(grad_qkv)
     grad_one, grad_gain_attn, grad_bias_attn = attn_norm_back(back_project(grad_qkv, w_qkv))
     grad_one = grad_one + grad_two
     grad_b_skip = jnp.sum(grad_one, axis=0)
     skip_in = grad_one.astype(BF16)
-    grad_w_skip = matrix_grad(joined, skip_in, 640, order_pair)
+    skip_in = sum_qkv.advance(skip_in)
+    sum_skip = Halving(weight_grad(joined, skip_in).astype(BF16), 640)
+    skip_in = sum_skip.advance(skip_in)
     skip_here = go.back(skip_in[:block], skip_in[block:])
     grad_joined = back_project(skip_here.reshape(rows, width), w_skip).reshape(2, block, 2 * width)
     image_shape = image_tokens.shape
@@ -402,7 +606,7 @@
     packed.append(jnp.broadcast_to(whole[None], (devices, whole.shape[0])))
     packed = jnp.concatenate(packed, axis=1)
     packed = jnp.pad(packed, ((0, 0), (0, -packed.shape[1] % 128)))
-    packed = scatter_sum(packed, order_pair[0], F32)[0]
+    packed = Halving(packed, None, F32).finish()[0]
     small = []
     start = 0
     for v in vectors:
@@ -420,18 +624,18 @@
         grad_text,
         grad_image_skip,
         grad_text_skip,
-        grad_w_skip,
+        sum_skip.finish(),
         small[0],
         small[1],
         small[2],
-        grad_w_qkv,
-        grad_w_proj,
+        sum_qkv.finish(),
+        sum_proj.finish(),
         small[3],
         small[4],
         small[5],
-        grad_w_up,
+        sum_up.finish(),
         small[6],
-        grad_w_down,
+        sum_down.finish(),
         small[7],
         small[8],
         small[9],

time: 901 us -> 757 us (0.84)
  waiting for transfers between devices: 244 us -> 102 us
  matrix products: 288 us -> 177 us
  Pallas kernels: 0 us -> 108 us
  local copies, waits for them, and re-layouts: 113 us -> 165 us
  other arithmetic: 134 us -> 106 us
  starting transfers between devices: 106 us -> 84.4 us
    ppermute x55 -> x40, waiting for transfers between devices: 184 us -> 73.9 us  [send(): lax.ppermute(value, axis, [(i, i ^ 1 << bit) for i in range(self.sizes[ax...]
    dot_general x6 -> x0, matrix products: 108 us -> none  [the longest x1 30.6 us: per_device(): jnp.einsum('ihe,jhe->hij', grad_mixed_heads, value_heads, preferred_eleme...]
    pallas_call x0 -> x3, Pallas kernels: none -> 108 us  [the longest x2 69.5 us: attend_back(): pl.pallas_call(partial(attend_back_kernel, holders, width, keys // 2, fir...]
    ppermute x6, waiting for transfers between devices: 50.3 us -> 14.2 us  [there(): out.append(lax.ppermute(send, ('gx', 'gy'), self.perms[turn]))]
    squeeze x55 -> x0, local copies, waits for them, and re-layouts: 31.1 us -> none  [scatter_sum(): send = lax.dynamic_index_in_dim(part, 1 - mine, 1, keepdims=False)]
    dynamic_slice x0 -> x6, local copies, waits for them, and re-layouts: none -> 26.6 us  [half(): p = lax.dynamic_index_in_dim(p, which, 1, keepdims=False)]
    ppermute x55 -> x40, starting transfers between devices: 59.6 us -> 38.5 us  [send(): lax.ppermute(value, axis, [(i, i ^ 1 << bit) for i in range(self.sizes[ax...]
    reduce_sum x1 -> x0, other arithmetic: 19.4 us -> none  [per_device(): totals = jnp.sum(expo, axis=2, keepdims=True)]
  transfers between devices with their start and end apart: 73 -> 58, of which waited for: 33 -> 19; matrix products, arithmetic and copies ran while one was open for 22% -> 39% of each run, Pallas kernels for 0% -> 9%
where the time goes in v2:
time: 757 us; the launch traced here: 745 us
  matrix products  177 us (23%)
  local copies, waits for them, and re-layouts  165 us (22%)
  Pallas kernels  108 us (14%)
  other arithmetic  106 us (14%)
  waiting for transfers between devices  102 us (13%)
  starting transfers between devices  84.4 us (11%)
    ppermute x40, waiting for transfers between devices, send(): lax.ppermute(value, axis, [(i, i ^ 1 << bit) for i in range(self.sizes[ax...  73.9 us
    pallas_call x2, Pallas kernels, attend_back(): pl.pallas_call(partial(attend_back_kernel, holders, width, keys // 2, fir...  69.5 us
    dot_general x6, matrix products, project(): return jnp.einsum('rd,de->re', rows, weight, preferred_element_type=F32)  63.5 us
    convert_element_type x40, other arithmetic, half(): return total.astype(self.wire)  58.8 us
    dot_general x5, matrix products, back_project(): return jnp.einsum('re,de->rd', grads, weight, preferred_element_type=F32)  51.1 us
    dot_general x5, matrix products, weight_grad(): return jnp.einsum('rd,re->de', rows, grads, preferred_element_type=F32)  40.4 us
    ppermute x40, starting transfers between devices, send(): lax.ppermute(value, axis, [(i, i ^ 1 << bit) for i in range(self.sizes[ax...  38.5 us
    pallas_call x1, Pallas kernels, attend(): pl.pallas_call(partial(attend_kernel, holders, width, 288), out_shape=(ja...  38 us
  transfers between devices with their start and end apart: 58, of which 19 were waited for; matrix products, arithmetic and copies ran while one was open for 39% of the time, Pallas kernels for 9%

profile of v2, /device:TPU:0, one launch (start us, length us, event | category | flops | bytes accessed | tf_op | source)
XLA Modules:
  0.0 744.6 jit_solution(7365281109638816833)
XLA Ops:
  1.7 5.0 collective-permute-start.2
  12.7 7.1 fusion.16
  21.0 6.7 collective-permute-start
  35.0 3.0 copy.177
  38.3 14.2 %collective-permute-done.1 = bf16[288,1152]{1,0:T(8,128)(2,1)} collective-permute-done((bf16[288,1152]{1,0:T(8,128)(2,1)}, bf16[288,1152]{1,0:T(8,128)(2,1)}, u32[]{:S(2)}, u32[]{:S(2)}) %collective-permute-start.1) | collective-permute-done | bytes 663584 | tf_op jit(solution)/shard_map/ppermute | solution.py:91
  52.4 2.9 maximum_convert_fusion
  60.9 9.4 %convolution_convert_fusion.5.refs_0_ = bf16[576,3456]{1,0:T(8,128)(2,1)S(1)} fusion(bf16[1152,3456]{1,0:T(8,128)(2,1)} %param.39, f32[576,1152]{1,0:T(8,128)S(1)} %copy-done.1, f32[1152]{0:T(1024)S(1)} %copy-done.82, f32[1152]{0:T(1024)S(1)} %copy-done.69, f32[576]{0:T(1024)S(1)} %fusion.132, f32[576]{0:T(1024)S(1)} %broadcast_multiply_fusion.1), kind=kOutput, calls=%fused_computation.23 | convolution fusion | flops 4591779840 | bytes 14611968 | tf_op jit(solution)/shard_map/rd,de->re/dot_general | solution.py:54
  74.5 5.1 collective-permute-start.6
  86.2 3.5 dynamic-slice_bitcast_fusion.1
  90.8 38.0 %attend.1 = (bf16[576,1152]{1,0:T(8,128)(2,1)}, f32[576,128]{1,0:T(8,128)}) custom-call(bf16[576,3456]{1,0:T(8,128)(2,1)} %copy-done.37, bf16[576,2304]{1,0:T(8,128)(2,1)} %collective-permute-done.4.refs_1_, f32[1152,128]{1,0:T(8,128)} %broadcast_in_dim.35.refs_2_), custom_call_target="tpu_custom_call" | custom-call | flops 21743271936 | bytes 10616832 | tf_op jit(solution)/shard_map/attend/pallas_call | solution.py:254
  128.9 3.6 fusion.191
  133.3 34.9 %multiply_convert_fusion = (bf16[576,4608]{1,0:T(8,128)(2,1)S(1)}, f32[576,4608]{1,0:T(8,128)}, f32[576,4608]{1,0:T(8,128)}) fusion(f32[4608]{0:T(1024)S(1)} %copy-done.76, bf16[1152,4608]{1,0:T(8,128)(2,1)} %param.44, f32[576,1152]{1,0:T(8,128)S(1)} %get-tuple-element.372, f32[1152]{0:T(1024)S(1)} %copy-done.80, f32[1152]{0:T(1024)S(1)} %copy-done.68, ...), kind=kOutput, calls=%fused_computation.8 | convolution fusion | flops 6293790720 | bytes 39845376 | tf_op jit(solution)/shard_map/rd,de->re/dot_general | solution.py:54
  168.3 8.2 %fusion.192 = (bf16[576,1152]{1,0:T(8,128)(2,1)}, f32[576,1152]{1,0:T(8,128)S(1)}) fusion(f32[1152]{0:T(1024)S(1)} %copy-done.79, f32[576,1152]{1,0:T(8,128)S(1)} %get-tuple-element.372, bf16[576,4608]{1,0:T(8,128)(2,1)S(1)} %get-tuple-element.245, bf16[4608,1152]{1,0:T(8,128)(2,1)S(1)} %bitcast.510), kind=kOutput, calls=%fused_computation.455 | convolution fusion | flops 6117285888 | bytes 22565376 | tf_op jit(solution)/shard_map/rd,de->re/dot_general | solution.py:54
  183.7 11.6 %convolution_convert_fusion.1 = bf16[4608,1152]{1,0:T(8,128)(2,1)} fusion(bf16[576,4608]{1,0:T(8,128)(2,1)S(1)} %get-tuple-element.245, bf16[576,1152]{1,0:T(8,128)(2,1)S(1)} %fusion.25), kind=kOutput, calls=%fused_computation.1 | convolution fusion | flops 6120603648 | bytes 17252352 | tf_op jit(solution)/shard_map/rd,re->de/dot_general | solution.py:58
  195.3 8.8 %constant_dynamic-slice_fusion.27 = (bf16[4,1,576,1152]{3,2,1,0:T(8,128)(2,1)}, bf16[4,1,576,1152]{3,2,1,0:T(8,128)(2,1)}) fusion(bf16[4,2,576,1152]{3,2,1,0:T(8,128)(2,1)} %bitcast.446, s32[]{:T(128)S(6)} %select_n.342, s32[]{:T(128)S(6)} %select_n.344), kind=kLoop, calls=%fused_computation.336 | loop fusion | bytes 21233672 | tf_op jit(solution)/shard_map/jit(dynamic_index_in_dim)/dynamic_slice | solution.py:150
  204.1 3.2 collective-permute-start.15
  211.9 19.2 %convert_reduce_fusion = (f32[4608]{0:T(1024)S(1)}, bf16[576,4608]{1,0:T(8,128)(2,1)}) fusion(f32[576,4608]{1,0:T(8,128)} %get-tuple-element.246, f32[576,4608]{1,0:T(8,128)} %get-tuple-element.373, f32[4608]{0:T(1024)S(1)} %copy-done.76, bf16[576,1152]{1,0:T(8,128)(2,1)} %copy-done.38, bf16[4608,1152]{1,0:T(8,128)(2,1)} %param.46), kind=kOutput, calls=%fused_computation.6 | convolution fusion | flops 6160412160 | bytes 38522880 | tf_op jit(solution)/shard_map/re,de->rd/dot_general | solution.py:62
  231.1 3.2 slice.455
  234.3 3.7 slice.453
  250.8 4.8 collective-permute-done.10
  272.2 11.6 %convolution_convert_fusion = bf16[1152,4608]{1,0:T(8,128)(2,1)} fusion(bf16[576,4608]{1,0:T(8,128)(2,1)S(1)} %bitcast.514, f32[576,1152]{1,0:T(8,128)S(1)} %copy-done.8, f32[1152]{0:T(1024)S(1)} %copy-done.81, f32[1152]{0:T(1024)S(1)} %copy-done.68, f32[576]{0:T(1024)S(1)} %fusion.133, f32[576]{0:T(1024)S(1)} %broadcast_multiply_fusion), kind=kOutput, calls=%fused_computation | convolution fusion | flops 6123921408 | bytes 18593280 | tf_op jit(solution)/shard_map/rd,re->de/dot_general | solution.py:58
  283.9 8.8 %constant_dynamic-slice_fusion.25 = (bf16[4,1,144,4608]{3,2,1,0:T(8,128)(2,1)}, bf16[4,1,144,4608]{3,2,1,0:T(8,128)(2,1)}) fusion(bf16[4,2,144,4608]{3,2,1,0:T(8,128)(2,1)} %bitcast.447, s32[]{:T(128)S(6)} %select_n.342, s32[]{:T(128)S(6)} %select_n.344), kind=kLoop, calls=%fused_computation.334 | loop fusion | bytes 21233672 | tf_op jit(solution)/shard_map/jit(dynamic_index_in_dim)/dynamic_slice | solution.py:150
  299.4 14.2 %multiply_reduce_fusion = (f32[1152]{0:T(1024)}, f32[576]{0:T(1024)S(1)}, f32[1152]{0:T(1024)}, f32[576,1152]{1,0:T(8,128)S(1)}) fusion(f32[576,1152]{1,0:T(8,128)} %copy-done.7, f32[576]{0:T(1024)S(1)} %fusion.133, f32[576]{0:T(1024)S(1)} %broadcast_multiply_fusion, f32[1152]{0:T(1024)S(1)} %copy-done.68, bf16[576,4608]{1,0:T(8,128)(2,1)} %get-tuple-element.99, ...), kind=kOutput, calls=%fused_computation.56 | convolution fusion | flops 6120601088 | bytes 21254400 | tf_op jit(solution)/shard_map/re,de->rd/dot_general | solution.py:62
  318.1 7.0 collective-permute-done.21
  327.7 4.9 collective-permute-done.20
  346.9 3.1 convolution_convert_fusion.6.refs_5_
  352.1 30.7 %attend_back.2 = (bf16[8,576,128]{2,1,0:T(8,128)(2,1)}, bf16[2,8,1152,128]{3,2,1,0:T(8,128)(2,1)}) custom-call(bf16[576,3456]{1,0:T(8,128)(2,1)} %copy-done.37, bf16[576,2304]{1,0:T(8,128)(2,1)} %collective-permute-done.4.refs_1_, f32[1152,128]{1,0:T(8,128)} %broadcast_in_dim.35.refs_2_, bf16[576,1152]{1,0:T(8,128)(2,1)} %get-tuple-element.92.refs_3_, ...), custom_call_target="tpu_custom_call" | custom-call | flops 27179089920 | bytes 21233664 | tf_op jit(solution)/shard_map/attend_back/pallas_call | solution.py:356
  385.2 12.1 %collective-permute-start.13 = (bf16[288,2304]{1,0:T(8,128)(2,1)}, bf16[288,2304]{1,0:T(8,128)(2,1)}, u32[]{:S(2)}, u32[]{:S(2)}) collective-permute-start(bf16[288,2304]{1,0:T(8,128)(2,1)} %get-tuple-element.280), channel_id=1, source_target_pairs={{0,0},{1,1},{2,4},{3,5},{4,2},{5,3},{6,6},{7,7},{8,8},{9,9},{10,12... | collective-permute-start | bytes 3981320 | tf_op jit(solution)/shard_map/ppermute | solution.py:91
  417.2 38.8 %attend_back.3 = (bf16[576,1152]{1,0:T(8,128)(2,1)}, bf16[576,2304]{1,0:T(8,128)(2,1)}, bf16[576,2304]{1,0:T(8,128)(2,1)}) custom-call(bf16[576,3456]{1,0:T(8,128)(2,1)} %copy-done.37, bf16[576,2304]{1,0:T(8,128)(2,1)} %collective-permute-done.4.refs_1_, f32[1152,128]{1,0:T(8,128)} %broadcast_in_dim.35.refs_2_, bf16[576,1152]{1,0:T(8,128)(2,1)} %get-tuple-element.92.refs_3_, ...), custom_call_target="tpu_custom_call" | custom-call | flops 27179089920 | bytes 21233664 | tf_op jit(solution)/shard_map/attend_back/pallas_call | solution.py:356
  504.3 3.3 collective-permute-done.52
  521.0 3.2 add_convert_fusion.1
  527.0 7.9 %convolution_convert_fusion.2 = bf16[1152,3456]{1,0:T(8,128)(2,1)S(1)} fusion(f32[576,1152]{1,0:T(8,128)S(1)} %copy-done.3, f32[1152]{0:T(1024)S(1)} %copy-done.83, f32[1152]{0:T(1024)S(1)} %copy-done.70, f32[576]{0:T(1024)S(1)} %copy-done.66, f32[576]{0:T(1024)S(1)} %copy-done.54, bf16[576,2304]{1,0:T(8,128)(2,1)S(1)} %add_convert_fusion.1, ...), kind=kOutput, calls=%fused_computation.3 | convolution fusion | flops 4601733120 | bytes 14611968 | tf_op jit(solution)/shard_map/rd,re->de/dot_general | solution.py:58
  534.9 3.8 constant_dynamic-slice_fusion.13
  538.7 10.9 %multiply_reduce_fusion.1 = (f32[1152]{0:T(1024)}, f32[576]{0:T(1024)S(1)}, f32[1152]{0:T(1024)}, f32[576,1152]{1,0:T(8,128)S(1)}) fusion(f32[576,1152]{1,0:T(8,128)S(1)} %copy-done.3, f32[576]{0:T(1024)S(1)} %copy-done.66, f32[576]{0:T(1024)S(1)} %copy-done.54, f32[1152]{0:T(1024)S(1)} %copy-done.70, bf16[576,3456]{1,0:T(8,128)(2,1)} %pad_maximum_fusion, ...), kind=kOutput, calls=%fused_computation.57 | convolution fusion | flops 4591777280 | bytes 17273088 | tf_op jit(solution)/shard_map/re,de->rd/dot_general | solution.py:62
  579.8 2.9 collective-permute-start.54
  594.7 4.1 collective-permute-done.43
  598.8 3.3 collective-permute-start.44
  602.1 7.3 collective-permute-done.56
  611.4 2.9 slice.467
  624.9 6.6 convolution_convert_fusion.3
  641.0 8.7 %collective-permute-done.32 = bf16[288,1152]{1,0:T(8,128)(2,1)S(1)} collective-permute-done((bf16[288,1152]{1,0:T(8,128)(2,1)S(1)}, bf16[288,1152]{1,0:T(8,128)(2,1)S(1)}, u32[]{:S(2)}, u32[]{:S(2)}) %collective-permute-start.32) | collective-permute-done | bytes 663584 | tf_op jit(solution)/shard_map/ppermute | solution.py:96
  649.9 3.6 fusion.10
  653.6 8.3 %collective-permute-done.47 = bf16[288,1664]{1,0:T(8,128)(2,1)S(1)} collective-permute-done((bf16[288,1664]{1,0:T(8,128)(2,1)S(1)}, bf16[288,1664]{1,0:T(8,128)(2,1)S(1)}, u32[]{:S(2)}, u32[]{:S(2)}) %collective-permute-start.47) | collective-permute-done | bytes 958496 | tf_op jit(solution)/shard_map/ppermute | solution.py:166
  672.7 3.4 collective-permute-done.48
  693.8 7.7 %collective-permute-done.36 = bf16[576,512]{1,0:T(8,128)(2,1)} collective-permute-done((bf16[576,512]{1,0:T(8,128)(2,1)}, bf16[576,512]{1,0:T(8,128)(2,1)}, u32[]{:S(2)}, u32[]{:S(2)}) %collective-permute-start.36) | collective-permute-done | bytes 589856 | tf_op jit(solution)/shard_map/ppermute | solution.py:166
  704.3 4.5 collective-permute-done.34
  725.5 9.0 %collective-permute-done.38 = bf16[144,1152]{1,0:T(8,128)(2,1)S(1)} collective-permute-done((bf16[144,1152]{1,0:T(8,128)(2,1)S(1)}, bf16[144,1152]{1,0:T(8,128)(2,1)S(1)}, u32[]{:S(2)}, u32[]{:S(2)}) %collective-permute-start.38) | collective-permute-done | bytes 331808 | tf_op jit(solution)/shard_map/ppermute | solution.py:166
  734.5 6.8 collective-permute-done.50
  (550 shorter events, 306.0 us)
Async XLA Ops:
  1.7 29.0 %collective-permute-start.2 = (f32[2,4,64,1]{2,1,3,0:T(4,128)S(1)}, f32[2,4,64,1]{2,1,3,0:T(4,128)S(1)}, u32[]{:S(2)}, u32[]{:S(2)}) collective-permute-start(f32[2,4,64,1]{2,1,3,0:T(4,128)S(1)} %get-tuple-element.348), channel_id=1, source_target_pairs={{0,1},{1,2},{2,3},{4,5},{5,6},{6,7},{8,9},{9,10},{10,11},{12,13},{... | collective-permute-start | bytes 6152 | tf_op jit(solution)/shard_map/ppermute | solution.py:32
  6.7 24.0 %collective-permute-start.3 = (f32[2,4,64,1]{2,1,3,0:T(4,128)S(1)}, f32[2,4,64,1]{2,1,3,0:T(4,128)S(1)}, u32[]{:S(2)}, u32[]{:S(2)}) collective-permute-start(f32[2,4,64,1]{2,1,3,0:T(4,128)S(1)} %get-tuple-element.349), channel_id=1, source_target_pairs={{1,0},{2,1},{3,2},{5,4},{6,5},{7,6},{9,8},{10,9},{11,10},{13,12},{... | collective-permute-start | bytes 6152 | tf_op jit(solution)/shard_map/ppermute | solution.py:35
  21.0 17.2 %collective-permute-start = (bf16[288,1152]{1,0:T(8,128)(2,1)}, bf16[288,1152]{1,0:T(8,128)(2,1)}, u32[]{:S(2)}, u32[]{:S(2)}) collective-permute-start(bf16[288,1152]{1,0:T(8,128)(2,1)} %get-tuple-element.316), channel_id=1, source_target_pairs={{0,0},{1,1},{2,4},{3,5},{4,2},{5,3},{6,6},{7,7},{8,8},{9,9},{10,12... | collective-permute-start | bytes 1990664 | tf_op jit(solution)/shard_map/ppermute | solution.py:91
  27.7 24.7 %collective-permute-start.1 = (bf16[288,1152]{1,0:T(8,128)(2,1)}, bf16[288,1152]{1,0:T(8,128)(2,1)}, u32[]{:S(2)}, u32[]{:S(2)}) collective-permute-start(bf16[288,1152]{1,0:T(8,128)(2,1)} %get-tuple-element.317), channel_id=1, source_target_pairs={{0,1},{1,0},{2,5},{3,4},{4,3},{5,2},{6,7},{7,6},{8,9},{9,8},{10,13... | collective-permute-start | bytes 1990664 | tf_op jit(solution)/shard_map/ppermute | solution.py:91
  74.0 15.8 %collective-permute-start.4 = (bf16[576,2304]{1,0:T(8,128)(2,1)}, bf16[576,2304]{1,0:T(8,128)(2,1)}, u32[]{:S(2)}, u32[]{:S(2)}) collective-permute-start(bf16[576,2304]{1,0:T(8,128)(2,1)} %slice.434), channel_id=1, source_target_pairs={{0,4},{1,5},{2,6},{3,7},{4,0},{5,1},{6,2},{7,3},{8,12},{9,13},{10,... | collective-permute-start | bytes 7962632 | tf_op jit(solution)/shard_map/ppermute | solution.py:112
  74.5 9.3 %collective-permute-start.6 = (f32[25,1152]{1,0:T(8,128)S(1)}, f32[25,1152]{1,0:T(8,128)S(1)}, u32[]{:S(2)}, u32[]{:S(2)}) collective-permute-start(f32[25,1152]{1,0:T(8,128)S(1)} %get-tuple-element.332), channel_id=1, source_target_pairs={{0,1},{1,0},{2,5},{3,4},{4,3},{5,2},{6,7},{7,6},{8,9},{9,8},{10,13... | collective-permute-start | bytes 345608 | tf_op jit(solution)/shard_map/ppermute | solution.py:91
  204.1 58.5 %collective-permute-start.15 = (bf16[2304,1152]{1,0:T(8,128)(2,1)}, bf16[2304,1152]{1,0:T(8,128)(2,1)}, u32[]{:S(2)}, u32[]{:S(2)}) collective-permute-start(bf16[2304,1152]{1,0:T(8,128)(2,1)} %bitcast.467), channel_id=1, source_target_pairs={{0,4},{4,0},{8,12},{12,8},{16,20},{20,16},{24,28},{28,24},{1,5},{5... | collective-permute-start | bytes 15925256 | tf_op jit(solution)/shard_map/ppermute | solution.py:166
  207.3 34.3 %collective-permute-start.7 = (f32[256,16]{0,1:T(8,128)S(1)}, f32[256,16]{0,1:T(8,128)S(1)}, u32[]{:S(2)}, u32[]{:S(2)}) collective-permute-start(f32[256,16]{0,1:T(8,128)S(1)} %get-tuple-element.354), channel_id=1, source_target_pairs={{0,0},{1,1},{4,2},{5,3},{2,4},{3,5},{6,6},{7,7},{8,8},{9,9},{12,10... | collective-permute-start | bytes 49160 | tf_op jit(solution)/shard_map/ppermute | solution.py:96
  208.0 33.7 %collective-permute-start.8 = (f32[256,16]{0,1:T(8,128)S(1)}, f32[256,16]{0,1:T(8,128)S(1)}, u32[]{:S(2)}, u32[]{:S(2)}) collective-permute-start(f32[256,16]{0,1:T(8,128)S(1)} %get-tuple-element.355), channel_id=1, source_target_pairs={{1,0},{0,1},{5,2},{4,3},{3,4},{2,5},{7,6},{6,7},{9,8},{8,9},{13,10... | collective-permute-start | bytes 49160 | tf_op jit(solution)/shard_map/ppermute | solution.py:96
  292.7 41.4 %collective-permute-start.16 = (bf16[576,4608]{1,0:T(8,128)(2,1)}, bf16[576,4608]{1,0:T(8,128)(2,1)}, u32[]{:S(2)}, u32[]{:S(2)}) collective-permute-start(bf16[576,4608]{1,0:T(8,128)(2,1)} %bitcast.468), channel_id=1, source_target_pairs={{0,4},{4,0},{8,12},{12,8},{16,20},{20,16},{24,28},{28,24},{1,5},{5... | collective-permute-start | bytes 15925256 | tf_op jit(solution)/shard_map/ppermute | solution.py:166
  296.4 28.7 %collective-permute-start.21 = (bf16[1152,512]{1,0:T(8,128)(2,1)}, bf16[1152,512]{1,0:T(8,128)(2,1)}, u32[]{:S(2)}, u32[]{:S(2)}) collective-permute-start(bf16[1152,512]{1,0:T(8,128)(2,1)} %get-tuple-element.106), channel_id=1, source_target_pairs={{0,16},{4,20},{8,24},{12,28},{16,0},{20,4},{24,8},{28,12},{1,17},{... | collective-permute-start | bytes 3538952 | tf_op jit(solution)/shard_map/ppermute | solution.py:166
  297.9 34.6 %collective-permute-start.20 = (bf16[1152,640]{1,0:T(8,128)(2,1)}, bf16[1152,640]{1,0:T(8,128)(2,1)S(1)}, u32[]{:S(2)}, u32[]{:S(2)}) collective-permute-start(bf16[1152,640]{1,0:T(8,128)(2,1)} %bitcast.486), channel_id=1, source_target_pairs={{0,8},{4,12},{8,0},{12,4},{16,24},{20,28},{24,16},{28,20},{1,9},{5... | collective-permute-start | bytes 4423688 | tf_op jit(solution)/shard_map/ppermute | solution.py:166
  340.5 65.7 %collective-permute-start.17 = (bf16[288,2304]{1,0:T(8,128)(2,1)}, bf16[288,2304]{1,0:T(8,128)(2,1)}, u32[]{:S(2)}, u32[]{:S(2)}) collective-permute-start(bf16[288,2304]{1,0:T(8,128)(2,1)} %bitcast.69), channel_id=1, source_target_pairs={{0,8},{4,12},{8,0},{12,4},{16,24},{20,28},{24,16},{28,20},{1,9},{5... | collective-permute-start | bytes 3981320 | tf_op jit(solution)/shard_map/ppermute | solution.py:166
  342.0 66.9 %collective-permute-start.18 = (bf16[288,2304]{1,0:T(8,128)(2,1)}, bf16[288,2304]{1,0:T(8,128)(2,1)}, u32[]{:S(2)}, u32[]{:S(2)}) collective-permute-start(bf16[288,2304]{1,0:T(8,128)(2,1)} %get-tuple-element.101), channel_id=1, source_target_pairs={{0,16},{4,20},{8,24},{12,28},{16,0},{20,4},{24,8},{28,12},{1,17},{... | collective-permute-start | bytes 3981320 | tf_op jit(solution)/shard_map/ppermute | solution.py:166
  350.0 35.2 %collective-permute-start.27 = (bf16[576,512]{1,0:T(8,128)(2,1)}, bf16[576,512]{1,0:T(8,128)(2,1)S(1)}, u32[]{:S(2)}, u32[]{:S(2)}) collective-permute-start(bf16[576,512]{1,0:T(8,128)(2,1)} %get-tuple-element.118), channel_id=1, source_target_pairs={{0,8},{4,12},{8,0},{12,4},{16,24},{20,28},{24,16},{28,20},{1,9},{5... | collective-permute-start | bytes 1769480 | tf_op jit(solution)/shard_map/ppermute | solution.py:166
  350.6 49.1 %collective-permute-start.26 = (bf16[576,640]{1,0:T(8,128)(2,1)}, bf16[576,640]{1,0:T(8,128)(2,1)}, u32[]{:S(2)}, u32[]{:S(2)}) collective-permute-start(bf16[576,640]{1,0:T(8,128)(2,1)} %get-tuple-element.117), channel_id=1, source_target_pairs={{0,16},{4,20},{8,24},{12,28},{16,0},{20,4},{24,8},{28,12},{1,17},{... | collective-permute-start | bytes 2211848 | tf_op jit(solution)/shard_map/ppermute | solution.py:166
  352.1 49.8 %collective-permute-start.19 = (bf16[576,1152]{1,0:T(8,128)(2,1)}, bf16[576,1152]{1,0:T(8,128)(2,1)}, u32[]{:S(2)}, u32[]{:S(2)}) collective-permute-start(bf16[576,1152]{1,0:T(8,128)(2,1)} %bitcast.81), channel_id=1, source_target_pairs={{0,4},{4,0},{8,12},{12,8},{16,20},{20,16},{24,28},{28,24},{1,5},{5... | collective-permute-start | bytes 3981320 | tf_op jit(solution)/shard_map/ppermute | solution.py:166
  385.2 238.9 %collective-permute-start.13 = (bf16[288,2304]{1,0:T(8,128)(2,1)}, bf16[288,2304]{1,0:T(8,128)(2,1)}, u32[]{:S(2)}, u32[]{:S(2)}) collective-permute-start(bf16[288,2304]{1,0:T(8,128)(2,1)} %get-tuple-element.280), channel_id=1, source_target_pairs={{0,0},{1,1},{2,4},{3,5},{4,2},{5,3},{6,6},{7,7},{8,8},{9,9},{10,12... | collective-permute-start | bytes 3981320 | tf_op jit(solution)/shard_map/ppermute | solution.py:91
  411.6 48.5 %collective-permute-start.25 = (bf16[288,512]{1,0:T(8,128)(2,1)}, bf16[288,512]{1,0:T(8,128)(2,1)}, u32[]{:S(2)}, u32[]{:S(2)}) collective-permute-start(bf16[288,512]{1,0:T(8,128)(2,1)} %get-tuple-element.116), channel_id=1, source_target_pairs={{0,16},{4,20},{8,24},{12,28},{16,0},{20,4},{24,8},{28,12},{1,17},{... | collective-permute-start | bytes 884744 | tf_op jit(solution)/shard_map/ppermute | solution.py:166
  412.1 49.9 %collective-permute-start.24 = (bf16[288,640]{1,0:T(8,128)(2,1)}, bf16[288,640]{1,0:T(8,128)(2,1)}, u32[]{:S(2)}, u32[]{:S(2)}) collective-permute-start(bf16[288,640]{1,0:T(8,128)(2,1)} %bitcast.83), channel_id=1, source_target_pairs={{0,8},{4,12},{8,0},{12,4},{16,24},{20,28},{24,16},{28,20},{1,9},{5... | collective-permute-start | bytes 1105928 | tf_op jit(solution)/shard_map/ppermute | solution.py:166
  413.6 51.0 %collective-permute-start.28 = (bf16[288,1152]{1,0:T(8,128)(2,1)}, bf16[288,1152]{1,0:T(8,128)(2,1)}, u32[]{:S(2)}, u32[]{:S(2)}) collective-permute-start(bf16[288,1152]{1,0:T(8,128)(2,1)} %pad_maximum_fusion.4), channel_id=1, source_target_pairs={{0,1},{1,0},{2,3},{3,2},{4,5},{5,4},{6,7},{7,6},{8,9},{9,8},{10,11... | collective-permute-start | bytes 1990664 | tf_op jit(solution)/shard_map/ppermute | solution.py:166
  415.7 53.1 %collective-permute-start.22 = (bf16[144,2304]{1,0:T(8,128)(2,1)}, bf16[144,2304]{1,0:T(8,128)(2,1)}, u32[]{:S(2)}, u32[]{:S(2)}) collective-permute-start(bf16[144,2304]{1,0:T(8,128)(2,1)} %get-tuple-element.113), channel_id=1, source_target_pairs={{0,16},{4,20},{8,24},{12,28},{16,0},{20,4},{24,8},{28,12},{1,17},{... | collective-permute-start | bytes 1990664 | tf_op jit(solution)/shard_map/ppermute | solution.py:166
  460.1 164.0 %collective-permute-start.14 = (bf16[288,2304]{1,0:T(8,128)(2,1)}, bf16[288,2304]{1,0:T(8,128)(2,1)}, u32[]{:S(2)}, u32[]{:S(2)}) collective-permute-start(bf16[288,2304]{1,0:T(8,128)(2,1)} %get-tuple-element.281), channel_id=1, source_target_pairs={{0,1},{1,0},{2,5},{3,4},{4,3},{5,2},{6,7},{7,6},{8,9},{9,8},{10,13... | collective-permute-start | bytes 3981320 | tf_op jit(solution)/shard_map/ppermute | solution.py:91
  462.1 14.8 %collective-permute-start.23 = (bf16[144,2304]{1,0:T(8,128)(2,1)}, bf16[144,2304]{1,0:T(8,128)(2,1)}, u32[]{:S(2)}, u32[]{:S(2)}) collective-permute-start(bf16[144,2304]{1,0:T(8,128)(2,1)} %get-tuple-element.114), channel_id=1, source_target_pairs={{0,8},{4,12},{8,0},{12,4},{16,24},{20,28},{24,16},{28,20},{1,9},{5... | collective-permute-start | bytes 1990664 | tf_op jit(solution)/shard_map/ppermute | solution.py:166
  464.6 29.7 %collective-permute-start.11 = (bf16[20,1152]{1,0:T(8,128)(2,1)}, bf16[20,1152]{1,0:T(8,128)(2,1)}, u32[]{:S(2)}, u32[]{:S(2)}) collective-permute-start(bf16[20,1152]{1,0:T(8,128)(2,1)} %get-tuple-element.314), channel_id=1, source_target_pairs={{0,0},{1,1},{4,2},{5,3},{2,4},{3,5},{6,6},{7,7},{8,8},{9,9},{12,10... | collective-permute-start | bytes 138248 | tf_op jit(solution)/shard_map/ppermute | solution.py:96
  468.7 25.6 %collective-permute-start.12 = (bf16[20,1152]{1,0:T(8,128)(2,1)}, bf16[20,1152]{1,0:T(8,128)(2,1)}, u32[]{:S(2)}, u32[]{:S(2)}) collective-permute-start(bf16[20,1152]{1,0:T(8,128)(2,1)} %get-tuple-element.315), channel_id=1, source_target_pairs={{1,0},{0,1},{5,2},{4,3},{3,4},{2,5},{7,6},{6,7},{9,8},{8,9},{13,10... | collective-permute-start | bytes 138248 | tf_op jit(solution)/shard_map/ppermute | solution.py:96
  484.7 34.7 %collective-permute-start.29 = (bf16[576,2304]{1,0:T(8,128)(2,1)}, bf16[576,2304]{1,0:T(8,128)(2,1)}, u32[]{:S(2)}, u32[]{:S(2)}) collective-permute-start(bf16[576,2304]{1,0:T(8,128)(2,1)} %get-tuple-element.135), channel_id=1, source_target_pairs={{0,4},{1,5},{2,6},{3,7},{4,0},{5,1},{6,2},{7,3},{8,12},{9,13},{10,... | collective-permute-start | bytes 7962632 | tf_op jit(solution)/shard_map/ppermute | solution.py:112
  507.6 60.3 %collective-permute-start.57 = (bf16[144,1152]{1,0:T(8,128)(2,1)}, bf16[144,1152]{1,0:T(8,128)(2,1)}, u32[]{:S(2)}, u32[]{:S(2)}) collective-permute-start(bf16[144,1152]{1,0:T(8,128)(2,1)} %fusion.59), channel_id=1, source_target_pairs={{0,2},{1,3},{2,0},{3,1},{4,6},{5,7},{6,4},{7,5},{8,10},{9,11},{10,... | collective-permute-start | bytes 995336 | tf_op jit(solution)/shard_map/ppermute | solution.py:166
  512.4 67.3 %collective-permute-start.55 = (bf16[72,4608]{1,0:T(8,128)(2,1)}, bf16[72,4608]{1,0:T(8,128)(2,1)}, u32[]{:S(2)}, u32[]{:S(2)}) collective-permute-start(bf16[72,4608]{1,0:T(8,128)(2,1)} %pad_maximum_fusion.3), channel_id=1, source_target_pairs={{0,1},{1,0},{2,3},{3,2},{4,5},{5,4},{6,7},{7,6},{8,9},{9,8},{10,11... | collective-permute-start | bytes 1990664 | tf_op jit(solution)/shard_map/ppermute | solution.py:166
  519.4 50.7 %collective-permute-start.53 = (bf16[72,1152]{1,0:T(8,128)(2,1)}, bf16[72,1152]{1,0:T(8,128)(2,1)}, u32[]{:S(2)}, u32[]{:S(2)}) collective-permute-start(bf16[72,1152]{1,0:T(8,128)(2,1)} %pad_maximum_fusion.8), channel_id=1, source_target_pairs={{0,1},{1,0},{2,3},{3,2},{4,5},{5,4},{6,7},{7,6},{8,9},{9,8},{10,11... | collective-permute-start | bytes 497672 | tf_op jit(solution)/shard_map/ppermute | solution.py:166
  571.7 46.4 %collective-permute-start.30 = (bf16[576,3456]{1,0:T(8,128)(2,1)}, bf16[576,3456]{1,0:T(8,128)(2,1)}, u32[]{:S(2)}, u32[]{:S(2)}) collective-permute-start(bf16[576,3456]{1,0:T(8,128)(2,1)} %bitcast.475), channel_id=1, source_target_pairs={{0,4},{4,0},{8,12},{12,8},{16,20},{20,16},{24,28},{28,24},{1,5},{5... | collective-permute-start | bytes 11943944 | tf_op jit(solution)/shard_map/ppermute | solution.py:166
  579.8 12.8 %collective-permute-start.54 = (bf16[36,1152]{1,0:T(8,128)(2,1)}, bf16[36,1152]{1,0:T(8,128)(2,1)}, u32[]{:S(2)}, u32[]{:S(2)}) collective-permute-start(bf16[36,1152]{1,0:T(8,128)(2,1)} %fusion.82), channel_id=1, source_target_pairs={{0,2},{1,3},{2,0},{3,1},{4,6},{5,7},{6,4},{7,5},{8,10},{9,11},{10,... | collective-permute-start | bytes 248840 | tf_op jit(solution)/shard_map/ppermute | solution.py:166
  591.7 17.6 %collective-permute-start.56 = (bf16[36,4608]{1,0:T(8,128)(2,1)}, bf16[36,4608]{1,0:T(8,128)(2,1)}, u32[]{:S(2)}, u32[]{:S(2)}) collective-permute-start(bf16[36,4608]{1,0:T(8,128)(2,1)} %fusion.56), channel_id=1, source_target_pairs={{0,2},{1,3},{2,0},{3,1},{4,6},{5,7},{6,4},{7,5},{8,10},{9,11},{10,... | collective-permute-start | bytes 995336 | tf_op jit(solution)/shard_map/ppermute | solution.py:166
  598.8 17.0 %collective-permute-start.44 = (f32[1,1280]{1,0:T(1,128)S(1)}, f32[1,1280]{1,0:T(1,128)S(1)}, u32[]{:S(2)}, u32[]{:S(2)}) collective-permute-start(f32[1,1280]{1,0:T(1,128)S(1)} %fusion.127), channel_id=1, source_target_pairs={{0,2},{1,3},{2,0},{3,1},{4,6},{5,7},{6,4},{7,5},{8,10},{9,11},{10,... | collective-permute-start | bytes 15368 | tf_op jit(solution)/shard_map/ppermute | solution.py:166
  634.4 15.3 %collective-permute-start.32 = (bf16[288,1152]{1,0:T(8,128)(2,1)S(1)}, bf16[288,1152]{1,0:T(8,128)(2,1)S(1)}, u32[]{:S(2)}, u32[]{:S(2)}) collective-permute-start(bf16[288,1152]{1,0:T(8,128)(2,1)S(1)} %get-tuple-element.313), channel_id=1, source_target_pairs={{1,0},{0,1},{5,2},{4,3},{3,4},{2,5},{7,6},{6,7},{9,8},{8,9},{13,10... | collective-permute-start | bytes 1990664 | tf_op jit(solution)/shard_map/ppermute | solution.py:96
  638.6 23.2 %collective-permute-start.47 = (bf16[288,1664]{1,0:T(8,128)(2,1)S(1)}, bf16[288,1664]{1,0:T(8,128)(2,1)S(1)}, u32[]{:S(2)}, u32[]{:S(2)}) collective-permute-start(bf16[288,1664]{1,0:T(8,128)(2,1)S(1)} %get-tuple-element.142), channel_id=1, source_target_pairs={{0,16},{4,20},{8,24},{12,28},{16,0},{20,4},{24,8},{28,12},{1,17},{... | collective-permute-start | bytes 2875400 | tf_op jit(solution)/shard_map/ppermute | solution.py:166
  639.4 25.3 %collective-permute-start.45 = (bf16[288,1792]{1,0:T(8,128)(2,1)S(1)}, bf16[288,1792]{1,0:T(8,128)(2,1)S(1)}, u32[]{:S(2)}, u32[]{:S(2)}) collective-permute-start(bf16[288,1792]{1,0:T(8,128)(2,1)S(1)} %bitcast.497), channel_id=1, source_target_pairs={{0,8},{4,12},{8,0},{12,4},{16,24},{20,28},{24,16},{28,20},{1,9},{5... | collective-permute-start | bytes 3096584 | tf_op jit(solution)/shard_map/ppermute | solution.py:166
  639.9 42.7 %collective-permute-start.33 = (bf16[1152,1152]{1,0:T(8,128)(2,1)}, bf16[1152,1152]{1,0:T(8,128)(2,1)}, u32[]{:S(2)}, u32[]{:S(2)}) collective-permute-start(bf16[1152,1152]{1,0:T(8,128)(2,1)} %bitcast.117), channel_id=1, source_target_pairs={{0,4},{4,0},{8,12},{12,8},{16,20},{20,16},{24,28},{28,24},{1,5},{5... | collective-permute-start | bytes 7962632 | tf_op jit(solution)/shard_map/ppermute | solution.py:166
  663.1 13.0 %collective-permute-start.48 = (bf16[144,1664]{1,0:T(8,128)(2,1)}, bf16[144,1664]{1,0:T(8,128)(2,1)}, u32[]{:S(2)}, u32[]{:S(2)}) collective-permute-start(bf16[144,1664]{1,0:T(8,128)(2,1)} %get-tuple-element.301), channel_id=1, source_target_pairs={{0,8},{4,12},{8,0},{12,4},{16,24},{20,28},{24,16},{28,20},{1,9},{5... | collective-permute-start | bytes 1437704 | tf_op jit(solution)/shard_map/ppermute | solution.py:166
  665.9 14.8 %collective-permute-start.46 = (bf16[144,1792]{1,0:T(8,128)(2,1)}, bf16[144,1792]{1,0:T(8,128)(2,1)}, u32[]{:S(2)}, u32[]{:S(2)}) collective-permute-start(bf16[144,1792]{1,0:T(8,128)(2,1)} %get-tuple-element.299), channel_id=1, source_target_pairs={{0,16},{4,20},{8,24},{12,28},{16,0},{20,4},{24,8},{28,12},{1,17},{... | collective-permute-start | bytes 1548296 | tf_op jit(solution)/shard_map/ppermute | solution.py:166
  685.6 15.9 %collective-permute-start.36 = (bf16[576,512]{1,0:T(8,128)(2,1)}, bf16[576,512]{1,0:T(8,128)(2,1)}, u32[]{:S(2)}, u32[]{:S(2)}) collective-permute-start(bf16[576,512]{1,0:T(8,128)(2,1)} %get-tuple-element.295), channel_id=1, source_target_pairs={{0,16},{4,20},{8,24},{12,28},{16,0},{20,4},{24,8},{28,12},{1,17},{... | collective-permute-start | bytes 1769480 | tf_op jit(solution)/shard_map/ppermute | solution.py:166
  689.1 19.7 %collective-permute-start.34 = (bf16[576,640]{1,0:T(8,128)(2,1)}, bf16[576,640]{1,0:T(8,128)(2,1)}, u32[]{:S(2)}, u32[]{:S(2)}) collective-permute-start(bf16[576,640]{1,0:T(8,128)(2,1)} %bitcast.126), channel_id=1, source_target_pairs={{0,8},{4,12},{8,0},{12,4},{16,24},{20,28},{24,16},{28,20},{1,9},{5... | collective-permute-start | bytes 2211848 | tf_op jit(solution)/shard_map/ppermute | solution.py:166
  693.7 21.3 %collective-permute-start.49 = (bf16[72,3456]{1,0:T(8,128)(2,1)S(1)}, bf16[72,3456]{1,0:T(8,128)(2,1)}, u32[]{:S(2)}, u32[]{:S(2)}) collective-permute-start(bf16[72,3456]{1,0:T(8,128)(2,1)S(1)} %pad_maximum_fusion.5), channel_id=1, source_target_pairs={{0,1},{1,0},{2,3},{3,2},{4,5},{5,4},{6,7},{7,6},{8,9},{9,8},{10,11... | collective-permute-start | bytes 1493000 | tf_op jit(solution)/shard_map/ppermute | solution.py:166
  703.8 13.2 %collective-permute-start.37 = (bf16[288,512]{1,0:T(8,128)(2,1)}, bf16[288,512]{1,0:T(8,128)(2,1)}, u32[]{:S(2)}, u32[]{:S(2)}) collective-permute-start(bf16[288,512]{1,0:T(8,128)(2,1)} %get-tuple-element.319), channel_id=1, source_target_pairs={{0,8},{4,12},{8,0},{12,4},{16,24},{20,28},{24,16},{28,20},{1,9},{5... | collective-permute-start | bytes 884744 | tf_op jit(solution)/shard_map/ppermute | solution.py:166
  711.1 9.6 %collective-permute-start.35 = (bf16[288,640]{1,0:T(8,128)(2,1)}, bf16[288,640]{1,0:T(8,128)(2,1)}, u32[]{:S(2)}, u32[]{:S(2)}) collective-permute-start(bf16[288,640]{1,0:T(8,128)(2,1)} %get-tuple-element.305), channel_id=1, source_target_pairs={{0,16},{4,20},{8,24},{12,28},{16,0},{20,4},{24,8},{28,12},{1,17},{... | collective-permute-start | bytes 1105928 | tf_op jit(solution)/shard_map/ppermute | solution.py:166
  722.0 12.4 %collective-permute-start.38 = (bf16[144,1152]{1,0:T(8,128)(2,1)S(1)}, bf16[144,1152]{1,0:T(8,128)(2,1)S(1)}, u32[]{:S(2)}, u32[]{:S(2)}) collective-permute-start(bf16[144,1152]{1,0:T(8,128)(2,1)S(1)} %pad_maximum_fusion.6), channel_id=1, source_target_pairs={{0,1},{1,0},{2,3},{3,2},{4,5},{5,4},{6,7},{7,6},{8,9},{9,8},{10,11... | collective-permute-start | bytes 995336 | tf_op jit(solution)/shard_map/ppermute | solution.py:166
  723.1 18.2 %collective-permute-start.50 = (bf16[36,3456]{1,0:T(8,128)(2,1)S(1)}, bf16[36,3456]{1,0:T(8,128)(2,1)S(1)}, u32[]{:S(2)}, u32[]{:S(2)}) collective-permute-start(bf16[36,3456]{1,0:T(8,128)(2,1)S(1)} %fusion.68), channel_id=1, source_target_pairs={{0,2},{1,3},{2,0},{3,1},{4,6},{5,7},{6,4},{7,5},{8,10},{9,11},{10,... | collective-permute-start | bytes 746504 | tf_op jit(solution)/shard_map/ppermute | solution.py:166
  734.5 9.2 %collective-permute-start.39 = (bf16[72,1152]{1,0:T(8,128)(2,1)S(1)}, bf16[72,1152]{1,0:T(8,128)(2,1)S(1)}, u32[]{:S(2)}, u32[]{:S(2)}) collective-permute-start(bf16[72,1152]{1,0:T(8,128)(2,1)S(1)} %fusion.75), channel_id=1, source_target_pairs={{0,2},{1,3},{2,0},{3,1},{4,6},{5,7},{6,4},{7,5},{8,10},{9,11},{10,... | collective-permute-start | bytes 497672 | tf_op jit(solution)/shard_map/ppermute | solution.py:166
  (105 other events, 1401.6 us)

commit v3 on v2

--- a/solution.py
+++ b/solution.py
@@ -12,11 +12,16 @@
 HEAD_DIM = 72
 LAT_CH = 4
 PATCH = 2
+LANES = 128
+NT = (((1,), (1,)), ((), ()))
+TN = (((0,), (0,)), ((), ()))
+NN = (((1,), (0,)), ((), ()))
 
 EPSILON = 1e-05
 HIGHEST = lax.Precision.HIGHEST
 F32 = jnp.float32
 BF16 = jnp.bfloat16
+COVER = pl.CostEstimate(flops=1 << 20, transcendentals=0, bytes_accessed=1 << 20)
 
 
 def bits_of(count):
@@ -50,12 +55,34 @@
     return jnp.concatenate([jnp.cos(angles), jnp.sin(angles)], axis=1)
 
 
+ERFC = (
+    -1.26551223,
+    1.00002368,
+    0.37409196,
+    0.09678418,
+    -0.18628806,
+    0.27886807,
+    -1.13520398,
+    1.48851587,
+    -0.82215223,
+    0.17087277,
+)
+
+
+def gelu_and_slope(values):
+    u = jnp.abs(values) * math.sqrt(0.5)
+    t = 1.0 / (1.0 + 0.5 * u)
+    poly = jnp.full_like(t, ERFC[-1])
+    for coefficient in reversed(ERFC[:-1]):
+        poly = poly * t + coefficient
+    bell = jnp.exp(-u * u)
+    tail = 0.5 * t * bell * jnp.exp(poly)
+    below = jnp.where(values < 0.0, tail, 1.0 - tail)
+    return values * below, below + values * bell * (1.0 / math.sqrt(2.0 * math.pi))
+
+
 def project(rows, weight):
     return jnp.einsum("rd,de->re", rows, weight, preferred_element_type=F32)
-
-
-def weight_grad(rows, grads):
-    return jnp.einsum("rd,re->de", rows, grads, preferred_element_type=F32)
 
 
 def back_project(grads, weight):
@@ -84,12 +111,17 @@
                     pairs.append((gx * self.gy + z, (2 * pair + to_c) * self.gy + to_z))
             self.perms.append(pairs)
 
+    def cut(self, blocks):
+        return [
+            lax.dynamic_index_in_dim(blocks, self.parity ^ turn, 0, keepdims=False)
+            for turn in range(2)
+        ]
+
+    def send(self, sends):
+        return [lax.ppermute(sends[t], ("gx", "gy"), self.perms[t]) for t in range(2)]
+
     def there(self, blocks):
-        out = []
-        for turn in range(2):
-            send = lax.dynamic_index_in_dim(blocks, self.parity ^ turn, 0, keepdims=False)
-            out.append(lax.ppermute(send, ("gx", "gy"), self.perms[turn]))
-        return out
+        return self.send(self.cut(blocks))
 
     def back(self, first, second):
         got = [
@@ -116,73 +148,213 @@
         return 2 * d + ((self.item % 2) ^ turn)
 
 
-class Halving:
-    def __init__(self, part, columns=None, wire=BF16):
-        self.sizes = {axis: lax.axis_size(axis) for axis in ("gx", "gy")}
-        gx, gy = bits_of(self.sizes["gx"]), bits_of(self.sizes["gy"])
-        dims = [("gx", b) for b in reversed(range(gx))] + [("gy", b) for b in reversed(range(gy))]
-        self.rows = part.shape[0] >> len(dims)
-        self.pieces = [([part], dims)]
-        rising = [("gx", b) for b in range(1, gx)]
-        self.orders = [[("gx", 0)]] + [list(pair) for pair in zip(rising, reversed(rising))]
-        self.orders += [[("gy", b)] for b in range(gy)]
-        self.columns, self.wire = columns, wire
-        if columns is None:
-            self.orders = [order[:1] for order in self.orders]
-
-    def cut(self):
-        steps = self.orders.pop(0)
-        if len(steps) > len(self.pieces):
-            (parts, dims), c = self.pieces[0], self.columns
-            self.pieces = [([p[:, :c] for p in parts], dims), ([p[:, c:] for p in parts], dims)]
-        self.kept, sends = [], []
-        together = len(steps) < len(self.pieces)
-        for i, (parts, dims) in enumerate(self.pieces):
-            axis, bit = steps[0 if together else i]
-            place = dims.index((axis, bit))
-            before, after = 1 << place, 1 << (len(dims) - place - 1)
-            mine = (lax.axis_index(axis) >> bit) & 1
-
-            def half(which):
-                total = 0.0
-                for p in parts:
-                    p = p.reshape((before, 2, after * self.rows) + p.shape[1:])
-                    p = lax.dynamic_index_in_dim(p, which, 1, keepdims=False)
-                    p = p.reshape((before * after * self.rows,) + p.shape[2:])
-                    total = p if len(parts) == 1 else total + p.astype(F32)
-                return total.astype(self.wire)
-
-            sends.append(half(1 - mine))
-            self.kept.append((half(mine), [d for d in dims if d != (axis, bit)]))
-        if together:
-            sends = [jnp.concatenate(sends, axis=1)]
-            self.kept = [(jnp.concatenate([k for k, _ in self.kept], axis=1), self.kept[0][1])]
-        self.steps = steps
+def back_kernel(grads, weight, *refs):
+    value = dot(grads[...], weight[...], NT)
+    if len(refs) == 2:
+        value = value * refs[0][...].astype(F32)
+    refs[-1][...] = value.astype(refs[-1].dtype)
+
+
+def back(grads, weight, dtype, *slope):
+    count, width = grads.shape
+    height = weight.shape[0]
+    tile = 1152 if width == 1152 and height % 1152 == 0 else 384
+    tile = tile if height % tile == 0 else height
+    part = pl.BlockSpec((count, tile), lambda j: (0, j))
+    return pl.pallas_call(
+        back_kernel,
+        out_shape=jax.ShapeDtypeStruct((count, height), dtype),
+        grid=(height // tile,),
+        in_specs=[
+            pl.BlockSpec((count, width), lambda j: (0, 0)),
+            pl.BlockSpec((tile, width), lambda j: (j, 0)),
+            *[part for _ in slope],
+        ],
+        out_specs=part,
+        compiler_params=pltpu.CompilerParams(vmem_limit_bytes=48 << 20),
+        cost_estimate=COVER,
+        name="back",
+    )(grads, weight, *slope)
+
+
+def weight_grad_kernel(pairs, block, other, rows, grads, full, send, sums):
+    full[...] = dot(rows[...], grads[...], TN).astype(full.dtype)
+    for pair in range(pairs):
+        start = pl.multiple_of((2 * pair + other[0]) * block, 16)
+        send[pair * block : (pair + 1) * block, :] = full[pl.ds(start, block), :]
+    sums[...] = jnp.sum(grads[...].astype(F32), axis=0, keepdims=True)
+
+
+def weight_grad(rows, grads):
+    count, height = rows.shape
+    width = grads.shape[1]
+    block = height >> bits_of(lax.axis_size("gx"))
+    tall = 1152 if height % 1152 == 0 and 1152 % (2 * block) == 0 else height
+    wide = 1152 if width % 1152 == 0 else width
+    other = (1 - lax.axis_index("gx") % 2).astype(jnp.int32).reshape(1)
+    return pl.pallas_call(
+        partial(weight_grad_kernel, tall // (2 * block), block),
+        out_shape=(
+            jax.ShapeDtypeStruct((height, width), BF16),
+            jax.ShapeDtypeStruct((height // 2, width), BF16),
+            jax.ShapeDtypeStruct((1, width), F32),
+        ),
+        grid_spec=pltpu.PrefetchScalarGridSpec(
+            num_scalar_prefetch=1,
+            grid=(height // tall, width // wide),
+            in_specs=[
+                pl.BlockSpec((count, tall), lambda i, j, ref: (0, i)),
+                pl.BlockSpec((count, wide), lambda i, j, ref: (0, j)),
+            ],
+            out_specs=[
+                pl.BlockSpec((tall, wide), lambda i, j, ref: (i, j)),
+                pl.BlockSpec((tall // 2, wide), lambda i, j, ref: (i, j)),
+                pl.BlockSpec((1, wide), lambda i, j, ref: (0, j)),
+            ],
+        ),
+        compiler_params=pltpu.CompilerParams(vmem_limit_bytes=48 << 20),
+        cost_estimate=COVER,
+        name="weight_grad",
+    )(other, rows, grads)
+
+
+def split_kernel(count, places, rows, index, *refs):
+    parts, outs, acc = refs[:count], refs[count : count + places], refs[-1]
+    value = parts[0][...].astype(F32)
+    for part in parts[1:]:
+        value = value + part[...].astype(F32)
+    acc[...] = value
+    z = index[index.shape[0] - 1]
+    for place in range(places):
+
+        @pl.when(z == place)
+        def _():
+            for step in range(places):
+                start = (place + step) % places * rows
+                outs[step][...] = acc[start : start + rows, :].astype(outs[step].dtype)
+
+
+def split(addends, index, places, wire):
+    block, width = addends[0][0].shape[-2:]
+    rows = block // places
+    tile = 1152 if width % 1152 == 0 else width
+
+    def spec(dims):
+        return pl.BlockSpec(
+            (None,) * len(dims) + (block, tile), lambda j, ref: (*[ref[d] for d in dims], 0, j)
+        )
+
+    return pl.pallas_call(
+        partial(split_kernel, len(addends), places, rows),
+        out_shape=[
+            jax.ShapeDtypeStruct((rows, width), wire if step else F32) for step in range(places)
+        ],
+        grid_spec=pltpu.PrefetchScalarGridSpec(
+            num_scalar_prefetch=1,
+            grid=(width // tile,),
+            in_specs=[spec(dims) for _, dims in addends],
+            out_specs=[pl.BlockSpec((rows, tile), lambda j, ref: (0, j))] * places,
+            scratch_shapes=[pltpu.VMEM((block, tile), F32)],
+        ),
+        compiler_params=pltpu.CompilerParams(vmem_limit_bytes=40 << 20),
+        name="split",
+    )(index, *[value for value, _ in addends])
+
+
+class Scatter:
+    def __init__(self, line, part, falling, wire=BF16, first=None):
+        self.gx, self.gy = lax.axis_size("gx"), lax.axis_size("gy")
+        bits = bits_of(self.gx)
+        rest = range(1, bits)
+        self.stages = [0] + list(reversed(rest) if falling else rest) + [None]
+        block = part.shape[0] >> bits
+        dims = list(reversed(range(bits)))
+        self.addends = [(part.reshape((2,) * bits + (block, part.shape[1])), dims)]
+        self.fixed, self.first = {}, first
+        self.line, self.wire = line, wire
+
+    def mine(self, bit):
+        return (lax.axis_index("gx") >> bit) & 1
+
+    def total(self, chosen):
+        out = None
+        for value, dims in self.addends:
+            tail = value.shape[len(dims) :]
+            starts = [chosen.get(d, 0) for d in dims] + [0] * len(tail)
+            shape = tuple(1 if d in chosen else 2 for d in dims) + tail
+            value = lax.dynamic_slice(value, [jnp.int32(i) for i in starts], shape)
+            value = value.reshape(tuple(2 for d in dims if d not in chosen) + tail)
+            out = value if out is None else out.astype(F32) + value.astype(F32)
+        return out
+
+    def cut(self, after):
+        bit = self.bit = self.stages.pop(0)
+        if bit == 0 and self.first is not None:
+            return [self.first]
+        newest, dims = self.addends[-1]
+        newest = lax.optimization_barrier((newest, *after, *self.line))[0]
+        self.addends[-1] = (newest, dims)
+        if bit is not None:
+            send = self.total({**self.fixed, bit: 1 - self.mine(bit)}).astype(self.wire)
+            return [send.reshape(-1, send.shape[-1])]
+        z = lax.axis_index("gy")
+        block, width = self.addends[0][0].shape[-2:]
+        rows = block // self.gy
+        if rows % 8:
+            bits = bits_of(self.gx)
+            index = jnp.stack([self.mine(d) for d in range(bits)] + [z]).astype(jnp.int32)
+            self.keep, *sends = split(self.addends, index, self.gy, self.wire)
+            return sends
+        shares = []
+        whole = self.addends
+        for step in range(self.gy):
+            place = lax.rem(z + step, self.gy)
+            self.addends = [
+                (value.reshape(value.shape[:-2] + (self.gy, rows, width)), dims) for value, dims in whole
+            ]
+            out = None
+            for value, dims in self.addends:
+                starts = [jnp.int32(self.fixed[d]) for d in dims] + [place, 0, 0]
+                value = lax.dynamic_slice(
+                    value, [jnp.int32(i) for i in starts], (1,) * (len(dims) + 1) + (rows, width)
+                ).reshape(rows, width)
+                out = value if out is None else out.astype(F32) + value.astype(F32)
+            shares.append(out.astype(self.wire) if step else out.astype(F32))
+        self.keep, *sends = shares
         return sends
 
     def send(self, sends):
-        self.pieces = []
-        for value, (kept, dims), (axis, bit) in zip(sends, self.kept, self.steps):
-            got = lax.ppermute(value, axis, [(i, i ^ (1 << bit)) for i in range(self.sizes[axis])])
-            self.pieces.append(([kept, got], dims))
-
-    def advance(self, *others):
-        sends = self.cut()
+        if self.bit is None:
+            self.got = [
+                lax.ppermute(value, "gy", [(i, (i + step) % self.gy) for i in range(self.gy)])
+                for step, value in enumerate(sends, 1)
+            ]
+            return
+        bit = self.bit
+        pairs = [(i, i ^ (1 << bit)) for i in range(self.gx)]
+        got = lax.ppermute(sends[0], "gx", pairs)
+        dims = [d for d in reversed(range(bits_of(self.gx))) if d not in self.fixed and d != bit]
+        tail = self.addends[0][0].shape[-2:]
+        self.addends.append((got.reshape((2,) * len(dims) + tail), dims))
+        self.fixed[bit] = self.mine(bit)
+
+    def advance(self, *others, after=()):
+        sends = self.cut(after)
+        count = len(sends)
         out = lax.optimization_barrier((*sends, *others))
-        self.send(out[: len(sends)])
-        return out[len(sends) :] if len(others) != 1 else out[-1]
+        self.send(out[:count])
+        self.line[:] = [out[count - 1]]
+        return out[count:] if len(others) != 1 else out[-1]
 
     def finish(self):
-        while self.orders:
-            self.send(self.cut())
-        (kept, got), _ = self.pieces[0]
-        return kept.astype(F32) + got.astype(F32)
-
-
-LANES = 128
-NT = (((1,), (1,)), ((), ()))
-TN = (((0,), (0,)), ((), ()))
-NN = (((1,), (0,)), ((), ()))
+        while self.stages:
+            self.advance()
+        out = self.keep
+        for got in lax.optimization_barrier((*self.got, *self.line))[: len(self.got)]:
+            out = out + got.astype(F32)
+        return out
+
+
 IN_VMEM = pl.BlockSpec(memory_space=pltpu.VMEM)
 
 
@@ -265,11 +437,7 @@
             pltpu.VMEM((HEADS, keys, LANES), BF16),
             pltpu.VMEM((HEADS, rows, LANES), F32),
         ],
-        cost_estimate=pl.CostEstimate(
-            flops=4 * rows * keys * 512 * HEADS,
-            transcendentals=rows * keys * HEADS,
-            bytes_accessed=2 * width * (rows * 4 + keys * 2),
-        ),
+        cost_estimate=COVER,
         compiler_params=pltpu.CompilerParams(vmem_limit_bytes=56 << 20),
         name="attend",
     )(qkv, *others, bias)
@@ -359,11 +527,7 @@
         in_specs=[IN_VMEM] * (holders + 4 + len(earlier)),
         out_specs=(IN_VMEM,) * len(out_shape),
         scratch_shapes=scratch,
-        cost_estimate=pl.CostEstimate(
-            flops=10 * rows * keys * 512 * heads,
-            transcendentals=rows * keys * heads,
-            bytes_accessed=2 * width * (rows * 8 + keys * 4),
-        ),
+        cost_estimate=COVER,
         compiler_params=pltpu.CompilerParams(vmem_limit_bytes=58 << 20),
         name="attend_back",
     )(qkv, *others, bias, mixed, lse, grad, *earlier)
@@ -408,6 +572,31 @@
     go = Regroup()
     devices = go.gx * go.gy
 
+    caption = jnp.broadcast_to(caption_len.astype(F32)[:, None, None], (2, 1, width))
+    message = go.there(jnp.concatenate([text_grad, caption], axis=1))
+
+    slots = lax.axis_index("gy") * text_dev + jnp.arange(text_dev, dtype=jnp.int32)
+    first_row = (slots == 0).astype(F32)
+    embed = time_embedding(time_steps, width)
+    text_in = (text_tokens.astype(F32) + first_row[None, :, None] * embed[:, None, :]).astype(BF16)
+
+    def rows_of(image, text):
+        return jnp.concatenate(
+            [
+                image.reshape(item_count, image_dev, width),
+                jnp.pad(text, ((0, 0), (0, text_pad - text_dev), (0, 0))),
+            ],
+            axis=1,
+        )
+
+    joined_here = jnp.concatenate(
+        [rows_of(image_tokens, text_in), rows_of(image_skip, text_skip)], axis=2
+    )
+    resid_here = (
+        project(joined_here.reshape(rows, 2 * width), w_skip) + b_skip
+    ).astype(BF16)
+    away = go.cut(resid_here.reshape(2, block, width))
+    *away, pred_grad = lax.optimization_barrier((*away, pred_grad))
     lat_shape = pred_grad.shape
     lat_rows, lat_cols = (lat_shape[2], lat_shape[3])
     grad_pad = jnp.pad(with_halo(pred_grad, "gy", 3, 1), ((0, 0), (0, 0), (1, 1), (0, 0)))
@@ -429,53 +618,20 @@
     grad_b_head = jnp.sum(grad_patches, axis=(0, 1))
     grad_b_conv = jnp.sum(pred_grad, axis=(0, 2, 3))
 
-    slots = lax.axis_index("gy") * text_dev + jnp.arange(text_dev, dtype=jnp.int32)
-    first_row = (slots == 0).astype(F32)
-    embed = time_embedding(time_steps, width)
-    text_in = (text_tokens.astype(F32) + first_row[None, :, None] * embed[:, None, :]).astype(BF16)
-
-    def rows_of(image, text):
-        return jnp.concatenate(
-            [
-                image.reshape(item_count, image_dev, width),
-                jnp.pad(text, ((0, 0), (0, text_pad - text_dev), (0, 0))),
-            ],
-            axis=1,
-        )
-
-    joined_here = jnp.concatenate(
-        [rows_of(image_tokens, text_in), rows_of(image_skip, text_skip)], axis=2
-    )
-    resid_here = (
-        project(joined_here.reshape(rows, 2 * width), w_skip) + b_skip
-    ).astype(BF16)
-    resid = jnp.concatenate(go.there(resid_here.reshape(2, block, width)), axis=0).astype(F32)
-    gate, joined_late, text_grad, grad_patches, caption = lax.optimization_barrier(
-        (resid, joined_here, text_grad, grad_patches, caption_len.astype(F32))
-    )
-    resid = gate
-    patch_rows = -(-grad_patches.shape[1] * grad_patches.shape[2] // width)
+    resid = jnp.concatenate(go.send(away), axis=0).astype(F32)
+    resid, joined_late, grad_patches = lax.optimization_barrier((resid, joined_here, grad_patches))
+    joined = go.there(joined_late)
+    patch_rows = -(-grad_patches.shape[1] * grad_patches.shape[2] // LANES)
     flat = grad_patches.reshape(2, -1)
-    flat = jnp.pad(flat, ((0, 0), (0, patch_rows * width - flat.shape[1])))
-    message = jnp.concatenate(
-        [
-            text_grad,
-            flat.reshape(2, patch_rows, width),
-            jnp.broadcast_to(caption[:, None, None], (2, 1, width)),
-        ],
-        axis=1,
-    )
-    message = go.there(message)
-    joined_late, *message = lax.optimization_barrier((joined_late, *message))
-    joined = jnp.concatenate(go.there(joined_late), axis=0)
-    text_grad_rows = [part[:text_dev] for part in message]
+    flat = jnp.pad(flat, ((0, 0), (0, patch_rows * LANES - flat.shape[1])))
     grad_patches = jnp.concatenate(
         [
-            part[text_dev : text_dev + patch_rows].reshape(-1)[: image_dev * 16].reshape(-1, 16)
-            for part in message
+            part.reshape(-1)[: image_dev * 16].reshape(-1, 16)
+            for part in go.there(flat.reshape(2, patch_rows, LANES))
         ],
         axis=0,
     )
+    text_grad_rows = [part[:text_dev] for part in message]
     caption = message[0][-1, 0].astype(jnp.int32)
 
     normed_attn, attn_norm_back = jax.vjp(layer_norm, resid, gain_attn, bias_attn)
@@ -497,8 +653,10 @@
     normed_mlp, mlp_norm_back = jax.vjp(layer_norm, resid_two, gain_mlp, bias_mlp)
     normed_two = normed_mlp.astype(BF16)
     pre_act = project(normed_two, w_up) + b_up
-    activated, gelu_back = jax.vjp(partial(jax.nn.gelu, approximate=False), pre_act)
-    hidden = activated.astype(BF16)
+    activated, slope = gelu_and_slope(pre_act)
+    hidden, slope = activated.astype(BF16), slope.astype(BF16)
+    hidden, slope, *joined = lax.optimization_barrier((hidden, slope, *joined))
+    joined = jnp.concatenate(joined, axis=0)
     resid_three = resid_two + project(hidden, w_down) + b_down
 
     def image_of(values):
@@ -541,53 +699,54 @@
         axis=0,
     )
     grad_b_down = jnp.sum(grad_three, axis=0)
+    line = []
+
+    def scatter(left, right, falling):
+        full, first, sums = weight_grad(left, right)
+        return Scatter(line, full, falling, BF16, first), sums[0]
+
     down_in = grad_three.astype(BF16)
-    sum_down = Halving(weight_grad(hidden, down_in).astype(BF16), 640)
+    sum_down, _ = scatter(hidden, down_in, False)
     down_in = sum_down.advance(down_in)
-    (grad_pre,) = gelu_back(back_project(down_in, w_down))
-    pre_low = grad_pre.astype(BF16)
-    grad_b_up = jnp.sum(pre_low.astype(F32), axis=0)
+    pre_low = back(down_in, w_down, BF16, slope)
     pre_low = sum_down.advance(pre_low)
-    sum_up = Halving(weight_grad(normed_two, pre_low).astype(BF16), 2304)
+    sum_up, grad_b_up = scatter(normed_two, pre_low, True)
     pre_low = sum_up.advance(pre_low)
-    grad_two, grad_gain_mlp, grad_bias_mlp = mlp_norm_back(back_project(pre_low, w_up))
+    grad_two, grad_gain_mlp, grad_bias_mlp = mlp_norm_back(back(pre_low, w_up, F32))
     grad_two = grad_two + grad_three
     grad_b_proj = jnp.sum(grad_two, axis=0)
     proj_in = grad_two.astype(BF16)
     proj_in = sum_up.advance(proj_in)
-    sum_proj = Halving(weight_grad(mixed, proj_in).astype(BF16), 640)
+    sum_proj, _ = scatter(mixed, proj_in, False)
     proj_in = sum_proj.advance(proj_in)
-    grad_mixed = back_project(proj_in, w_proj).astype(BF16)
-    grad_mixed = sum_down.advance(grad_mixed)
+    grad_mixed = back(proj_in, w_proj, BF16)
     parts = attend_back(qkv, others, bias, mixed, lse, grad_mixed, 0, HEADS // 2, ())
-    parts = sum_proj.advance(*parts)
-    parts = sum_up.advance(*parts)
+    parts = sum_proj.advance(*parts, after=parts[:1])
     parts = sum_down.advance(*parts)
     grads = attend_back(qkv, others, bias, mixed, lse, grad_mixed, HEADS // 2, HEADS // 2, parts)
-    grads = sum_down.advance(*grads)
-    grads = sum_proj.advance(*grads)
-    grads = sum_up.advance(*grads)
-    grad_kv = grads[1].astype(F32)
-    for step in range(1, go.holders):
-        grad_kv = grad_kv + go.share(grads[1 + step], go.holders - step).astype(F32)
-    grad_qkv = jnp.concatenate([grads[0], grad_kv.astype(BF16)], axis=1)
-    sum_qkv = Halving(weight_grad(normed, grad_qkv).astype(BF16), 1792)
-    grad_qkv = sum_qkv.advance(grad_qkv)
-    grad_one, grad_gain_attn, grad_bias_attn = attn_norm_back(back_project(grad_qkv, w_qkv))
+    shared = [go.share(grads[1 + step], go.holders - step) for step in range(1, go.holders)]
+    sum_q, _ = scatter(normed, grads[0], True)
+    first = sum_q.advance(grads[1])
+    first = sum_up.advance(first, after=grads[:1])
+    grad_kv = first.astype(F32)
+    for value in shared:
+        grad_kv = grad_kv + value.astype(F32)
+    grad_kv = grad_kv.astype(BF16)
+    sum_kv, _ = scatter(normed, grad_kv, False)
+    grad_kv = sum_kv.advance(grad_kv)
+    grad_kv = sum_proj.advance(grad_kv)
+    grad_kv = sum_down.advance(grad_kv)
+    grad_kv = sum_q.advance(grad_kv)
+    grad_qkv = jnp.concatenate([grads[0], grad_kv], axis=1)
+    grad_one = back(grad_qkv, w_qkv, F32)
+    grad_one = sum_kv.advance(grad_one, after=(grad_one,))
+    grad_one, grad_gain_attn, grad_bias_attn = attn_norm_back(grad_one)
     grad_one = grad_one + grad_two
     grad_b_skip = jnp.sum(grad_one, axis=0)
     skip_in = grad_one.astype(BF16)
-    skip_in = sum_qkv.advance(skip_in)
-    sum_skip = Halving(weight_grad(joined, skip_in).astype(BF16), 640)
-    skip_in = sum_skip.advance(skip_in)
     skip_here = go.back(skip_in[:block], skip_in[block:])
-    grad_joined = back_project(skip_here.reshape(rows, width), w_skip).reshape(2, block, 2 * width)
-    image_shape = image_tokens.shape
-    grad_image = grad_joined[:, :image_dev, :width].reshape(image_shape)
-    grad_image_skip = grad_joined[:, :image_dev, width:].reshape(image_shape)
-    grad_text = grad_joined[:, image_dev : image_dev + text_dev, :width]
-    grad_text_skip = grad_joined[:, image_dev : image_dev + text_dev, width:]
-
+    sum_skip, _ = scatter(joined, skip_in, True)
+    sum_skip.advance()
     vectors = (
         grad_b_skip,
         grad_gain_attn,
@@ -605,8 +764,34 @@
     packed = [v.reshape(devices, -1) for v in vectors]
     packed.append(jnp.broadcast_to(whole[None], (devices, whole.shape[0])))
     packed = jnp.concatenate(packed, axis=1)
-    packed = jnp.pad(packed, ((0, 0), (0, -packed.shape[1] % 128)))
-    packed = Halving(packed, None, F32).finish()[0]
+    tile = 8 * LANES
+    packed = jnp.pad(packed, ((0, 0), (0, -packed.shape[1] % tile)))
+    packed = packed.reshape(-1, LANES)
+    sum_small = Scatter(line, packed, True, F32)
+    sum_small.advance()
+    sum_up.advance()
+    sum_q.advance()
+    sum_skip.advance()
+    sum_small.advance()
+    sum_kv.advance()
+    skip_here = lax.optimization_barrier((skip_here, *line))[0]
+    grad_joined = back_project(skip_here.reshape(rows, width), w_skip).reshape(2, block, 2 * width)
+    image_shape = image_tokens.shape
+    grad_image = grad_joined[:, :image_dev, :width].reshape(image_shape)
+    grad_image_skip = grad_joined[:, :image_dev, width:].reshape(image_shape)
+    grad_text = grad_joined[:, image_dev : image_dev + text_dev, :width]
+    grad_text_skip = grad_joined[:, image_dev : image_dev + text_dev, width:]
+
+    sum_proj.advance()
+    sum_q.advance()
+    sum_skip.advance()
+    sum_small.advance()
+    sum_kv.advance()
+    sum_skip.advance()
+    sum_small.advance()
+    down_done, up_done, proj_done = sum_down.finish(), sum_up.finish(), sum_proj.finish()
+    q_done, kv_done, skip_done = sum_q.finish(), sum_kv.finish(), sum_skip.finish()
+    packed = sum_small.finish().reshape(-1)
     small = []
     start = 0
     for v in vectors:
@@ -624,18 +809,18 @@
         grad_text,
         grad_image_skip,
         grad_text_skip,
-        sum_skip.finish(),
+        skip_done,
         small[0],
         small[1],
         small[2],
-        sum_qkv.finish(),
-        sum_proj.finish(),
+        jnp.concatenate([q_done, kv_done], axis=1),
+        proj_done,
         small[3],
         small[4],
         small[5],
-        sum_up.finish(),
+        up_done,
         small[6],
-        sum_down.finish(),
+        down_done,
         small[7],
         small[8],
         small[9],

time: 757 us -> 637 us (0.84)
  local copies, waits for them, and re-layouts: 165 us -> 58.7 us
  matrix products: 177 us -> 73.3 us
  Pallas kernels: 108 us -> 208 us
  starting transfers between devices: 84.4 us -> 140 us
  other arithmetic: 106 us -> 70.9 us
  waiting for transfers between devices: 102 us -> 73 us
    pallas_call x0 -> x14, Pallas kernels: none -> 99.3 us  [the longest x6 54.4 us: weight_grad(): pl.pallas_call(partial(weight_grad_kernel, tall // (2 * block), block), o...]
    ppermute x46 -> x50, starting transfers between devices: 66.2 us -> 114 us  [the longest x21 56.2 us: send(): lax.ppermute(value, 'gy', [(i, (i + step) % self.gy) for i in range(self....]
    dot_general x5 -> x1, matrix products: 51.1 us -> 6.13 us  [back_project(): return jnp.einsum('re,de->rd', grads, weight, preferred_element_type=F32)]
    dot_general x5 -> x0, matrix products: 40.4 us -> none  [weight_grad(): return jnp.einsum('rd,re->de', rows, grads, preferred_element_type=F32)]
    slice x28 -> x0, local copies, waits for them, and re-layouts: 32.6 us -> none  [the longest x10 17.9 us: cut(): p[:, c:]]
    convert_element_type x43 -> x19, other arithmetic: 64.9 us -> 35.6 us  [the longest x12 24 us: cut(): send = self.total({**self.fixed, bit: 1 - self.mine(bit)}).astype(self.wire)]
    reshape x16 -> x1, local copies, waits for them, and re-layouts: 24.1 us -> 0.13 us  [per_device(): flat.reshape(2, patch_rows, LANES)]
    ppermute x46 -> x50, waiting for transfers between devices: 88 us -> 69.8 us  [the longest x21 38.3 us: send(): lax.ppermute(value, 'gy', [(i, (i + step) % self.gy) for i in range(self....]
  transfers between devices with their start and end apart: 58 -> 62, of which waited for: 19 -> 13; matrix products, arithmetic and copies ran while one was open for 39% -> 23% of each run, Pallas kernels for 9% -> 29%
where the time goes in v3:
time: 637 us; the launch traced here: 627 us
  Pallas kernels  208 us (33%)
  starting transfers between devices  140 us (22%)
  matrix products  73.3 us (12%)
  waiting for transfers between devices  73 us (11%)
  other arithmetic  70.9 us (11%)
  local copies, waits for them, and re-layouts  58.7 us (9%)
    pallas_call x2, Pallas kernels, attend_back(): pl.pallas_call(partial(attend_back_kernel, holders, width, keys // 2, fir...  70.2 us
    ppermute x21, starting transfers between devices, send(): lax.ppermute(value, 'gy', [(i, (i + step) % self.gy) for i in range(self....  56.2 us
    pallas_call x6, Pallas kernels, weight_grad(): pl.pallas_call(partial(weight_grad_kernel, tall // (2 * block), block), o...  54.4 us
    dot_general x6, matrix products, project(): return jnp.einsum('rd,de->re', rows, weight, preferred_element_type=F32)  51.6 us
    ppermute x21, waiting for transfers between devices, send(): lax.ppermute(value, 'gy', [(i, (i + step) % self.gy) for i in range(self....  38.3 us
    pallas_call x1, Pallas kernels, attend(): pl.pallas_call(partial(attend_kernel, holders, width, 288), out_shape=(ja...  38.2 us
    pallas_call x4, Pallas kernels, back(): pl.pallas_call(back_kernel, out_shape=jax.ShapeDtypeStruct((count, height...  37.1 us
    ppermute x21, starting transfers between devices, send(): got = lax.ppermute(sends[0], 'gx', pairs)  30.8 us
  transfers between devices with their start and end apart: 62, of which 13 were waited for; matrix products, arithmetic and copies ran while one was open for 23% of the time, Pallas kernels for 29%

profile of v3, /device:TPU:0, one launch (start us, length us, event | category | flops | bytes accessed | tf_op | source)
XLA Modules:
  0.0 627.1 jit_solution(15834872406925426867)
XLA Ops:
  5.4 7.1 %fusion.13 = bf16[576,1152]{1,0:T(8,128)(2,1)S(1)} fusion(bf16[576,2304]{1,0:T(8,128)(2,1)S(1)} %bitcast.546, bf16[2304,1152]{1,0:T(8,128)(2,1)} %param.35, f32[1152]{0:T(1024)S(1)} %copy-done.79), kind=kOutput, calls=%fused_computation.31 | convolution fusion | flops 3058974720 | bytes 9294336 | tf_op jit(solution)/shard_map/rd,de->re/dot_general | solution.py:85
  13.4 5.0 collective-permute-start.2
  21.2 2.6 collective-permute-start.1
  29.9 9.2 %collective-permute-done.1 = bf16[288,1152]{1,0:T(8,128)(2,1)} collective-permute-done((bf16[288,1152]{1,0:T(8,128)(2,1)S(1)}, bf16[288,1152]{1,0:T(8,128)(2,1)}, u32[]{:S(2)}, u32[]{:S(2)}) %collective-permute-start.1) | collective-permute-done | bytes 663584 | tf_op jit(solution)/shard_map/ppermute | solution.py:121
  44.5 9.0 %convolution_convert_fusion.refs_0_ = bf16[576,3456]{1,0:T(8,128)(2,1)S(1)} fusion(bf16[576,1152]{1,0:T(8,128)(2,1)S(1)} %add_convert_fusion.3.rows, bf16[1152,3456]{1,0:T(8,128)(2,1)} %weight.7), kind=kOutput, calls=%fused_computation.5 | convolution fusion | flops 4588462080 | bytes 13271040 | tf_op jit(solution)/shard_map/rd,de->re/dot_general | solution.py:85
  55.2 8.9 %collective-permute-start.4 = (bf16[576,2304]{1,0:T(8,128)(2,1)}, bf16[576,2304]{1,0:T(8,128)(2,1)}, u32[]{:S(2)}, u32[]{:S(2)}) collective-permute-start(bf16[576,2304]{1,0:T(8,128)(2,1)} %slice.279), channel_id=1, source_target_pairs={{0,4},{1,5},{2,6},{3,7},{4,0},{5,1},{6,2},{7,3},{8,12},{9,13},{10,... | collective-permute-start | bytes 7962632 | tf_op jit(solution)/shard_map/ppermute | solution.py:144
  65.0 7.8 %collective-permute-start.16 = (f32[21,1152]{1,0:T(8,128)S(1)}, f32[21,1152]{1,0:T(8,128)S(1)}, u32[]{:S(2)}, u32[]{:S(2)}) collective-permute-start(f32[21,1152]{1,0:T(8,128)S(1)} %get-tuple-element.433), channel_id=1, source_target_pairs={{0,1},{1,0},{2,5},{3,4},{4,3},{5,2},{6,7},{7,6},{8,9},{9,8},{10,13... | collective-permute-start | bytes 290312 | tf_op jit(solution)/shard_map/ppermute | solution.py:121
  78.6 3.5 dynamic-slice_bitcast_fusion
  82.1 12.1 %collective-permute-start.6 = (bf16[288,2304]{1,0:T(8,128)(2,1)}, bf16[288,2304]{1,0:T(8,128)(2,1)}, u32[]{:S(2)}, u32[]{:S(2)}) collective-permute-start(bf16[288,2304]{1,0:T(8,128)(2,1)} %get-tuple-element.417), channel_id=1, source_target_pairs={{0,0},{1,1},{2,4},{3,5},{4,2},{5,3},{6,6},{7,7},{8,8},{9,9},{10,12... | collective-permute-start | bytes 3981320 | tf_op jit(solution)/shard_map/ppermute | solution.py:121
  95.6 38.2 %attend.1 = (bf16[576,1152]{1,0:T(8,128)(2,1)}, f32[576,128]{1,0:T(8,128)}) custom-call(bf16[576,3456]{1,0:T(8,128)(2,1)} %copy-done.22, bf16[576,2304]{1,0:T(8,128)(2,1)} %collective-permute-done.4.refs_1_, f32[1152,128]{1,0:T(8,128)} %broadcast_in_dim.37.refs_2_), custom_call_target="tpu_custom_call" | custom-call | flops 1048576 | bytes 1048576 | tf_op jit(solution)/shard_map/attend/pallas_call | solution.py:426
  133.8 4.4 fusion.193
  139.5 22.5 %add_convert_fusion = (bf16[576,4608]{1,0:T(8,128)(2,1)}, bf16[576,4608]{1,0:T(8,128)(2,1)S(1)}) fusion(f32[4608]{0:T(1024)S(1)} %copy-done.78, bf16[576,1152]{1,0:T(8,128)(2,1)S(1)} %add_convert_fusion.2.rows, bf16[1152,4608]{1,0:T(8,128)(2,1)} %weight.5), kind=kOutput, calls=%fused_computation.3 | convolution fusion | flops 6216155136 | bytes 22579200 | tf_op jit(solution)/shard_map/rd,de->re/dot_general | solution.py:85
  162.2 8.1 %fusion.194 = (bf16[576,1152]{1,0:T(8,128)(2,1)}, f32[576,1152]{1,0:T(8,128)S(1)}) fusion(f32[1152]{0:T(1024)S(1)} %copy-done.81, f32[576,1152]{1,0:T(8,128)S(1)} %get-tuple-element.467, bf16[576,4608]{1,0:T(8,128)(2,1)S(1)} %get-tuple-element.171.rows, bf16[4608,1152]{1,0:T(8,128)(2,1)S(1)} %bitcast.545), kind=kOutput, calls=%fused_computation.387 | convolution fusion | flops 6117285888 | bytes 22565376 | tf_op jit(solution)/shard_map/rd,de->re/dot_general | solution.py:85
  178.0 14.1 %weight_grad.6 = (bf16[4608,1152]{1,0:T(8,128)(2,1)}, bf16[2304,1152]{1,0:T(8,128)(2,1)}, f32[1,1152]{1,0:T(1,128)}) custom-call(s32[1]{0:T(128)} %bitcast.54.other, bf16[576,4608]{1,0:T(8,128)(2,1)} %copy-done.35, bf16[576,1152]{1,0:T(8,128)(2,1)S(1)} %fusion.23.grads), custom_call_target="tpu_custom_call" | custom-call | flops 1048576 | bytes 1048576 | tf_op jit(solution)/shard_map/weight_grad/pallas_call | solution.py:195
  193.6 12.6 %back.4.grads = bf16[576,4608]{1,0:T(8,128)(2,1)} custom-call(bf16[576,1152]{1,0:T(8,128)(2,1)S(1)} %fusion.23.grads, bf16[4608,1152]{1,0:T(8,128)(2,1)} %weight.4, bf16[576,4608]{1,0:T(8,128)(2,1)} %get-tuple-element.178.refs_0_), custom_call_target="tpu_custom_call" | custom-call | flops 1048576 | bytes 1048576 | tf_op jit(solution)/shard_map/back/pallas_call | solution.py:164
  212.7 13.9 %weight_grad.7 = (bf16[1152,4608]{1,0:T(8,128)(2,1)}, bf16[576,4608]{1,0:T(8,128)(2,1)}, f32[1,4608]{1,0:T(1,128)S(1)}) custom-call(s32[1]{0:T(128)} %bitcast.54.other, bf16[576,1152]{1,0:T(8,128)(2,1)S(1)} %copy-done.11, bf16[576,4608]{1,0:T(8,128)(2,1)} %back.4.grads), custom_call_target="tpu_custom_call" | custom-call | flops 1048576 | bytes 1048576 | tf_op jit(solution)/shard_map/weight_grad/pallas_call | solution.py:195
  237.2 3.0 pad_maximum_fusion.2.rows
  247.0 12.4 %back.5 = f32[576,1152]{1,0:T(8,128)S(1)} custom-call(bf16[576,4608]{1,0:T(8,128)(2,1)} %back.4.grads, bf16[1152,4608]{1,0:T(8,128)(2,1)} %weight.5), custom_call_target="tpu_custom_call" | custom-call | flops 1048576 | bytes 1048576 | tf_op jit(solution)/shard_map/back/pallas_call | solution.py:164
  271.1 4.5 weight_grad.8
  275.5 4.5 collective-permute-start.21
  280.0 3.1 collective-permute-start.10
  285.5 3.2 collective-permute-done.11
  300.9 31.3 %attend_back.2 = (bf16[8,576,128]{2,1,0:T(8,128)(2,1)}, bf16[2,8,1152,128]{3,2,1,0:T(8,128)(2,1)}) custom-call(bf16[576,3456]{1,0:T(8,128)(2,1)} %copy-done.22, bf16[576,2304]{1,0:T(8,128)(2,1)} %collective-permute-done.4.refs_1_, f32[1152,128]{1,0:T(8,128)} %broadcast_in_dim.37.refs_2_, bf16[576,1152]{1,0:T(8,128)(2,1)} %get-tuple-element.169.rows.refs_3_, ...), custom_call_target="tpu_custom_call" | custom-call | flops 1048576 | bytes 1048576 | tf_op jit(solution)/shard_map/attend_back/pallas_call | solution.py:524
  334.6 3.7 fusion.20
  338.3 38.9 %attend_back.3 = (bf16[576,1152]{1,0:T(8,128)(2,1)}, bf16[576,2304]{1,0:T(8,128)(2,1)}, bf16[576,2304]{1,0:T(8,128)(2,1)}) custom-call(bf16[576,3456]{1,0:T(8,128)(2,1)} %copy-done.22, bf16[576,2304]{1,0:T(8,128)(2,1)} %collective-permute-done.4.refs_1_, f32[1152,128]{1,0:T(8,128)} %broadcast_in_dim.37.refs_2_, ...), custom_call_target="tpu_custom_call" | custom-call | flops 1048576 | bytes 1048576 | tf_op jit(solution)/shard_map/attend_back/pallas_call | solution.py:524
  382.2 4.4 weight_grad.9
  386.6 4.4 fusion.19
  393.2 8.8 %weight_grad.10 = (bf16[1152,2304]{1,0:T(8,128)(2,1)}, bf16[576,2304]{1,0:T(8,128)(2,1)}, f32[1,2304]{1,0:T(1,128)}) custom-call(s32[1]{0:T(128)} %bitcast.54.other, bf16[576,1152]{1,0:T(8,128)(2,1)S(1)} %add_convert_fusion.3.rows, bf16[576,2304]{1,0:T(8,128)(2,1)} %add_convert_fusion.1.grads), custom_call_target="tpu_custom_call" | custom-call | flops 1048576 | bytes 1048576 | tf_op jit(solution)/shard_map/weight_grad/pallas_call | solution.py:195
  409.1 4.1 collective-permute-done.25
  414.6 3.6 fusion.42
  422.7 9.9 %back.7 = f32[576,1152]{1,0:T(8,128)S(1)} custom-call(bf16[576,3456]{1,0:T(8,128)(2,1)} %pad_maximum_fusion.grads, bf16[1152,3456]{1,0:T(8,128)(2,1)} %weight.7), custom_call_target="tpu_custom_call" | custom-call | flops 1048576 | bytes 1048576 | tf_op jit(solution)/shard_map/back/pallas_call | solution.py:164
  440.5 8.8 %weight_grad.11 = (bf16[2304,1152]{1,0:T(8,128)(2,1)}, bf16[1152,1152]{1,0:T(8,128)(2,1)}, f32[1,1152]{1,0:T(1,128)}) custom-call(s32[1]{0:T(128)} %bitcast.54.other, bf16[576,2304]{1,0:T(8,128)(2,1)} %pad_maximum_fusion.2.rows, bf16[576,1152]{1,0:T(8,128)(2,1)S(1)} %get-tuple-element.409.grads), custom_call_target="tpu_custom_call" | custom-call | flops 1048576 | bytes 1048576 | tf_op jit(solution)/shard_map/weight_grad/pallas_call | solution.py:195
  455.6 3.9 split.4
  459.5 8.8 %collective-permute-done.32 = bf16[288,1152]{1,0:T(8,128)(2,1)S(1)} collective-permute-done((bf16[288,1152]{1,0:T(8,128)(2,1)}, bf16[288,1152]{1,0:T(8,128)(2,1)S(1)}, u32[]{:S(2)}, u32[]{:S(2)}) %collective-permute-start.32) | collective-permute-done | bytes 663584 | tf_op jit(solution)/shard_map/ppermute | solution.py:335
  475.8 8.6 %collective-permute-start.30 = (f32[256,128]{1,0:T(8,128)S(1)}, f32[256,128]{1,0:T(8,128)S(1)}, u32[]{:S(2)}, u32[]{:S(2)}) collective-permute-start(f32[256,128]{1,0:T(8,128)S(1)} %bitcast.568), channel_id=1, source_target_pairs={{0,4},{4,0},{8,12},{12,8},{16,20},{20,16},{24,28},{28,24},{1,5},{5... | collective-permute-start | bytes 393224 | tf_op jit(solution)/shard_map/ppermute | solution.py:335
  490.1 7.9 %collective-permute-done.29 = bf16[288,2304]{1,0:T(8,128)(2,1)S(1)} collective-permute-done((bf16[288,2304]{1,0:T(8,128)(2,1)S(1)}, bf16[288,2304]{1,0:T(8,128)(2,1)S(1)}, u32[]{:S(2)}, u32[]{:S(2)}) %collective-permute-start.29) | collective-permute-done | bytes 1327136 | tf_op jit(solution)/shard_map/ppermute | solution.py:335
  498.9 21.0 %collective-permute-start.60 = (bf16[144,1152]{1,0:T(8,128)(2,1)}, bf16[144,1152]{1,0:T(8,128)(2,1)}, u32[]{:S(2)}, u32[]{:S(2)}) collective-permute-start(bf16[144,1152]{1,0:T(8,128)(2,1)} %get-tuple-element.301), channel_id=1, source_target_pairs={{0,2},{1,3},{2,0},{3,1},{4,6},{5,7},{6,4},{7,5},{8,10},{9,11},{10,... | collective-permute-start | bytes 995336 | tf_op jit(solution)/shard_map/ppermute | solution.py:329
  524.1 6.1 fusion.7
  539.4 3.6 collective-permute-start.56
  544.7 6.7 %collective-permute-start.53 = (bf16[36,1152]{1,0:T(8,128)(2,1)S(1)}, bf16[36,1152]{1,0:T(8,128)(2,1)S(1)}, u32[]{:S(2)}, u32[]{:S(2)}) collective-permute-start(bf16[36,1152]{1,0:T(8,128)(2,1)S(1)} %get-tuple-element.289), channel_id=1, source_target_pairs={{0,1},{1,2},{2,3},{3,0},{4,5},{5,6},{6,7},{7,4},{8,9},{9,10},{10,1... | collective-permute-start | bytes 248840 | tf_op jit(solution)/shard_map/ppermute | solution.py:329
  555.0 6.5 %collective-permute-done.56 = bf16[36,4608]{1,0:T(8,128)(2,1)S(1)} collective-permute-done((bf16[36,4608]{1,0:T(8,128)(2,1)S(1)}, bf16[36,4608]{1,0:T(8,128)(2,1)S(1)}, u32[]{:S(2)}, u32[]{:S(2)}) %collective-permute-start.56) | collective-permute-done | bytes 331808 | tf_op jit(solution)/shard_map/ppermute | solution.py:329
  561.5 18.3 %collective-permute-done.57 = bf16[36,4608]{1,0:T(8,128)(2,1)S(1)} collective-permute-done((bf16[36,4608]{1,0:T(8,128)(2,1)S(1)}, bf16[36,4608]{1,0:T(8,128)(2,1)S(1)}, u32[]{:S(2)}, u32[]{:S(2)}) %collective-permute-start.57) | collective-permute-done | bytes 331808 | tf_op jit(solution)/shard_map/ppermute | solution.py:329
  581.9 2.9 collective-permute-start.51
  591.0 6.5 %collective-permute-start.48 = (bf16[36,1152]{1,0:T(8,128)(2,1)S(1)}, bf16[36,1152]{1,0:T(8,128)(2,1)S(1)}, u32[]{:S(2)}, u32[]{:S(2)}) collective-permute-start(bf16[36,1152]{1,0:T(8,128)(2,1)S(1)} %get-tuple-element.278), channel_id=1, source_target_pairs={{0,2},{1,3},{2,0},{3,1},{4,6},{5,7},{6,4},{7,5},{8,10},{9,11},{10,... | collective-permute-start | bytes 248840 | tf_op jit(solution)/shard_map/ppermute | solution.py:329
  598.2 5.4 collective-permute-done.51
  604.6 2.9 collective-permute-done.48
  608.7 3.2 collective-permute-start.40
  611.9 2.6 fusion.40
  (481 shorter events, 180.7 us)
Async XLA Ops:
  21.2 17.9 %collective-permute-start.1 = (bf16[288,1152]{1,0:T(8,128)(2,1)S(1)}, bf16[288,1152]{1,0:T(8,128)(2,1)}, u32[]{:S(2)}, u32[]{:S(2)}) collective-permute-start(bf16[288,1152]{1,0:T(8,128)(2,1)S(1)} %get-tuple-element.166), channel_id=1, source_target_pairs={{0,1},{1,0},{2,5},{3,4},{4,3},{5,2},{6,7},{7,6},{8,9},{9,8},{10,13... | collective-permute-start | bytes 1990664 | tf_op jit(solution)/shard_map/ppermute | solution.py:121
  55.2 39.3 %collective-permute-start.4 = (bf16[576,2304]{1,0:T(8,128)(2,1)}, bf16[576,2304]{1,0:T(8,128)(2,1)}, u32[]{:S(2)}, u32[]{:S(2)}) collective-permute-start(bf16[576,2304]{1,0:T(8,128)(2,1)} %slice.279), channel_id=1, source_target_pairs={{0,4},{1,5},{2,6},{3,7},{4,0},{5,1},{6,2},{7,3},{8,12},{9,13},{10,... | collective-permute-start | bytes 7962632 | tf_op jit(solution)/shard_map/ppermute | solution.py:144
  75.8 18.5 %collective-permute-start.14 = (f32[32,128]{1,0:T(8,128)S(1)}, f32[32,128]{1,0:T(8,128)S(1)}, u32[]{:S(2)}, u32[]{:S(2)}) collective-permute-start(f32[32,128]{1,0:T(8,128)S(1)} %get-tuple-element.449), channel_id=1, source_target_pairs={{0,0},{1,1},{2,4},{3,5},{4,2},{5,3},{6,6},{7,7},{8,8},{9,9},{10,12... | collective-permute-start | bytes 49160 | tf_op jit(solution)/shard_map/ppermute | solution.py:121
  76.5 17.7 %collective-permute-start.15 = (f32[32,128]{1,0:T(8,128)S(1)}, f32[32,128]{1,0:T(8,128)S(1)}, u32[]{:S(2)}, u32[]{:S(2)}) collective-permute-start(f32[32,128]{1,0:T(8,128)S(1)} %get-tuple-element.450), channel_id=1, source_target_pairs={{0,1},{1,0},{2,5},{3,4},{4,3},{5,2},{6,7},{7,6},{8,9},{9,8},{10,13... | collective-permute-start | bytes 49160 | tf_op jit(solution)/shard_map/ppermute | solution.py:121
  82.0 80.1 %collective-permute-start.7 = (bf16[288,2304]{1,0:T(8,128)(2,1)}, bf16[288,2304]{1,0:T(8,128)(2,1)S(1)}, u32[]{:S(2)}, u32[]{:S(2)}) collective-permute-start(bf16[288,2304]{1,0:T(8,128)(2,1)} %get-tuple-element.416), channel_id=1, source_target_pairs={{0,1},{1,0},{2,5},{3,4},{4,3},{5,2},{6,7},{7,6},{8,9},{9,8},{10,13... | collective-permute-start | bytes 3981320 | tf_op jit(solution)/shard_map/ppermute | solution.py:121
  82.1 80.1 %collective-permute-start.6 = (bf16[288,2304]{1,0:T(8,128)(2,1)}, bf16[288,2304]{1,0:T(8,128)(2,1)}, u32[]{:S(2)}, u32[]{:S(2)}) collective-permute-start(bf16[288,2304]{1,0:T(8,128)(2,1)} %get-tuple-element.417), channel_id=1, source_target_pairs={{0,0},{1,1},{2,4},{3,5},{4,2},{5,3},{6,6},{7,7},{8,8},{9,9},{10,12... | collective-permute-start | bytes 3981320 | tf_op jit(solution)/shard_map/ppermute | solution.py:121
  192.1 16.2 %collective-permute-start.17 = (bf16[2304,1152]{1,0:T(8,128)(2,1)}, bf16[2304,1152]{1,0:T(8,128)(2,1)}, u32[]{:S(2)}, u32[]{:S(2)}) collective-permute-start(bf16[2304,1152]{1,0:T(8,128)(2,1)} %get-tuple-element.175), channel_id=1, source_target_pairs={{0,4},{4,0},{8,12},{12,8},{16,20},{20,16},{24,28},{28,24},{1,5},{5... | collective-permute-start | bytes 15925256 | tf_op jit(solution)/shard_map/ppermute | solution.py:335
  226.7 39.5 %collective-permute-start.18 = (bf16[576,4608]{1,0:T(8,128)(2,1)}, bf16[576,4608]{1,0:T(8,128)(2,1)}, u32[]{:S(2)}, u32[]{:S(2)}) collective-permute-start(bf16[576,4608]{1,0:T(8,128)(2,1)} %get-tuple-element.182), channel_id=1, source_target_pairs={{0,4},{4,0},{8,12},{12,8},{16,20},{20,16},{24,28},{28,24},{1,5},{5... | collective-permute-start | bytes 15925256 | tf_op jit(solution)/shard_map/ppermute | solution.py:335
  231.4 218.0 %collective-permute-start.12 = (bf16[20,1152]{1,0:T(8,128)(2,1)}, bf16[20,1152]{1,0:T(8,128)(2,1)}, u32[]{:S(2)}, u32[]{:S(2)}) collective-permute-start(bf16[20,1152]{1,0:T(8,128)(2,1)} %get-tuple-element.426), channel_id=1, source_target_pairs={{0,0},{1,1},{4,2},{5,3},{2,4},{3,5},{6,6},{7,7},{8,8},{9,9},{12,10... | collective-permute-start | bytes 138248 | tf_op jit(solution)/shard_map/ppermute | solution.py:128
  245.4 89.2 %collective-permute-start.20 = (bf16[1152,1152]{1,0:T(8,128)(2,1)}, bf16[1152,1152]{1,0:T(8,128)(2,1)}, u32[]{:S(2)}, u32[]{:S(2)}) collective-permute-start(bf16[1152,1152]{1,0:T(8,128)(2,1)} %fusion.6), channel_id=1, source_target_pairs={{0,8},{4,12},{8,0},{12,4},{16,24},{20,28},{24,16},{28,20},{1,9},{5... | collective-permute-start | bytes 7962632 | tf_op jit(solution)/shard_map/ppermute | solution.py:335
  275.5 57.8 %collective-permute-start.21 = (bf16[576,1152]{1,0:T(8,128)(2,1)}, bf16[576,1152]{1,0:T(8,128)(2,1)S(1)}, u32[]{:S(2)}, u32[]{:S(2)}) collective-permute-start(bf16[576,1152]{1,0:T(8,128)(2,1)} %get-tuple-element.192), channel_id=1, source_target_pairs={{0,4},{4,0},{8,12},{12,8},{16,20},{20,16},{24,28},{28,24},{1,5},{5... | collective-permute-start | bytes 3981320 | tf_op jit(solution)/shard_map/ppermute | solution.py:335
  293.3 93.3 %collective-permute-start.19 = (bf16[288,4608]{1,0:T(8,128)(2,1)}, bf16[288,4608]{1,0:T(8,128)(2,1)S(1)}, u32[]{:S(2)}, u32[]{:S(2)}) collective-permute-start(bf16[288,4608]{1,0:T(8,128)(2,1)} %fusion.5), channel_id=1, source_target_pairs={{0,16},{4,20},{8,24},{12,28},{16,0},{20,4},{24,8},{28,12},{1,17},{... | collective-permute-start | bytes 7962632 | tf_op jit(solution)/shard_map/ppermute | solution.py:335
  377.2 13.7 %collective-permute-start.22 = (bf16[576,2304]{1,0:T(8,128)(2,1)}, bf16[576,2304]{1,0:T(8,128)(2,1)S(1)}, u32[]{:S(2)}, u32[]{:S(2)}) collective-permute-start(bf16[576,2304]{1,0:T(8,128)(2,1)} %get-tuple-element.209), channel_id=1, source_target_pairs={{0,4},{1,5},{2,6},{3,7},{4,0},{5,1},{6,2},{7,3},{8,12},{9,13},{10,... | collective-permute-start | bytes 7962632 | tf_op jit(solution)/shard_map/ppermute | solution.py:144
  381.0 25.8 %collective-permute-start.26 = (bf16[288,1152]{1,0:T(8,128)(2,1)}, bf16[288,1152]{1,0:T(8,128)(2,1)S(1)}, u32[]{:S(2)}, u32[]{:S(2)}) collective-permute-start(bf16[288,1152]{1,0:T(8,128)(2,1)} %fusion.27), channel_id=1, source_target_pairs={{0,8},{4,12},{8,0},{12,4},{16,24},{20,28},{24,16},{28,20},{1,9},{5... | collective-permute-start | bytes 1990664 | tf_op jit(solution)/shard_map/ppermute | solution.py:335
  381.7 31.6 %collective-permute-start.25 = (bf16[576,1152]{1,0:T(8,128)(2,1)}, bf16[576,1152]{1,0:T(8,128)(2,1)}, u32[]{:S(2)}, u32[]{:S(2)}) collective-permute-start(bf16[576,1152]{1,0:T(8,128)(2,1)} %fusion.20), channel_id=1, source_target_pairs={{0,16},{4,20},{8,24},{12,28},{16,0},{20,4},{24,8},{28,12},{1,17},{... | collective-permute-start | bytes 3981320 | tf_op jit(solution)/shard_map/ppermute | solution.py:335
  386.6 31.6 %collective-permute-start.24 = (bf16[576,1152]{1,0:T(8,128)(2,1)}, bf16[576,1152]{1,0:T(8,128)(2,1)}, u32[]{:S(2)}, u32[]{:S(2)}) collective-permute-start(bf16[576,1152]{1,0:T(8,128)(2,1)} %get-tuple-element.205), channel_id=1, source_target_pairs={{0,4},{4,0},{8,12},{12,8},{16,20},{20,16},{24,28},{28,24},{1,5},{5... | collective-permute-start | bytes 3981320 | tf_op jit(solution)/shard_map/ppermute | solution.py:335
  401.9 32.1 %collective-permute-start.23 = (bf16[576,2304]{1,0:T(8,128)(2,1)}, bf16[576,2304]{1,0:T(8,128)(2,1)S(1)}, u32[]{:S(2)}, u32[]{:S(2)}) collective-permute-start(bf16[576,2304]{1,0:T(8,128)(2,1)} %get-tuple-element.212), channel_id=1, source_target_pairs={{0,4},{4,0},{8,12},{12,8},{16,20},{20,16},{24,28},{28,24},{1,5},{5... | collective-permute-start | bytes 7962632 | tf_op jit(solution)/shard_map/ppermute | solution.py:335
  406.8 42.6 %collective-permute-start.13 = (bf16[20,1152]{1,0:T(8,128)(2,1)}, bf16[20,1152]{1,0:T(8,128)(2,1)S(1)}, u32[]{:S(2)}, u32[]{:S(2)}) collective-permute-start(bf16[20,1152]{1,0:T(8,128)(2,1)} %get-tuple-element.427), channel_id=1, source_target_pairs={{1,0},{0,1},{5,2},{4,3},{3,4},{2,5},{7,6},{6,7},{9,8},{8,9},{13,10... | collective-permute-start | bytes 138248 | tf_op jit(solution)/shard_map/ppermute | solution.py:128
  413.2 40.7 %collective-permute-start.33 = (bf16[144,4608]{1,0:T(8,128)(2,1)}, bf16[144,4608]{1,0:T(8,128)(2,1)}, u32[]{:S(2)}, u32[]{:S(2)}) collective-permute-start(bf16[144,4608]{1,0:T(8,128)(2,1)} %fusion.19), channel_id=1, source_target_pairs={{0,8},{4,12},{8,0},{12,4},{16,24},{20,28},{24,16},{28,20},{1,9},{5... | collective-permute-start | bytes 3981320 | tf_op jit(solution)/shard_map/ppermute | solution.py:335
  449.3 26.5 %collective-permute-start.31 = (bf16[1152,1152]{1,0:T(8,128)(2,1)}, bf16[1152,1152]{1,0:T(8,128)(2,1)}, u32[]{:S(2)}, u32[]{:S(2)}) collective-permute-start(bf16[1152,1152]{1,0:T(8,128)(2,1)} %get-tuple-element.231), channel_id=1, source_target_pairs={{0,4},{4,0},{8,12},{12,8},{16,20},{20,16},{24,28},{28,24},{1,5},{5... | collective-permute-start | bytes 7962632 | tf_op jit(solution)/shard_map/ppermute | solution.py:335
  450.2 18.1 %collective-permute-start.32 = (bf16[288,1152]{1,0:T(8,128)(2,1)}, bf16[288,1152]{1,0:T(8,128)(2,1)S(1)}, u32[]{:S(2)}, u32[]{:S(2)}) collective-permute-start(bf16[288,1152]{1,0:T(8,128)(2,1)} %fusion.26), channel_id=1, source_target_pairs={{0,16},{4,20},{8,24},{12,28},{16,0},{20,4},{24,8},{28,12},{1,17},{... | collective-permute-start | bytes 1990664 | tf_op jit(solution)/shard_map/ppermute | solution.py:335
  452.8 19.5 %collective-permute-start.27 = (bf16[288,1152]{1,0:T(8,128)(2,1)S(1)}, bf16[288,1152]{1,0:T(8,128)(2,1)S(1)}, u32[]{:S(2)}, u32[]{:S(2)}) collective-permute-start(bf16[288,1152]{1,0:T(8,128)(2,1)S(1)} %get-tuple-element.424), channel_id=1, source_target_pairs={{0,0},{1,1},{4,2},{5,3},{2,4},{3,5},{6,6},{7,7},{8,8},{9,9},{12,10... | collective-permute-start | bytes 1990664 | tf_op jit(solution)/shard_map/ppermute | solution.py:128
  453.7 20.2 %collective-permute-start.28 = (bf16[288,1152]{1,0:T(8,128)(2,1)S(1)}, bf16[288,1152]{1,0:T(8,128)(2,1)S(1)}, u32[]{:S(2)}, u32[]{:S(2)}) collective-permute-start(bf16[288,1152]{1,0:T(8,128)(2,1)S(1)} %get-tuple-element.425), channel_id=1, source_target_pairs={{1,0},{0,1},{5,2},{4,3},{3,4},{2,5},{7,6},{6,7},{9,8},{8,9},{13,10... | collective-permute-start | bytes 1990664 | tf_op jit(solution)/shard_map/ppermute | solution.py:128
  454.0 44.9 %collective-permute-start.36 = (bf16[144,1152]{1,0:T(8,128)(2,1)}, bf16[144,1152]{1,0:T(8,128)(2,1)S(1)}, u32[]{:S(2)}, u32[]{:S(2)}) collective-permute-start(bf16[144,1152]{1,0:T(8,128)(2,1)} %fusion.45), channel_id=1, source_target_pairs={{0,16},{4,20},{8,24},{12,28},{16,0},{20,4},{24,8},{28,12},{1,17},{... | collective-permute-start | bytes 995336 | tf_op jit(solution)/shard_map/ppermute | solution.py:335
  468.3 74.7 %collective-permute-start.61 = (bf16[144,1152]{1,0:T(8,128)(2,1)}, bf16[144,1152]{1,0:T(8,128)(2,1)S(1)}, u32[]{:S(2)}, u32[]{:S(2)}) collective-permute-start(bf16[144,1152]{1,0:T(8,128)(2,1)} %get-tuple-element.220), channel_id=1, source_target_pairs={{0,3},{1,0},{2,1},{3,2},{4,7},{5,4},{6,5},{7,6},{8,11},{9,8},{10,9... | collective-permute-start | bytes 995336 | tf_op jit(solution)/shard_map/ppermute | solution.py:329
  472.4 64.7 %collective-permute-start.59 = (bf16[144,1152]{1,0:T(8,128)(2,1)}, bf16[144,1152]{1,0:T(8,128)(2,1)}, u32[]{:S(2)}, u32[]{:S(2)}) collective-permute-start(bf16[144,1152]{1,0:T(8,128)(2,1)} %get-tuple-element.300), channel_id=1, source_target_pairs={{0,1},{1,2},{2,3},{3,0},{4,5},{5,6},{6,7},{7,4},{8,9},{9,10},{10,1... | collective-permute-start | bytes 995336 | tf_op jit(solution)/shard_map/ppermute | solution.py:329
  473.8 24.1 %collective-permute-start.29 = (bf16[288,2304]{1,0:T(8,128)(2,1)S(1)}, bf16[288,2304]{1,0:T(8,128)(2,1)S(1)}, u32[]{:S(2)}, u32[]{:S(2)}) collective-permute-start(bf16[288,2304]{1,0:T(8,128)(2,1)S(1)} %copy-done.40), channel_id=1, source_target_pairs={{0,8},{4,12},{8,0},{12,4},{16,24},{20,28},{24,16},{28,20},{1,9},{5... | collective-permute-start | bytes 3981320 | tf_op jit(solution)/shard_map/ppermute | solution.py:335
  475.8 11.6 %collective-permute-start.30 = (f32[256,128]{1,0:T(8,128)S(1)}, f32[256,128]{1,0:T(8,128)S(1)}, u32[]{:S(2)}, u32[]{:S(2)}) collective-permute-start(f32[256,128]{1,0:T(8,128)S(1)} %bitcast.568), channel_id=1, source_target_pairs={{0,4},{4,0},{8,12},{12,8},{16,20},{20,16},{24,28},{28,24},{1,5},{5... | collective-permute-start | bytes 393224 | tf_op jit(solution)/shard_map/ppermute | solution.py:335
  487.5 42.7 %collective-permute-start.34 = (bf16[576,1152]{1,0:T(8,128)(2,1)}, bf16[576,1152]{1,0:T(8,128)(2,1)S(1)}, u32[]{:S(2)}, u32[]{:S(2)}) collective-permute-start(bf16[576,1152]{1,0:T(8,128)(2,1)} %fusion.17), channel_id=1, source_target_pairs={{0,16},{4,20},{8,24},{12,28},{16,0},{20,4},{24,8},{28,12},{1,17},{... | collective-permute-start | bytes 3981320 | tf_op jit(solution)/shard_map/ppermute | solution.py:335
  497.9 22.8 %collective-permute-start.35 = (bf16[144,1152]{1,0:T(8,128)(2,1)}, bf16[144,1152]{1,0:T(8,128)(2,1)S(1)}, u32[]{:S(2)}, u32[]{:S(2)}) collective-permute-start(bf16[144,1152]{1,0:T(8,128)(2,1)} %fusion.41), channel_id=1, source_target_pairs={{0,8},{4,12},{8,0},{12,4},{16,24},{20,28},{24,16},{28,20},{1,9},{5... | collective-permute-start | bytes 995336 | tf_op jit(solution)/shard_map/ppermute | solution.py:335
  498.9 40.5 %collective-permute-start.60 = (bf16[144,1152]{1,0:T(8,128)(2,1)}, bf16[144,1152]{1,0:T(8,128)(2,1)}, u32[]{:S(2)}, u32[]{:S(2)}) collective-permute-start(bf16[144,1152]{1,0:T(8,128)(2,1)} %get-tuple-element.301), channel_id=1, source_target_pairs={{0,2},{1,3},{2,0},{3,1},{4,6},{5,7},{6,4},{7,5},{8,10},{9,11},{10,... | collective-permute-start | bytes 995336 | tf_op jit(solution)/shard_map/ppermute | solution.py:329
  520.7 11.6 %collective-permute-start.39 = (f32[128,128]{1,0:T(8,128)S(1)}, f32[128,128]{1,0:T(8,128)S(1)}, u32[]{:S(2)}, u32[]{:S(2)}) collective-permute-start(f32[128,128]{1,0:T(8,128)S(1)} %bitcast_add_fusion), channel_id=1, source_target_pairs={{0,16},{4,20},{8,24},{12,28},{16,0},{20,4},{24,8},{28,12},{1,17},{... | collective-permute-start | bytes 196616 | tf_op jit(solution)/shard_map/ppermute | solution.py:335
  530.2 14.5 %collective-permute-start.38 = (bf16[144,2304]{1,0:T(8,128)(2,1)S(1)}, bf16[144,2304]{1,0:T(8,128)(2,1)S(1)}, u32[]{:S(2)}, u32[]{:S(2)}) collective-permute-start(bf16[144,2304]{1,0:T(8,128)(2,1)S(1)} %fusion.25), channel_id=1, source_target_pairs={{0,16},{4,20},{8,24},{12,28},{16,0},{20,4},{24,8},{28,12},{1,17},{... | collective-permute-start | bytes 1990664 | tf_op jit(solution)/shard_map/ppermute | solution.py:335
  532.3 19.0 %collective-permute-start.37 = (bf16[288,1152]{1,0:T(8,128)(2,1)S(1)}, bf16[288,1152]{1,0:T(8,128)(2,1)S(1)}, u32[]{:S(2)}, u32[]{:S(2)}) collective-permute-start(bf16[288,1152]{1,0:T(8,128)(2,1)S(1)} %fusion.24), channel_id=1, source_target_pairs={{0,8},{4,12},{8,0},{12,4},{16,24},{20,28},{24,16},{28,20},{1,9},{5... | collective-permute-start | bytes 1990664 | tf_op jit(solution)/shard_map/ppermute | solution.py:335
  537.1 42.8 %collective-permute-start.58 = (bf16[36,4608]{1,0:T(8,128)(2,1)S(1)}, bf16[36,4608]{1,0:T(8,128)(2,1)S(1)}, u32[]{:S(2)}, u32[]{:S(2)}) collective-permute-start(bf16[36,4608]{1,0:T(8,128)(2,1)S(1)} %get-tuple-element.239), channel_id=1, source_target_pairs={{0,3},{1,0},{2,1},{3,2},{4,7},{5,4},{6,5},{7,6},{8,11},{9,8},{10,9... | collective-permute-start | bytes 995336 | tf_op jit(solution)/shard_map/ppermute | solution.py:329
  539.4 22.2 %collective-permute-start.56 = (bf16[36,4608]{1,0:T(8,128)(2,1)S(1)}, bf16[36,4608]{1,0:T(8,128)(2,1)S(1)}, u32[]{:S(2)}, u32[]{:S(2)}) collective-permute-start(bf16[36,4608]{1,0:T(8,128)(2,1)S(1)} %get-tuple-element.295), channel_id=1, source_target_pairs={{0,1},{1,2},{2,3},{3,0},{4,5},{5,6},{6,7},{7,4},{8,9},{9,10},{10,1... | collective-permute-start | bytes 995336 | tf_op jit(solution)/shard_map/ppermute | solution.py:329
  543.0 36.8 %collective-permute-start.57 = (bf16[36,4608]{1,0:T(8,128)(2,1)S(1)}, bf16[36,4608]{1,0:T(8,128)(2,1)S(1)}, u32[]{:S(2)}, u32[]{:S(2)}) collective-permute-start(bf16[36,4608]{1,0:T(8,128)(2,1)S(1)} %get-tuple-element.296), channel_id=1, source_target_pairs={{0,2},{1,3},{2,0},{3,1},{4,6},{5,7},{6,4},{7,5},{8,10},{9,11},{10,... | collective-permute-start | bytes 995336 | tf_op jit(solution)/shard_map/ppermute | solution.py:329
  544.7 35.2 %collective-permute-start.53 = (bf16[36,1152]{1,0:T(8,128)(2,1)S(1)}, bf16[36,1152]{1,0:T(8,128)(2,1)S(1)}, u32[]{:S(2)}, u32[]{:S(2)}) collective-permute-start(bf16[36,1152]{1,0:T(8,128)(2,1)S(1)} %get-tuple-element.289), channel_id=1, source_target_pairs={{0,1},{1,2},{2,3},{3,0},{4,5},{5,6},{6,7},{7,4},{8,9},{9,10},{10,1... | collective-permute-start | bytes 248840 | tf_op jit(solution)/shard_map/ppermute | solution.py:329
  551.4 30.5 %collective-permute-start.43 = (f32[64,128]{1,0:T(8,128)S(1)}, f32[64,128]{1,0:T(8,128)S(1)}, u32[]{:S(2)}, u32[]{:S(2)}) collective-permute-start(f32[64,128]{1,0:T(8,128)S(1)} %bitcast_add_fusion.1), channel_id=1, source_target_pairs={{0,8},{4,12},{8,0},{12,4},{16,24},{20,28},{24,16},{28,20},{1,9},{5... | collective-permute-start | bytes 98312 | tf_op jit(solution)/shard_map/ppermute | solution.py:335
  561.5 27.2 %collective-permute-start.55 = (bf16[36,1152]{1,0:T(8,128)(2,1)S(1)}, bf16[36,1152]{1,0:T(8,128)(2,1)S(1)}, u32[]{:S(2)}, u32[]{:S(2)}) collective-permute-start(bf16[36,1152]{1,0:T(8,128)(2,1)S(1)} %get-tuple-element.249), channel_id=1, source_target_pairs={{0,3},{1,0},{2,1},{3,2},{4,7},{5,4},{6,5},{7,6},{8,11},{9,8},{10,9... | collective-permute-start | bytes 248840 | tf_op jit(solution)/shard_map/ppermute | solution.py:329
  579.9 23.7 %collective-permute-start.52 = (bf16[36,2304]{1,0:T(8,128)(2,1)S(1)}, bf16[36,2304]{1,0:T(8,128)(2,1)S(1)}, u32[]{:S(2)}, u32[]{:S(2)}) collective-permute-start(bf16[36,2304]{1,0:T(8,128)(2,1)S(1)} %get-tuple-element.261), channel_id=1, source_target_pairs={{0,3},{1,0},{2,1},{3,2},{4,7},{5,4},{6,5},{7,6},{8,11},{9,8},{10,9... | collective-permute-start | bytes 497672 | tf_op jit(solution)/shard_map/ppermute | solution.py:329
  581.9 21.7 %collective-permute-start.51 = (bf16[36,2304]{1,0:T(8,128)(2,1)S(1)}, bf16[36,2304]{1,0:T(8,128)(2,1)S(1)}, u32[]{:S(2)}, u32[]{:S(2)}) collective-permute-start(bf16[36,2304]{1,0:T(8,128)(2,1)S(1)} %get-tuple-element.284), channel_id=1, source_target_pairs={{0,2},{1,3},{2,0},{3,1},{4,6},{5,7},{6,4},{7,5},{8,10},{9,11},{10,... | collective-permute-start | bytes 497672 | tf_op jit(solution)/shard_map/ppermute | solution.py:329
  588.7 18.8 %collective-permute-start.49 = (bf16[36,1152]{1,0:T(8,128)(2,1)S(1)}, bf16[36,1152]{1,0:T(8,128)(2,1)S(1)}, u32[]{:S(2)}, u32[]{:S(2)}) collective-permute-start(bf16[36,1152]{1,0:T(8,128)(2,1)S(1)} %get-tuple-element.254), channel_id=1, source_target_pairs={{0,3},{1,0},{2,1},{3,2},{4,7},{5,4},{6,5},{7,6},{8,11},{9,8},{10,9... | collective-permute-start | bytes 248840 | tf_op jit(solution)/shard_map/ppermute | solution.py:329
  588.8 15.8 %collective-permute-start.47 = (bf16[36,1152]{1,0:T(8,128)(2,1)S(1)}, bf16[36,1152]{1,0:T(8,128)(2,1)S(1)}, u32[]{:S(2)}, u32[]{:S(2)}) collective-permute-start(bf16[36,1152]{1,0:T(8,128)(2,1)S(1)} %get-tuple-element.277), channel_id=1, source_target_pairs={{0,1},{1,2},{2,3},{3,0},{4,5},{5,6},{6,7},{7,4},{8,9},{9,10},{10,1... | collective-permute-start | bytes 248840 | tf_op jit(solution)/shard_map/ppermute | solution.py:329
  591.0 16.5 %collective-permute-start.48 = (bf16[36,1152]{1,0:T(8,128)(2,1)S(1)}, bf16[36,1152]{1,0:T(8,128)(2,1)S(1)}, u32[]{:S(2)}, u32[]{:S(2)}) collective-permute-start(bf16[36,1152]{1,0:T(8,128)(2,1)S(1)} %get-tuple-element.278), channel_id=1, source_target_pairs={{0,2},{1,3},{2,0},{3,1},{4,6},{5,7},{6,4},{7,5},{8,10},{9,11},{10,... | collective-permute-start | bytes 248840 | tf_op jit(solution)/shard_map/ppermute | solution.py:329
  603.6 13.7 %collective-permute-start.46 = (f32[16,128]{1,0:T(8,128)S(1)}, f32[16,128]{1,0:T(8,128)S(1)}, u32[]{:S(2)}, u32[]{:S(2)}) collective-permute-start(f32[16,128]{1,0:T(8,128)S(1)} %get-tuple-element.267), channel_id=1, source_target_pairs={{0,3},{1,0},{2,1},{3,2},{4,7},{5,4},{6,5},{7,6},{8,11},{9,8},{10,9... | collective-permute-start | bytes 24584 | tf_op jit(solution)/shard_map/ppermute | solution.py:329
  603.6 21.1 %collective-permute-start.42 = (bf16[72,1152]{1,0:T(8,128)(2,1)S(1)}, bf16[72,1152]{1,0:T(8,128)(2,1)S(1)}, u32[]{:S(2)}, u32[]{:S(2)}) collective-permute-start(bf16[72,1152]{1,0:T(8,128)(2,1)S(1)} %get-tuple-element.265), channel_id=1, source_target_pairs={{0,3},{1,0},{2,1},{3,2},{4,7},{5,4},{6,5},{7,6},{8,11},{9,8},{10,9... | collective-permute-start | bytes 497672 | tf_op jit(solution)/shard_map/ppermute | solution.py:329
  608.7 13.4 %collective-permute-start.40 = (bf16[72,1152]{1,0:T(8,128)(2,1)S(1)}, bf16[72,1152]{1,0:T(8,128)(2,1)S(1)}, u32[]{:S(2)}, u32[]{:S(2)}) collective-permute-start(bf16[72,1152]{1,0:T(8,128)(2,1)S(1)} %get-tuple-element.263), channel_id=1, source_target_pairs={{0,1},{1,2},{2,3},{3,0},{4,5},{5,6},{6,7},{7,4},{8,9},{9,10},{10,1... | collective-permute-start | bytes 497672 | tf_op jit(solution)/shard_map/ppermute | solution.py:329
  (102 other events, 1330.2 us)

commit v4 on v3

--- a/solution.py
+++ b/solution.py
@@ -671,20 +671,6 @@
     patches = project(head_in, w_head) + b_head
     patches = go.back(patches[:image_dev], patches[image_dev:])
 
-    patch_grid = patches.reshape(item_count, grid_rows, grid_cols, PATCH, PATCH, LAT_CH)
-    latent = jnp.transpose(patch_grid, (0, 5, 1, 3, 2, 4)).reshape(lat_shape)
-    padded = jnp.pad(with_halo(latent, "gy", 3, 1), ((0, 0), (0, 0), (1, 1), (0, 0)))
-    prediction = jnp.zeros(lat_shape, F32) + b_conv[None, :, None, None]
-    conv_taps = []
-    for row_off in range(3):
-        for col_off in range(3):
-            window = padded[:, :, row_off : row_off + lat_rows, col_off : col_off + lat_cols]
-            prediction = prediction + jnp.einsum(
-                "oi,bihw->bohw", w_conv[:, :, row_off, col_off], window, precision=HIGHEST
-            )
-            conv_taps.append(jnp.einsum("bohw,bihw->oi", pred_grad, window, precision=HIGHEST))
-    grad_w_conv = jnp.stack(conv_taps, axis=-1)
-
     grad_w_head = jnp.einsum("rd,ro->do", head_in.astype(F32), grad_patches, precision=HIGHEST)
     grad_normed_head = jnp.einsum("ro,do->rd", grad_patches, w_head.astype(F32), precision=HIGHEST)
     grad_image_out, grad_gain_head, grad_bias_head = head_norm_back(grad_normed_head)
@@ -720,6 +706,21 @@
     sum_proj, _ = scatter(mixed, proj_in, False)
     proj_in = sum_proj.advance(proj_in)
     grad_mixed = back(proj_in, w_proj, BF16)
+    grad_mixed, text_out, patches = lax.optimization_barrier((grad_mixed, text_out, patches))
+    patch_grid = patches.reshape(item_count, grid_rows, grid_cols, PATCH, PATCH, LAT_CH)
+    latent = jnp.transpose(patch_grid, (0, 5, 1, 3, 2, 4)).reshape(lat_shape)
+    padded = jnp.pad(with_halo(latent, "gy", 3, 1), ((0, 0), (0, 0), (1, 1), (0, 0)))
+    prediction = jnp.zeros(lat_shape, F32) + b_conv[None, :, None, None]
+    conv_taps = []
+    for row_off in range(3):
+        for col_off in range(3):
+            window = padded[:, :, row_off : row_off + lat_rows, col_off : col_off + lat_cols]
+            prediction = prediction + jnp.einsum(
+                "oi,bihw->bohw", w_conv[:, :, row_off, col_off], window, precision=HIGHEST
+            )
+            conv_taps.append(jnp.einsum("bohw,bihw->oi", pred_grad, window, precision=HIGHEST))
+    grad_w_conv = jnp.stack(conv_taps, axis=-1)
+
     parts = attend_back(qkv, others, bias, mixed, lse, grad_mixed, 0, HEADS // 2, ())
     parts = sum_proj.advance(*parts, after=parts[:1])
     parts = sum_down.advance(*parts)
@@ -734,9 +735,9 @@
     grad_kv = grad_kv.astype(BF16)
     sum_kv, _ = scatter(normed, grad_kv, False)
     grad_kv = sum_kv.advance(grad_kv)
-    grad_kv = sum_proj.advance(grad_kv)
     grad_kv = sum_down.advance(grad_kv)
     grad_kv = sum_q.advance(grad_kv)
+    grad_kv = sum_proj.advance(grad_kv)
     grad_qkv = jnp.concatenate([grads[0], grad_kv], axis=1)
     grad_one = back(grad_qkv, w_qkv, F32)
     grad_one = sum_kv.advance(grad_one, after=(grad_one,))
@@ -747,6 +748,8 @@
     skip_here = go.back(skip_in[:block], skip_in[block:])
     sum_skip, _ = scatter(joined, skip_in, True)
     sum_skip.advance()
+    down_done = sum_down.finish()
+    line.append(down_done)
     vectors = (
         grad_b_skip,
         grad_gain_attn,
@@ -789,7 +792,7 @@
     sum_kv.advance()
     sum_skip.advance()
     sum_small.advance()
-    down_done, up_done, proj_done = sum_down.finish(), sum_up.finish(), sum_proj.finish()
+    up_done, proj_done = sum_up.finish(), sum_proj.finish()
     q_done, kv_done, skip_done = sum_q.finish(), sum_kv.finish(), sum_skip.finish()
     packed = sum_small.finish().reshape(-1)
     small = []

time: 637 us -> 624 us (0.980)
  waiting for transfers between devices: 73 us -> 55.4 us
  local copies, waits for them, and re-layouts: 58.7 us -> 65.3 us
    ppermute x21, waiting for transfers between devices: 38.3 us -> 17 us  [send(): lax.ppermute(value, 'gy', [(i, (i + step) % self.gy) for i in range(self....]
    ppermute x21, waiting for transfers between devices: 20.8 us -> 27.8 us  [send(): got = lax.ppermute(sends[0], 'gx', pairs)]
    unnamed x185 -> x153, local copies, waits for them, and re-layouts: 16.8 us -> 13.4 us
  transfers between devices with their start and end apart: 62 -> 62, of which waited for: 13 -> 11; matrix products, arithmetic and copies ran while one was open for 23% -> 25% of each run, Pallas kernels for 29% -> 30%
where the time goes in v4:
time: 624 us; the launch traced here: 613 us
  Pallas kernels  209 us (33%)
  starting transfers between devices  138 us (22%)
  matrix products  73 us (12%)
  other arithmetic  69.1 us (11%)
  local copies, waits for them, and re-layouts  65.3 us (10%)
  waiting for transfers between devices  55.4 us (9%)
    pallas_call x2, Pallas kernels, attend_back(): pl.pallas_call(partial(attend_back_kernel, holders, width, keys // 2, fir...  70.1 us
    ppermute x21, starting transfers between devices, send(): lax.ppermute(value, 'gy', [(i, (i + step) % self.gy) for i in range(self....  61.2 us
    pallas_call x6, Pallas kernels, weight_grad(): pl.pallas_call(partial(weight_grad_kernel, tall // (2 * block), block), o...  54.4 us
    dot_general x6, matrix products, project(): return jnp.einsum('rd,de->re', rows, weight, preferred_element_type=F32)  51 us
    pallas_call x1, Pallas kernels, attend(): pl.pallas_call(partial(attend_kernel, holders, width, 288), out_shape=(ja...  38.4 us
    pallas_call x4, Pallas kernels, back(): pl.pallas_call(back_kernel, out_shape=jax.ShapeDtypeStruct((count, height...  37.4 us
    ppermute x21, waiting for transfers between devices, send(): got = lax.ppermute(sends[0], 'gx', pairs)  27.8 us
    ppermute x8, starting transfers between devices, send(): lax.ppermute(sends[t], ('gx', 'gy'), self.perms[t])  27.2 us
  transfers between devices with their start and end apart: 62, of which 11 were waited for; matrix products, arithmetic and copies ran while one was open for 25% of the time, Pallas kernels for 30%

profile of v4, /device:TPU:0, one launch (start us, length us, event | category | flops | bytes accessed | tf_op | source)
XLA Modules:
  0.0 613.4 jit_solution(6577291770502687521)
XLA Ops:
  5.4 7.1 %fusion.13 = bf16[576,1152]{1,0:T(8,128)(2,1)S(1)} fusion(bf16[576,2304]{1,0:T(8,128)(2,1)S(1)} %bitcast.542, bf16[2304,1152]{1,0:T(8,128)(2,1)} %param.35, f32[1152]{0:T(1024)S(1)} %copy-done.63), kind=kOutput, calls=%fused_computation.31 | convolution fusion | flops 3058974720 | bytes 9294336 | tf_op jit(solution)/shard_map/rd,de->re/dot_general | solution.py:85
  13.4 5.0 collective-permute-start.2
  29.9 9.1 %collective-permute-done.1 = bf16[288,1152]{1,0:T(8,128)(2,1)} collective-permute-done((bf16[288,1152]{1,0:T(8,128)(2,1)S(1)}, bf16[288,1152]{1,0:T(8,128)(2,1)}, u32[]{:S(2)}, u32[]{:S(2)}) %collective-permute-start.1) | collective-permute-done | bytes 663584 | tf_op jit(solution)/shard_map/ppermute | solution.py:121
  41.9 9.4 %convolution_convert_fusion.refs_0_ = bf16[576,3456]{1,0:T(8,128)(2,1)S(1)} fusion(bf16[576,1152]{1,0:T(8,128)(2,1)S(1)} %add_convert_fusion.3.rows, bf16[1152,3456]{1,0:T(8,128)(2,1)} %weight.7), kind=kOutput, calls=%fused_computation.5 | convolution fusion | flops 4588462080 | bytes 13271040 | tf_op jit(solution)/shard_map/rd,de->re/dot_general | solution.py:85
  53.0 9.1 %collective-permute-start.4 = (bf16[576,2304]{1,0:T(8,128)(2,1)}, bf16[576,2304]{1,0:T(8,128)(2,1)}, u32[]{:S(2)}, u32[]{:S(2)}) collective-permute-start(bf16[576,2304]{1,0:T(8,128)(2,1)} %slice.279), channel_id=1, source_target_pairs={{0,4},{1,5},{2,6},{3,7},{4,0},{5,1},{6,2},{7,3},{8,12},{9,13},{10,... | collective-permute-start | bytes 7962632 | tf_op jit(solution)/shard_map/ppermute | solution.py:144
  62.9 7.8 %collective-permute-start.10 = (f32[21,1152]{1,0:T(8,128)S(1)}, f32[21,1152]{1,0:T(8,128)S(1)}, u32[]{:S(2)}, u32[]{:S(2)}) collective-permute-start(f32[21,1152]{1,0:T(8,128)S(1)} %get-tuple-element.438), channel_id=1, source_target_pairs={{0,1},{1,0},{2,5},{3,4},{4,3},{5,2},{6,7},{7,6},{8,9},{9,8},{10,13... | collective-permute-start | bytes 290312 | tf_op jit(solution)/shard_map/ppermute | solution.py:121
  76.5 3.4 dynamic-slice_bitcast_fusion
  80.0 11.9 %collective-permute-start.6 = (bf16[288,2304]{1,0:T(8,128)(2,1)}, bf16[288,2304]{1,0:T(8,128)(2,1)}, u32[]{:S(2)}, u32[]{:S(2)}) collective-permute-start(bf16[288,2304]{1,0:T(8,128)(2,1)} %get-tuple-element.423), channel_id=1, source_target_pairs={{0,0},{1,1},{2,4},{3,5},{4,2},{5,3},{6,6},{7,7},{8,8},{9,9},{10,12... | collective-permute-start | bytes 3981320 | tf_op jit(solution)/shard_map/ppermute | solution.py:121
  93.2 38.4 %attend.1 = (bf16[576,1152]{1,0:T(8,128)(2,1)}, f32[576,128]{1,0:T(8,128)}) custom-call(bf16[576,3456]{1,0:T(8,128)(2,1)} %copy-done.16, bf16[576,2304]{1,0:T(8,128)(2,1)} %collective-permute-done.4.refs_1_, f32[1152,128]{1,0:T(8,128)} %broadcast_in_dim.37.refs_2_), custom_call_target="tpu_custom_call" | custom-call | flops 1048576 | bytes 1048576 | tf_op jit(solution)/shard_map/attend/pallas_call | solution.py:426
  131.6 3.6 fusion.193
  136.5 22.4 %add_convert_fusion = (bf16[576,4608]{1,0:T(8,128)(2,1)}, bf16[576,4608]{1,0:T(8,128)(2,1)S(1)}) fusion(f32[4608]{0:T(1024)S(1)} %copy-done.62, bf16[576,1152]{1,0:T(8,128)(2,1)S(1)} %add_convert_fusion.2.rows, bf16[1152,4608]{1,0:T(8,128)(2,1)} %weight.5), kind=kOutput, calls=%fused_computation.3 | convolution fusion | flops 6216155136 | bytes 22579200 | tf_op jit(solution)/shard_map/rd,de->re/dot_general | solution.py:85
  159.0 8.1 %fusion.194 = (bf16[576,1152]{1,0:T(8,128)(2,1)}, f32[576,1152]{1,0:T(8,128)S(1)}) fusion(f32[1152]{0:T(1024)S(1)} %copy-done.65, f32[576,1152]{1,0:T(8,128)S(1)} %get-tuple-element.472, bf16[576,4608]{1,0:T(8,128)(2,1)S(1)} %get-tuple-element.174.rows, bf16[4608,1152]{1,0:T(8,128)(2,1)S(1)} %bitcast.541), kind=kOutput, calls=%fused_computation.387 | convolution fusion | flops 6117285888 | bytes 22565376 | tf_op jit(solution)/shard_map/rd,de->re/dot_general | solution.py:85
  174.4 14.1 %weight_grad.6 = (bf16[4608,1152]{1,0:T(8,128)(2,1)}, bf16[2304,1152]{1,0:T(8,128)(2,1)}, f32[1,1152]{1,0:T(1,128)}) custom-call(s32[1]{0:T(128)} %bitcast.other, bf16[576,4608]{1,0:T(8,128)(2,1)} %copy-done.29, bf16[576,1152]{1,0:T(8,128)(2,1)S(1)} %fusion.23.grads), custom_call_target="tpu_custom_call" | custom-call | flops 1048576 | bytes 1048576 | tf_op jit(solution)/shard_map/weight_grad/pallas_call | solution.py:195
  193.1 12.6 %back.4.grads = bf16[576,4608]{1,0:T(8,128)(2,1)} custom-call(bf16[576,1152]{1,0:T(8,128)(2,1)S(1)} %fusion.23.grads, bf16[4608,1152]{1,0:T(8,128)(2,1)} %weight.4, bf16[576,4608]{1,0:T(8,128)(2,1)} %get-tuple-element.181.refs_0_), custom_call_target="tpu_custom_call" | custom-call | flops 1048576 | bytes 1048576 | tf_op jit(solution)/shard_map/back/pallas_call | solution.py:164
  212.1 14.0 %weight_grad.7 = (bf16[1152,4608]{1,0:T(8,128)(2,1)}, bf16[576,4608]{1,0:T(8,128)(2,1)}, f32[1,4608]{1,0:T(1,128)S(1)}) custom-call(s32[1]{0:T(128)} %bitcast.other, bf16[576,1152]{1,0:T(8,128)(2,1)S(1)} %add_convert_fusion.2.rows, bf16[576,4608]{1,0:T(8,128)(2,1)} %back.4.grads), custom_call_target="tpu_custom_call" | custom-call | flops 1048576 | bytes 1048576 | tf_op jit(solution)/shard_map/weight_grad/pallas_call | solution.py:195
  232.4 3.4 pad_maximum_fusion.2.rows
  241.7 12.8 %back.5 = f32[576,1152]{1,0:T(8,128)S(1)} custom-call(bf16[576,4608]{1,0:T(8,128)(2,1)} %back.4.grads, bf16[1152,4608]{1,0:T(8,128)(2,1)} %weight.5), custom_call_target="tpu_custom_call" | custom-call | flops 1048576 | bytes 1048576 | tf_op jit(solution)/shard_map/back/pallas_call | solution.py:164
  268.3 4.4 weight_grad.8
  278.4 6.6 %collective-permute-start.21 = (bf16[576,1152]{1,0:T(8,128)(2,1)}, bf16[576,1152]{1,0:T(8,128)(2,1)}, u32[]{:S(2)}, u32[]{:S(2)}) collective-permute-start(bf16[576,1152]{1,0:T(8,128)(2,1)} %get-tuple-element.198), channel_id=1, source_target_pairs={{0,4},{4,0},{8,12},{12,8},{16,20},{20,16},{24,28},{28,24},{1,5},{5... | collective-permute-start | bytes 3981320 | tf_op jit(solution)/shard_map/ppermute | solution.py:335
  296.2 31.0 %attend_back.2 = (bf16[8,576,128]{2,1,0:T(8,128)(2,1)}, bf16[2,8,1152,128]{3,2,1,0:T(8,128)(2,1)}) custom-call(bf16[576,3456]{1,0:T(8,128)(2,1)} %copy-done.16, bf16[576,2304]{1,0:T(8,128)(2,1)} %collective-permute-done.4.refs_1_, f32[1152,128]{1,0:T(8,128)} %broadcast_in_dim.37.refs_2_, bf16[576,1152]{1,0:T(8,128)(2,1)} %get-tuple-element.172.rows.refs_3_, ...), custom_call_target="tpu_custom_call" | custom-call | flops 1048576 | bytes 1048576 | tf_op jit(solution)/shard_map/attend_back/pallas_call | solution.py:524
  334.7 3.7 fusion.20
  338.3 39.1 %attend_back.3 = (bf16[576,1152]{1,0:T(8,128)(2,1)}, bf16[576,2304]{1,0:T(8,128)(2,1)}, bf16[576,2304]{1,0:T(8,128)(2,1)}) custom-call(bf16[576,3456]{1,0:T(8,128)(2,1)} %copy-done.16, bf16[576,2304]{1,0:T(8,128)(2,1)} %collective-permute-done.4.refs_1_, f32[1152,128]{1,0:T(8,128)} %broadcast_in_dim.37.refs_2_, ...), custom_call_target="tpu_custom_call" | custom-call | flops 1048576 | bytes 1048576 | tf_op jit(solution)/shard_map/attend_back/pallas_call | solution.py:524
  382.4 4.4 weight_grad.9
  387.0 4.3 fusion.19
  393.5 8.8 %weight_grad.10 = (bf16[1152,2304]{1,0:T(8,128)(2,1)}, bf16[576,2304]{1,0:T(8,128)(2,1)}, f32[1,2304]{1,0:T(1,128)}) custom-call(s32[1]{0:T(128)} %bitcast.other, bf16[576,1152]{1,0:T(8,128)(2,1)S(1)} %copy-done.3, bf16[576,2304]{1,0:T(8,128)(2,1)} %add_convert_fusion.1.grads), custom_call_target="tpu_custom_call" | custom-call | flops 1048576 | bytes 1048576 | tf_op jit(solution)/shard_map/weight_grad/pallas_call | solution.py:195
  408.0 4.5 collective-permute-done.26
  412.5 3.4 fusion.43
  415.9 3.5 collective-permute-start.32
  428.5 9.9 %back.7 = f32[576,1152]{1,0:T(8,128)S(1)} custom-call(bf16[576,3456]{1,0:T(8,128)(2,1)} %pad_maximum_fusion.grads, bf16[1152,3456]{1,0:T(8,128)(2,1)} %weight.7), custom_call_target="tpu_custom_call" | custom-call | flops 1048576 | bytes 1048576 | tf_op jit(solution)/shard_map/back/pallas_call | solution.py:164
  439.9 4.1 collective-permute-start.31
  449.4 8.6 %weight_grad.11 = (bf16[2304,1152]{1,0:T(8,128)(2,1)}, bf16[1152,1152]{1,0:T(8,128)(2,1)}, f32[1,1152]{1,0:T(1,128)}) custom-call(s32[1]{0:T(128)} %bitcast.other, bf16[576,2304]{1,0:T(8,128)(2,1)} %pad_maximum_fusion.2.rows, bf16[576,1152]{1,0:T(8,128)(2,1)S(1)} %get-tuple-element.415.grads), custom_call_target="tpu_custom_call" | custom-call | flops 1048576 | bytes 1048576 | tf_op jit(solution)/shard_map/weight_grad/pallas_call | solution.py:195
  471.1 3.9 split.4
  481.1 5.9 collective-permute-start.61
  492.9 18.4 %collective-permute-done.29 = bf16[288,2304]{1,0:T(8,128)(2,1)S(1)} collective-permute-done((bf16[288,2304]{1,0:T(8,128)(2,1)S(1)}, bf16[288,2304]{1,0:T(8,128)(2,1)S(1)}, u32[]{:S(2)}, u32[]{:S(2)}) %collective-permute-start.29) | collective-permute-done | bytes 1327136 | tf_op jit(solution)/shard_map/ppermute | solution.py:335
  514.7 3.7 collective-permute-done.38.refs_3_
  521.0 6.1 %fusion.7 = f32[2,288,2304]{2,1,0:T(8,128)S(1)} fusion(bf16[2,288,1152]{2,1,0:T(8,128)(2,1)S(1)} %pad_maximum_fusion.4, bf16[2304,1152]{1,0:T(8,128)(2,1)} %param.35), kind=kOutput, calls=%fused_computation.17 | convolution fusion | flops 3057647616 | bytes 11943936 | tf_op jit(solution)/shard_map/re,de->rd/dot_general | solution.py:89
  532.3 18.5 %collective-permute-start.60 = (bf16[36,4608]{1,0:T(8,128)(2,1)S(1)}, bf16[36,4608]{1,0:T(8,128)(2,1)S(1)}, u32[]{:S(2)}, u32[]{:S(2)}) collective-permute-start(bf16[36,4608]{1,0:T(8,128)(2,1)S(1)} %get-tuple-element.307), channel_id=1, source_target_pairs={{0,2},{1,3},{2,0},{3,1},{4,6},{5,7},{6,4},{7,5},{8,10},{9,11},{10,... | collective-permute-start | bytes 995336 | tf_op jit(solution)/shard_map/ppermute | solution.py:329
  555.4 3.8 collective-permute-start.58
  559.1 6.4 %collective-permute-done.60 = bf16[36,4608]{1,0:T(8,128)(2,1)S(1)} collective-permute-done((bf16[36,4608]{1,0:T(8,128)(2,1)S(1)}, bf16[36,4608]{1,0:T(8,128)(2,1)S(1)}, u32[]{:S(2)}, u32[]{:S(2)}) %collective-permute-start.60) | collective-permute-done | bytes 331808 | tf_op jit(solution)/shard_map/ppermute | solution.py:329
  565.5 3.1 collective-permute-start.55
  568.6 3.2 collective-permute-start.53
  571.7 3.8 collective-permute-start.54
  577.4 2.8 collective-permute-start.52
  580.1 6.8 %collective-permute-start.51 = (bf16[36,1152]{1,0:T(8,128)(2,1)S(1)}, bf16[36,1152]{1,0:T(8,128)(2,1)S(1)}, u32[]{:S(2)}, u32[]{:S(2)}) collective-permute-start(bf16[36,1152]{1,0:T(8,128)(2,1)S(1)} %get-tuple-element.289), channel_id=1, source_target_pairs={{0,2},{1,3},{2,0},{3,1},{4,6},{5,7},{6,4},{7,5},{8,10},{9,11},{10,... | collective-permute-start | bytes 248840 | tf_op jit(solution)/shard_map/ppermute | solution.py:329
  586.9 3.3 collective-permute-done.54
  591.7 3.8 collective-permute-done.51
  595.5 4.4 collective-permute-start.43
  607.9 3.3 collective-permute-done.44
  (446 shorter events, 180.8 us)
Async XLA Ops:
  21.2 17.8 %collective-permute-start.1 = (bf16[288,1152]{1,0:T(8,128)(2,1)S(1)}, bf16[288,1152]{1,0:T(8,128)(2,1)}, u32[]{:S(2)}, u32[]{:S(2)}) collective-permute-start(bf16[288,1152]{1,0:T(8,128)(2,1)S(1)} %get-tuple-element.169), channel_id=1, source_target_pairs={{0,1},{1,0},{2,5},{3,4},{4,3},{5,2},{6,7},{7,6},{8,9},{9,8},{10,13... | collective-permute-start | bytes 1990664 | tf_op jit(solution)/shard_map/ppermute | solution.py:121
  53.0 39.2 %collective-permute-start.4 = (bf16[576,2304]{1,0:T(8,128)(2,1)}, bf16[576,2304]{1,0:T(8,128)(2,1)}, u32[]{:S(2)}, u32[]{:S(2)}) collective-permute-start(bf16[576,2304]{1,0:T(8,128)(2,1)} %slice.279), channel_id=1, source_target_pairs={{0,4},{1,5},{2,6},{3,7},{4,0},{5,1},{6,2},{7,3},{8,12},{9,13},{10,... | collective-permute-start | bytes 7962632 | tf_op jit(solution)/shard_map/ppermute | solution.py:144
  73.7 18.3 %collective-permute-start.8 = (f32[32,128]{1,0:T(8,128)S(1)}, f32[32,128]{1,0:T(8,128)S(1)}, u32[]{:S(2)}, u32[]{:S(2)}) collective-permute-start(f32[32,128]{1,0:T(8,128)S(1)} %get-tuple-element.454), channel_id=1, source_target_pairs={{0,0},{1,1},{2,4},{3,5},{4,2},{5,3},{6,6},{7,7},{8,8},{9,9},{10,12... | collective-permute-start | bytes 49160 | tf_op jit(solution)/shard_map/ppermute | solution.py:121
  74.4 17.4 %collective-permute-start.9 = (f32[32,128]{1,0:T(8,128)S(1)}, f32[32,128]{1,0:T(8,128)S(1)}, u32[]{:S(2)}, u32[]{:S(2)}) collective-permute-start(f32[32,128]{1,0:T(8,128)S(1)} %get-tuple-element.455), channel_id=1, source_target_pairs={{0,1},{1,0},{2,5},{3,4},{4,3},{5,2},{6,7},{7,6},{8,9},{9,8},{10,13... | collective-permute-start | bytes 49160 | tf_op jit(solution)/shard_map/ppermute | solution.py:121
  79.9 79.0 %collective-permute-start.7 = (bf16[288,2304]{1,0:T(8,128)(2,1)}, bf16[288,2304]{1,0:T(8,128)(2,1)}, u32[]{:S(2)}, u32[]{:S(2)}) collective-permute-start(bf16[288,2304]{1,0:T(8,128)(2,1)} %get-tuple-element.422), channel_id=1, source_target_pairs={{0,1},{1,0},{2,5},{3,4},{4,3},{5,2},{6,7},{7,6},{8,9},{9,8},{10,13... | collective-permute-start | bytes 3981320 | tf_op jit(solution)/shard_map/ppermute | solution.py:121
  80.0 79.0 %collective-permute-start.6 = (bf16[288,2304]{1,0:T(8,128)(2,1)}, bf16[288,2304]{1,0:T(8,128)(2,1)}, u32[]{:S(2)}, u32[]{:S(2)}) collective-permute-start(bf16[288,2304]{1,0:T(8,128)(2,1)} %get-tuple-element.423), channel_id=1, source_target_pairs={{0,0},{1,1},{2,4},{3,5},{4,2},{5,3},{6,6},{7,7},{8,8},{9,9},{10,12... | collective-permute-start | bytes 3981320 | tf_op jit(solution)/shard_map/ppermute | solution.py:121
  188.5 19.1 %collective-permute-start.11 = (bf16[2304,1152]{1,0:T(8,128)(2,1)}, bf16[2304,1152]{1,0:T(8,128)(2,1)}, u32[]{:S(2)}, u32[]{:S(2)}) collective-permute-start(bf16[2304,1152]{1,0:T(8,128)(2,1)} %get-tuple-element.178), channel_id=1, source_target_pairs={{0,4},{4,0},{8,12},{12,8},{16,20},{20,16},{24,28},{28,24},{1,5},{5... | collective-permute-start | bytes 15925256 | tf_op jit(solution)/shard_map/ppermute | solution.py:335
  226.2 37.7 %collective-permute-start.12 = (bf16[576,4608]{1,0:T(8,128)(2,1)}, bf16[576,4608]{1,0:T(8,128)(2,1)}, u32[]{:S(2)}, u32[]{:S(2)}) collective-permute-start(bf16[576,4608]{1,0:T(8,128)(2,1)} %get-tuple-element.185), channel_id=1, source_target_pairs={{0,4},{4,0},{8,12},{12,8},{16,20},{20,16},{24,28},{28,24},{1,5},{5... | collective-permute-start | bytes 15925256 | tf_op jit(solution)/shard_map/ppermute | solution.py:335
  239.4 95.3 %collective-permute-start.20 = (bf16[1152,1152]{1,0:T(8,128)(2,1)}, bf16[1152,1152]{1,0:T(8,128)(2,1)}, u32[]{:S(2)}, u32[]{:S(2)}) collective-permute-start(bf16[1152,1152]{1,0:T(8,128)(2,1)} %fusion.6), channel_id=1, source_target_pairs={{0,8},{4,12},{8,0},{12,4},{16,24},{20,28},{24,16},{28,20},{1,9},{5... | collective-permute-start | bytes 7962632 | tf_op jit(solution)/shard_map/ppermute | solution.py:335
  278.4 54.0 %collective-permute-start.21 = (bf16[576,1152]{1,0:T(8,128)(2,1)}, bf16[576,1152]{1,0:T(8,128)(2,1)}, u32[]{:S(2)}, u32[]{:S(2)}) collective-permute-start(bf16[576,1152]{1,0:T(8,128)(2,1)} %get-tuple-element.198), channel_id=1, source_target_pairs={{0,4},{4,0},{8,12},{12,8},{16,20},{20,16},{24,28},{28,24},{1,5},{5... | collective-permute-start | bytes 3981320 | tf_op jit(solution)/shard_map/ppermute | solution.py:335
  285.6 41.6 %collective-permute-start.17 = (f32[2,4,64,1]{2,1,3,0:T(4,128)}, f32[2,4,64,1]{2,1,3,0:T(4,128)S(1)}, u32[]{:S(2)}, u32[]{:S(2)}) collective-permute-start(f32[2,4,64,1]{2,1,3,0:T(4,128)} %get-tuple-element.446), channel_id=1, source_target_pairs={{0,1},{1,2},{2,3},{4,5},{5,6},{6,7},{8,9},{9,10},{10,11},{12,13},{... | collective-permute-start | bytes 6152 | tf_op jit(solution)/shard_map/ppermute | solution.py:37
  288.1 39.1 %collective-permute-start.18 = (f32[2,4,64,1]{2,1,3,0:T(4,128)}, f32[2,4,64,1]{2,1,3,0:T(4,128)S(1)}, u32[]{:S(2)}, u32[]{:S(2)}) collective-permute-start(f32[2,4,64,1]{2,1,3,0:T(4,128)} %get-tuple-element.447), channel_id=1, source_target_pairs={{1,0},{2,1},{3,2},{5,4},{6,5},{7,6},{9,8},{10,9},{11,10},{13,12},{... | collective-permute-start | bytes 6152 | tf_op jit(solution)/shard_map/ppermute | solution.py:40
  292.2 94.8 %collective-permute-start.19 = (bf16[288,4608]{1,0:T(8,128)(2,1)}, bf16[288,4608]{1,0:T(8,128)(2,1)S(1)}, u32[]{:S(2)}, u32[]{:S(2)}) collective-permute-start(bf16[288,4608]{1,0:T(8,128)(2,1)} %fusion.5), channel_id=1, source_target_pairs={{0,16},{4,20},{8,24},{12,28},{16,0},{20,4},{24,8},{28,12},{1,17},{... | collective-permute-start | bytes 7962632 | tf_op jit(solution)/shard_map/ppermute | solution.py:335
  377.4 13.8 %collective-permute-start.22 = (bf16[576,2304]{1,0:T(8,128)(2,1)}, bf16[576,2304]{1,0:T(8,128)(2,1)S(1)}, u32[]{:S(2)}, u32[]{:S(2)}) collective-permute-start(bf16[576,2304]{1,0:T(8,128)(2,1)} %get-tuple-element.215), channel_id=1, source_target_pairs={{0,4},{1,5},{2,6},{3,7},{4,0},{5,1},{6,2},{7,3},{8,12},{9,13},{10,... | collective-permute-start | bytes 7962632 | tf_op jit(solution)/shard_map/ppermute | solution.py:144
  380.6 31.9 %collective-permute-start.26 = (bf16[576,1152]{1,0:T(8,128)(2,1)}, bf16[576,1152]{1,0:T(8,128)(2,1)}, u32[]{:S(2)}, u32[]{:S(2)}) collective-permute-start(bf16[576,1152]{1,0:T(8,128)(2,1)} %fusion.20), channel_id=1, source_target_pairs={{0,16},{4,20},{8,24},{12,28},{16,0},{20,4},{24,8},{28,12},{1,17},{... | collective-permute-start | bytes 3981320 | tf_op jit(solution)/shard_map/ppermute | solution.py:335
  386.8 32.6 %collective-permute-start.25 = (bf16[576,1152]{1,0:T(8,128)(2,1)}, bf16[576,1152]{1,0:T(8,128)(2,1)}, u32[]{:S(2)}, u32[]{:S(2)}) collective-permute-start(bf16[576,1152]{1,0:T(8,128)(2,1)} %get-tuple-element.211), channel_id=1, source_target_pairs={{0,4},{4,0},{8,12},{12,8},{16,20},{20,16},{24,28},{28,24},{1,5},{5... | collective-permute-start | bytes 3981320 | tf_op jit(solution)/shard_map/ppermute | solution.py:335
  402.2 37.6 %collective-permute-start.23 = (bf16[576,2304]{1,0:T(8,128)(2,1)}, bf16[576,2304]{1,0:T(8,128)(2,1)S(1)}, u32[]{:S(2)}, u32[]{:S(2)}) collective-permute-start(bf16[576,2304]{1,0:T(8,128)(2,1)} %get-tuple-element.218), channel_id=1, source_target_pairs={{0,4},{4,0},{8,12},{12,8},{16,20},{20,16},{24,28},{28,24},{1,5},{5... | collective-permute-start | bytes 7962632 | tf_op jit(solution)/shard_map/ppermute | solution.py:335
  404.8 18.0 %collective-permute-start.24 = (bf16[288,1152]{1,0:T(8,128)(2,1)}, bf16[288,1152]{1,0:T(8,128)(2,1)S(1)}, u32[]{:S(2)}, u32[]{:S(2)}) collective-permute-start(bf16[288,1152]{1,0:T(8,128)(2,1)} %fusion.27), channel_id=1, source_target_pairs={{0,8},{4,12},{8,0},{12,4},{16,24},{20,28},{24,16},{28,20},{1,9},{5... | collective-permute-start | bytes 1990664 | tf_op jit(solution)/shard_map/ppermute | solution.py:335
  406.5 64.0 %collective-permute-start.36 = (bf16[144,4608]{1,0:T(8,128)(2,1)}, bf16[144,4608]{1,0:T(8,128)(2,1)}, u32[]{:S(2)}, u32[]{:S(2)}) collective-permute-start(bf16[144,4608]{1,0:T(8,128)(2,1)} %fusion.19), channel_id=1, source_target_pairs={{0,8},{4,12},{8,0},{12,4},{16,24},{20,28},{24,16},{28,20},{1,9},{5... | collective-permute-start | bytes 3981320 | tf_op jit(solution)/shard_map/ppermute | solution.py:335
  415.9 51.9 %collective-permute-start.32 = (bf16[144,1152]{1,0:T(8,128)(2,1)}, bf16[144,1152]{1,0:T(8,128)(2,1)}, u32[]{:S(2)}, u32[]{:S(2)}) collective-permute-start(bf16[144,1152]{1,0:T(8,128)(2,1)} %get-tuple-element.223), channel_id=1, source_target_pairs={{0,3},{1,0},{2,1},{3,2},{4,7},{5,4},{6,5},{7,6},{8,11},{9,8},{10,9... | collective-permute-start | bytes 995336 | tf_op jit(solution)/shard_map/ppermute | solution.py:329
  419.4 38.6 %collective-permute-start.30 = (bf16[144,1152]{1,0:T(8,128)(2,1)S(1)}, bf16[144,1152]{1,0:T(8,128)(2,1)S(1)}, u32[]{:S(2)}, u32[]{:S(2)}) collective-permute-start(bf16[144,1152]{1,0:T(8,128)(2,1)S(1)} %get-tuple-element.238), channel_id=1, source_target_pairs={{0,1},{1,2},{2,3},{3,0},{4,5},{5,6},{6,7},{7,4},{8,9},{9,10},{10,1... | collective-permute-start | bytes 995336 | tf_op jit(solution)/shard_map/ppermute | solution.py:329
  422.8 52.3 %collective-permute-start.35 = (bf16[288,1152]{1,0:T(8,128)(2,1)}, bf16[288,1152]{1,0:T(8,128)(2,1)}, u32[]{:S(2)}, u32[]{:S(2)}) collective-permute-start(bf16[288,1152]{1,0:T(8,128)(2,1)} %fusion.26), channel_id=1, source_target_pairs={{0,16},{4,20},{8,24},{12,28},{16,0},{20,4},{24,8},{28,12},{1,17},{... | collective-permute-start | bytes 1990664 | tf_op jit(solution)/shard_map/ppermute | solution.py:335
  439.9 25.9 %collective-permute-start.31 = (bf16[144,1152]{1,0:T(8,128)(2,1)}, bf16[144,1152]{1,0:T(8,128)(2,1)}, u32[]{:S(2)}, u32[]{:S(2)}) collective-permute-start(bf16[144,1152]{1,0:T(8,128)(2,1)} %get-tuple-element.239), channel_id=1, source_target_pairs={{0,2},{1,3},{2,0},{3,1},{4,6},{5,7},{6,4},{7,5},{8,10},{9,11},{10,... | collective-permute-start | bytes 995336 | tf_op jit(solution)/shard_map/ppermute | solution.py:329
  458.0 29.8 %collective-permute-start.34 = (bf16[1152,1152]{1,0:T(8,128)(2,1)}, bf16[1152,1152]{1,0:T(8,128)(2,1)}, u32[]{:S(2)}, u32[]{:S(2)}) collective-permute-start(bf16[1152,1152]{1,0:T(8,128)(2,1)} %get-tuple-element.237), channel_id=1, source_target_pairs={{0,4},{4,0},{8,12},{12,8},{16,20},{20,16},{24,28},{28,24},{1,5},{5... | collective-permute-start | bytes 7962632 | tf_op jit(solution)/shard_map/ppermute | solution.py:335
  465.8 15.4 %collective-permute-start.27 = (bf16[288,1152]{1,0:T(8,128)(2,1)}, bf16[288,1152]{1,0:T(8,128)(2,1)S(1)}, u32[]{:S(2)}, u32[]{:S(2)}) collective-permute-start(bf16[288,1152]{1,0:T(8,128)(2,1)} %get-tuple-element.429), channel_id=1, source_target_pairs={{0,0},{1,1},{4,2},{5,3},{2,4},{3,5},{6,6},{7,7},{8,8},{9,9},{12,10... | collective-permute-start | bytes 1990664 | tf_op jit(solution)/shard_map/ppermute | solution.py:128
  467.8 19.2 %collective-permute-start.28 = (bf16[288,1152]{1,0:T(8,128)(2,1)}, bf16[288,1152]{1,0:T(8,128)(2,1)S(1)}, u32[]{:S(2)}, u32[]{:S(2)}) collective-permute-start(bf16[288,1152]{1,0:T(8,128)(2,1)} %get-tuple-element.430), channel_id=1, source_target_pairs={{1,0},{0,1},{5,2},{4,3},{3,4},{2,5},{7,6},{6,7},{9,8},{8,9},{13,10... | collective-permute-start | bytes 1990664 | tf_op jit(solution)/shard_map/ppermute | solution.py:128
  470.6 41.9 %collective-permute-start.39 = (bf16[144,1152]{1,0:T(8,128)(2,1)S(1)}, bf16[144,1152]{1,0:T(8,128)(2,1)S(1)}, u32[]{:S(2)}, u32[]{:S(2)}) collective-permute-start(bf16[144,1152]{1,0:T(8,128)(2,1)S(1)} %copy-done.35), channel_id=1, source_target_pairs={{0,16},{4,20},{8,24},{12,28},{16,0},{20,4},{24,8},{28,12},{1,17},{... | collective-permute-start | bytes 995336 | tf_op jit(solution)/shard_map/ppermute | solution.py:335
  475.1 17.4 %collective-permute-start.33 = (f32[256,128]{1,0:T(8,128)S(1)}, f32[256,128]{1,0:T(8,128)S(1)}, u32[]{:S(2)}, u32[]{:S(2)}) collective-permute-start(f32[256,128]{1,0:T(8,128)S(1)} %bitcast.565), channel_id=1, source_target_pairs={{0,4},{4,0},{8,12},{12,8},{16,20},{20,16},{24,28},{28,24},{1,5},{5... | collective-permute-start | bytes 393224 | tf_op jit(solution)/shard_map/ppermute | solution.py:335
  481.1 84.4 %collective-permute-start.61 = (bf16[36,4608]{1,0:T(8,128)(2,1)S(1)}, bf16[36,4608]{1,0:T(8,128)(2,1)}, u32[]{:S(2)}, u32[]{:S(2)}) collective-permute-start(bf16[36,4608]{1,0:T(8,128)(2,1)S(1)} %get-tuple-element.250), channel_id=1, source_target_pairs={{0,3},{1,0},{2,1},{3,2},{4,7},{5,4},{6,5},{7,6},{8,11},{9,8},{10,9... | collective-permute-start | bytes 995336 | tf_op jit(solution)/shard_map/ppermute | solution.py:329
  487.1 24.3 %collective-permute-start.29 = (bf16[288,2304]{1,0:T(8,128)(2,1)S(1)}, bf16[288,2304]{1,0:T(8,128)(2,1)S(1)}, u32[]{:S(2)}, u32[]{:S(2)}) collective-permute-start(bf16[288,2304]{1,0:T(8,128)(2,1)S(1)} %copy-done.32), channel_id=1, source_target_pairs={{0,8},{4,12},{8,0},{12,4},{16,24},{20,28},{24,16},{28,20},{1,9},{5... | collective-permute-start | bytes 3981320 | tf_op jit(solution)/shard_map/ppermute | solution.py:335
  487.9 30.6 %collective-permute-start.38 = (bf16[144,1152]{1,0:T(8,128)(2,1)}, bf16[144,1152]{1,0:T(8,128)(2,1)S(1)}, u32[]{:S(2)}, u32[]{:S(2)}) collective-permute-start(bf16[144,1152]{1,0:T(8,128)(2,1)} %fusion.38), channel_id=1, source_target_pairs={{0,8},{4,12},{8,0},{12,4},{16,24},{20,28},{24,16},{28,20},{1,9},{5... | collective-permute-start | bytes 995336 | tf_op jit(solution)/shard_map/ppermute | solution.py:335
  492.5 34.7 %collective-permute-start.37 = (bf16[576,1152]{1,0:T(8,128)(2,1)}, bf16[576,1152]{1,0:T(8,128)(2,1)S(1)}, u32[]{:S(2)}, u32[]{:S(2)}) collective-permute-start(bf16[576,1152]{1,0:T(8,128)(2,1)} %fusion.17), channel_id=1, source_target_pairs={{0,16},{4,20},{8,24},{12,28},{16,0},{20,4},{24,8},{28,12},{1,17},{... | collective-permute-start | bytes 3981320 | tf_op jit(solution)/shard_map/ppermute | solution.py:335
  511.4 44.0 %collective-permute-start.59 = (bf16[36,4608]{1,0:T(8,128)(2,1)S(1)}, bf16[36,4608]{1,0:T(8,128)(2,1)}, u32[]{:S(2)}, u32[]{:S(2)}) collective-permute-start(bf16[36,4608]{1,0:T(8,128)(2,1)S(1)} %get-tuple-element.306), channel_id=1, source_target_pairs={{0,1},{1,2},{2,3},{3,0},{4,5},{5,6},{6,7},{7,4},{8,9},{9,10},{10,1... | collective-permute-start | bytes 995336 | tf_op jit(solution)/shard_map/ppermute | solution.py:329
  512.5 19.8 %collective-permute-start.42 = (f32[128,128]{1,0:T(8,128)S(1)}, f32[128,128]{1,0:T(8,128)S(1)}, u32[]{:S(2)}, u32[]{:S(2)}) collective-permute-start(f32[128,128]{1,0:T(8,128)S(1)} %bitcast_add_fusion), channel_id=1, source_target_pairs={{0,16},{4,20},{8,24},{12,28},{16,0},{20,4},{24,8},{28,12},{1,17},{... | collective-permute-start | bytes 196616 | tf_op jit(solution)/shard_map/ppermute | solution.py:335
  518.5 32.3 %collective-permute-start.41 = (bf16[144,2304]{1,0:T(8,128)(2,1)}, bf16[144,2304]{1,0:T(8,128)(2,1)S(1)}, u32[]{:S(2)}, u32[]{:S(2)}) collective-permute-start(bf16[144,2304]{1,0:T(8,128)(2,1)} %fusion.25), channel_id=1, source_target_pairs={{0,16},{4,20},{8,24},{12,28},{16,0},{20,4},{24,8},{28,12},{1,17},{... | collective-permute-start | bytes 1990664 | tf_op jit(solution)/shard_map/ppermute | solution.py:335
  529.3 21.6 %collective-permute-start.40 = (bf16[288,1152]{1,0:T(8,128)(2,1)S(1)}, bf16[288,1152]{1,0:T(8,128)(2,1)S(1)}, u32[]{:S(2)}, u32[]{:S(2)}) collective-permute-start(bf16[288,1152]{1,0:T(8,128)(2,1)S(1)} %fusion.24), channel_id=1, source_target_pairs={{0,8},{4,12},{8,0},{12,4},{16,24},{20,28},{24,16},{28,20},{1,9},{5... | collective-permute-start | bytes 1990664 | tf_op jit(solution)/shard_map/ppermute | solution.py:335
  532.3 33.2 %collective-permute-start.60 = (bf16[36,4608]{1,0:T(8,128)(2,1)S(1)}, bf16[36,4608]{1,0:T(8,128)(2,1)S(1)}, u32[]{:S(2)}, u32[]{:S(2)}) collective-permute-start(bf16[36,4608]{1,0:T(8,128)(2,1)S(1)} %get-tuple-element.307), channel_id=1, source_target_pairs={{0,2},{1,3},{2,0},{3,1},{4,6},{5,7},{6,4},{7,5},{8,10},{9,11},{10,... | collective-permute-start | bytes 995336 | tf_op jit(solution)/shard_map/ppermute | solution.py:329
  550.8 17.8 %collective-permute-start.56 = (bf16[36,1152]{1,0:T(8,128)(2,1)S(1)}, bf16[36,1152]{1,0:T(8,128)(2,1)S(1)}, u32[]{:S(2)}, u32[]{:S(2)}) collective-permute-start(bf16[36,1152]{1,0:T(8,128)(2,1)S(1)} %get-tuple-element.300), channel_id=1, source_target_pairs={{0,1},{1,2},{2,3},{3,0},{4,5},{5,6},{6,7},{7,4},{8,9},{9,10},{10,1... | collective-permute-start | bytes 248840 | tf_op jit(solution)/shard_map/ppermute | solution.py:329
  550.8 20.9 %collective-permute-start.46 = (f32[64,128]{1,0:T(8,128)S(1)}, f32[64,128]{1,0:T(8,128)S(1)}, u32[]{:S(2)}, u32[]{:S(2)}) collective-permute-start(f32[64,128]{1,0:T(8,128)S(1)} %bitcast_add_fusion.1), channel_id=1, source_target_pairs={{0,8},{4,12},{8,0},{12,4},{16,24},{20,28},{24,16},{28,20},{1,9},{5... | collective-permute-start | bytes 98312 | tf_op jit(solution)/shard_map/ppermute | solution.py:335
  555.4 24.8 %collective-permute-start.58 = (bf16[36,1152]{1,0:T(8,128)(2,1)S(1)}, bf16[36,1152]{1,0:T(8,128)(2,1)S(1)}, u32[]{:S(2)}, u32[]{:S(2)}) collective-permute-start(bf16[36,1152]{1,0:T(8,128)(2,1)S(1)} %get-tuple-element.260), channel_id=1, source_target_pairs={{0,3},{1,0},{2,1},{3,2},{4,7},{5,4},{6,5},{7,6},{8,11},{9,8},{10,9... | collective-permute-start | bytes 248840 | tf_op jit(solution)/shard_map/ppermute | solution.py:329
  565.5 11.8 %collective-permute-start.57 = (bf16[36,1152]{1,0:T(8,128)(2,1)S(1)}, bf16[36,1152]{1,0:T(8,128)(2,1)S(1)}, u32[]{:S(2)}, u32[]{:S(2)}) collective-permute-start(bf16[36,1152]{1,0:T(8,128)(2,1)S(1)} %get-tuple-element.301), channel_id=1, source_target_pairs={{0,2},{1,3},{2,0},{3,1},{4,6},{5,7},{6,4},{7,5},{8,10},{9,11},{10,... | collective-permute-start | bytes 248840 | tf_op jit(solution)/shard_map/ppermute | solution.py:329
  565.5 26.1 %collective-permute-start.55 = (bf16[36,2304]{1,0:T(8,128)(2,1)S(1)}, bf16[36,2304]{1,0:T(8,128)(2,1)S(1)}, u32[]{:S(2)}, u32[]{:S(2)}) collective-permute-start(bf16[36,2304]{1,0:T(8,128)(2,1)S(1)} %get-tuple-element.272), channel_id=1, source_target_pairs={{0,3},{1,0},{2,1},{3,2},{4,7},{5,4},{6,5},{7,6},{8,11},{9,8},{10,9... | collective-permute-start | bytes 497672 | tf_op jit(solution)/shard_map/ppermute | solution.py:329
  571.7 18.5 %collective-permute-start.54 = (bf16[36,2304]{1,0:T(8,128)(2,1)S(1)}, bf16[36,2304]{1,0:T(8,128)(2,1)S(1)}, u32[]{:S(2)}, u32[]{:S(2)}) collective-permute-start(bf16[36,2304]{1,0:T(8,128)(2,1)S(1)} %get-tuple-element.295), channel_id=1, source_target_pairs={{0,2},{1,3},{2,0},{3,1},{4,6},{5,7},{6,4},{7,5},{8,10},{9,11},{10,... | collective-permute-start | bytes 497672 | tf_op jit(solution)/shard_map/ppermute | solution.py:329
  577.4 18.1 %collective-permute-start.52 = (bf16[36,1152]{1,0:T(8,128)(2,1)S(1)}, bf16[36,1152]{1,0:T(8,128)(2,1)S(1)}, u32[]{:S(2)}, u32[]{:S(2)}) collective-permute-start(bf16[36,1152]{1,0:T(8,128)(2,1)S(1)} %get-tuple-element.265), channel_id=1, source_target_pairs={{0,3},{1,0},{2,1},{3,2},{4,7},{5,4},{6,5},{7,6},{8,11},{9,8},{10,9... | collective-permute-start | bytes 248840 | tf_op jit(solution)/shard_map/ppermute | solution.py:329
  580.1 15.3 %collective-permute-start.51 = (bf16[36,1152]{1,0:T(8,128)(2,1)S(1)}, bf16[36,1152]{1,0:T(8,128)(2,1)S(1)}, u32[]{:S(2)}, u32[]{:S(2)}) collective-permute-start(bf16[36,1152]{1,0:T(8,128)(2,1)S(1)} %get-tuple-element.289), channel_id=1, source_target_pairs={{0,2},{1,3},{2,0},{3,1},{4,6},{5,7},{6,4},{7,5},{8,10},{9,11},{10,... | collective-permute-start | bytes 248840 | tf_op jit(solution)/shard_map/ppermute | solution.py:329
  590.2 13.5 %collective-permute-start.49 = (f32[16,128]{1,0:T(8,128)S(1)}, f32[16,128]{1,0:T(8,128)S(1)}, u32[]{:S(2)}, u32[]{:S(2)}) collective-permute-start(f32[16,128]{1,0:T(8,128)S(1)} %get-tuple-element.278), channel_id=1, source_target_pairs={{0,3},{1,0},{2,1},{3,2},{4,7},{5,4},{6,5},{7,6},{8,11},{9,8},{10,9... | collective-permute-start | bytes 24584 | tf_op jit(solution)/shard_map/ppermute | solution.py:329
  591.7 19.5 %collective-permute-start.45 = (bf16[72,1152]{1,0:T(8,128)(2,1)S(1)}, bf16[72,1152]{1,0:T(8,128)(2,1)S(1)}, u32[]{:S(2)}, u32[]{:S(2)}) collective-permute-start(bf16[72,1152]{1,0:T(8,128)(2,1)S(1)} %get-tuple-element.276), channel_id=1, source_target_pairs={{0,3},{1,0},{2,1},{3,2},{4,7},{5,4},{6,5},{7,6},{8,11},{9,8},{10,9... | collective-permute-start | bytes 497672 | tf_op jit(solution)/shard_map/ppermute | solution.py:329
  595.5 12.4 %collective-permute-start.43 = (bf16[72,1152]{1,0:T(8,128)(2,1)S(1)}, bf16[72,1152]{1,0:T(8,128)(2,1)S(1)}, u32[]{:S(2)}, u32[]{:S(2)}) collective-permute-start(bf16[72,1152]{1,0:T(8,128)(2,1)S(1)} %get-tuple-element.274), channel_id=1, source_target_pairs={{0,1},{1,2},{2,3},{3,0},{4,5},{5,6},{6,7},{7,4},{8,9},{9,10},{10,1... | collective-permute-start | bytes 497672 | tf_op jit(solution)/shard_map/ppermute | solution.py:329
  (86 other events, 1102.9 us)

commit v5 on v4

--- a/solution.py
+++ b/solution.py
@@ -70,13 +70,12 @@
 
 
 def gelu_and_slope(values):
-    u = jnp.abs(values) * math.sqrt(0.5)
-    t = 1.0 / (1.0 + 0.5 * u)
+    t = 1.0 / (1.0 + (0.5 * math.sqrt(0.5)) * jnp.abs(values))
     poly = jnp.full_like(t, ERFC[-1])
-    for coefficient in reversed(ERFC[:-1]):
+    for coefficient in reversed((ERFC[0] + math.log(0.5),) + ERFC[1:-1]):
         poly = poly * t + coefficient
-    bell = jnp.exp(-u * u)
-    tail = 0.5 * t * bell * jnp.exp(poly)
+    bell = jnp.exp(-0.5 * (values * values))
+    tail = t * bell * jnp.exp(poly)
     below = jnp.where(values < 0.0, tail, 1.0 - tail)
     return values * below, below + values * bell * (1.0 / math.sqrt(2.0 * math.pi))
 
@@ -180,8 +179,13 @@
 def weight_grad_kernel(pairs, block, other, rows, grads, full, send, sums):
     full[...] = dot(rows[...], grads[...], TN).astype(full.dtype)
     for pair in range(pairs):
-        start = pl.multiple_of((2 * pair + other[0]) * block, 16)
-        send[pair * block : (pair + 1) * block, :] = full[pl.ds(start, block), :]
+        rows_out = slice(pair * block, (pair + 1) * block)
+        if block % 16 == 0:
+            start = pl.multiple_of((2 * pair + other[0]) * block, 16)
+            send[rows_out, :] = full[pl.ds(start, block), :]
+            continue
+        low, high = (full[(2 * pair + k) * block : (2 * pair + k + 1) * block, :] for k in range(2))
+        send[rows_out, :] = jnp.where(other[0] == 0, low.astype(F32), high.astype(F32)).astype(send.dtype)
     sums[...] = jnp.sum(grads[...].astype(F32), axis=0, keepdims=True)
 
 

time: 624 us -> 623 us (level)
  no operation moved by 1% of the time
where the time goes in v5:
time: 623 us; the launch traced here: 613 us
  Pallas kernels  210 us (34%)
  starting transfers between devices  138 us (22%)
  matrix products  72.1 us (12%)
  other arithmetic  69.1 us (11%)
  local copies, waits for them, and re-layouts  65.3 us (10%)
  waiting for transfers between devices  55.6 us (9%)
    pallas_call x2, Pallas kernels, attend_back(): pl.pallas_call(partial(attend_back_kernel, holders, width, keys // 2, fir...  70.2 us
    ppermute x21, starting transfers between devices, send(): lax.ppermute(value, 'gy', [(i, (i + step) % self.gy) for i in range(self....  61.1 us
    pallas_call x6, Pallas kernels, weight_grad(): pl.pallas_call(partial(weight_grad_kernel, tall // (2 * block), block), o...  54.4 us
    dot_general x6, matrix products, project(): return jnp.einsum('rd,de->re', rows, weight, preferred_element_type=F32)  50.1 us
    pallas_call x1, Pallas kernels, attend(): pl.pallas_call(partial(attend_kernel, holders, width, 288), out_shape=(ja...  38.5 us
    pallas_call x4, Pallas kernels, back(): pl.pallas_call(back_kernel, out_shape=jax.ShapeDtypeStruct((count, height...  37.6 us
    ppermute x21, waiting for transfers between devices, send(): got = lax.ppermute(sends[0], 'gx', pairs)  27.9 us
    ppermute x8, starting transfers between devices, send(): lax.ppermute(sends[t], ('gx', 'gy'), self.perms[t])  27.3 us
  transfers between devices with their start and end apart: 62, of which 11 were waited for; matrix products, arithmetic and copies ran while one was open for 25% of the time, Pallas kernels for 30%

profile of v5, /device:TPU:0, one launch (start us, length us, event | category | flops | bytes accessed | tf_op | source)
XLA Modules:
  0.0 612.7 jit_solution(6751288127115684499)
XLA Ops:
  5.4 7.2 %fusion.12 = bf16[576,1152]{1,0:T(8,128)(2,1)S(1)} fusion(bf16[576,2304]{1,0:T(8,128)(2,1)S(1)} %bitcast.542, bf16[2304,1152]{1,0:T(8,128)(2,1)} %param.35, f32[1152]{0:T(1024)S(1)} %copy-done.63), kind=kOutput, calls=%fused_computation.30 | convolution fusion | flops 3058974720 | bytes 9294336 | tf_op jit(solution)/shard_map/rd,de->re/dot_general | solution.py:84
  13.5 4.9 collective-permute-start.2
  29.9 9.2 %collective-permute-done.1 = bf16[288,1152]{1,0:T(8,128)(2,1)} collective-permute-done((bf16[288,1152]{1,0:T(8,128)(2,1)S(1)}, bf16[288,1152]{1,0:T(8,128)(2,1)}, u32[]{:S(2)}, u32[]{:S(2)}) %collective-permute-start.1) | collective-permute-done | bytes 663584 | tf_op jit(solution)/shard_map/ppermute | solution.py:120
  41.9 9.4 %convolution_convert_fusion.refs_0_ = bf16[576,3456]{1,0:T(8,128)(2,1)S(1)} fusion(bf16[576,1152]{1,0:T(8,128)(2,1)S(1)} %add_convert_fusion.3.rows, bf16[1152,3456]{1,0:T(8,128)(2,1)} %weight.7), kind=kOutput, calls=%fused_computation.4 | convolution fusion | flops 4588462080 | bytes 13271040 | tf_op jit(solution)/shard_map/rd,de->re/dot_general | solution.py:84
  53.1 9.0 %collective-permute-start.4 = (bf16[576,2304]{1,0:T(8,128)(2,1)}, bf16[576,2304]{1,0:T(8,128)(2,1)}, u32[]{:S(2)}, u32[]{:S(2)}) collective-permute-start(bf16[576,2304]{1,0:T(8,128)(2,1)} %slice.279), channel_id=1, source_target_pairs={{0,4},{1,5},{2,6},{3,7},{4,0},{5,1},{6,2},{7,3},{8,12},{9,13},{10,... | collective-permute-start | bytes 7962632 | tf_op jit(solution)/shard_map/ppermute | solution.py:143
  62.9 7.8 %collective-permute-start.10 = (f32[21,1152]{1,0:T(8,128)S(1)}, f32[21,1152]{1,0:T(8,128)S(1)}, u32[]{:S(2)}, u32[]{:S(2)}) collective-permute-start(f32[21,1152]{1,0:T(8,128)S(1)} %get-tuple-element.438), channel_id=1, source_target_pairs={{0,1},{1,0},{2,5},{3,4},{4,3},{5,2},{6,7},{7,6},{8,9},{9,8},{10,13... | collective-permute-start | bytes 290312 | tf_op jit(solution)/shard_map/ppermute | solution.py:120
  76.5 3.4 dynamic-slice_bitcast_fusion
  80.0 11.9 %collective-permute-start.6 = (bf16[288,2304]{1,0:T(8,128)(2,1)}, bf16[288,2304]{1,0:T(8,128)(2,1)}, u32[]{:S(2)}, u32[]{:S(2)}) collective-permute-start(bf16[288,2304]{1,0:T(8,128)(2,1)} %get-tuple-element.423), channel_id=1, source_target_pairs={{0,0},{1,1},{2,4},{3,5},{4,2},{5,3},{6,6},{7,7},{8,8},{9,9},{10,12... | collective-permute-start | bytes 3981320 | tf_op jit(solution)/shard_map/ppermute | solution.py:120
  93.3 38.5 %attend.1 = (bf16[576,1152]{1,0:T(8,128)(2,1)}, f32[576,128]{1,0:T(8,128)}) custom-call(bf16[576,3456]{1,0:T(8,128)(2,1)} %copy-done.16, bf16[576,2304]{1,0:T(8,128)(2,1)} %collective-permute-done.4.refs_1_, f32[1152,128]{1,0:T(8,128)} %broadcast_in_dim.37.refs_2_), custom_call_target="tpu_custom_call" | custom-call | flops 1048576 | bytes 1048576 | tf_op jit(solution)/shard_map/attend/pallas_call | solution.py:430
  131.8 3.6 fusion.192
  136.7 21.4 %add_convert_fusion = (bf16[576,4608]{1,0:T(8,128)(2,1)}, bf16[576,4608]{1,0:T(8,128)(2,1)S(1)}) fusion(f32[4608]{0:T(1024)S(1)} %copy-done.62, bf16[576,1152]{1,0:T(8,128)(2,1)S(1)} %add_convert_fusion.2.rows, bf16[1152,4608]{1,0:T(8,128)(2,1)} %weight.5), kind=kOutput, calls=%fused_computation.1 | convolution fusion | flops 6210846720 | bytes 22579200 | tf_op jit(solution)/shard_map/rd,de->re/dot_general | solution.py:84
  158.2 8.1 %fusion.193 = (bf16[576,1152]{1,0:T(8,128)(2,1)}, f32[576,1152]{1,0:T(8,128)S(1)}) fusion(f32[1152]{0:T(1024)S(1)} %copy-done.65, f32[576,1152]{1,0:T(8,128)S(1)} %get-tuple-element.472, bf16[576,4608]{1,0:T(8,128)(2,1)S(1)} %get-tuple-element.174.rows, bf16[4608,1152]{1,0:T(8,128)(2,1)S(1)} %bitcast.541), kind=kOutput, calls=%fused_computation.386 | convolution fusion | flops 6117285888 | bytes 22565376 | tf_op jit(solution)/shard_map/rd,de->re/dot_general | solution.py:84
  173.6 14.1 %weight_grad.6 = (bf16[4608,1152]{1,0:T(8,128)(2,1)}, bf16[2304,1152]{1,0:T(8,128)(2,1)}, f32[1,1152]{1,0:T(1,128)}) custom-call(s32[1]{0:T(128)} %bitcast.other, bf16[576,4608]{1,0:T(8,128)(2,1)} %copy-done.29, bf16[576,1152]{1,0:T(8,128)(2,1)S(1)} %fusion.22.grads), custom_call_target="tpu_custom_call" | custom-call | flops 1048576 | bytes 1048576 | tf_op jit(solution)/shard_map/weight_grad/pallas_call | solution.py:199
  192.3 12.6 %back.4.grads = bf16[576,4608]{1,0:T(8,128)(2,1)} custom-call(bf16[576,1152]{1,0:T(8,128)(2,1)S(1)} %fusion.22.grads, bf16[4608,1152]{1,0:T(8,128)(2,1)} %weight.4, bf16[576,4608]{1,0:T(8,128)(2,1)} %get-tuple-element.181.refs_0_), custom_call_target="tpu_custom_call" | custom-call | flops 1048576 | bytes 1048576 | tf_op jit(solution)/shard_map/back/pallas_call | solution.py:163
  211.5 14.0 %weight_grad.7 = (bf16[1152,4608]{1,0:T(8,128)(2,1)}, bf16[576,4608]{1,0:T(8,128)(2,1)}, f32[1,4608]{1,0:T(1,128)S(1)}) custom-call(s32[1]{0:T(128)} %bitcast.other, bf16[576,1152]{1,0:T(8,128)(2,1)S(1)} %add_convert_fusion.2.rows, bf16[576,4608]{1,0:T(8,128)(2,1)} %back.4.grads), custom_call_target="tpu_custom_call" | custom-call | flops 1048576 | bytes 1048576 | tf_op jit(solution)/shard_map/weight_grad/pallas_call | solution.py:199
  231.7 3.4 pad_maximum_fusion.2.rows
  240.9 13.0 %back.5 = f32[576,1152]{1,0:T(8,128)S(1)} custom-call(bf16[576,4608]{1,0:T(8,128)(2,1)} %back.4.grads, bf16[1152,4608]{1,0:T(8,128)(2,1)} %weight.5), custom_call_target="tpu_custom_call" | custom-call | flops 1048576 | bytes 1048576 | tf_op jit(solution)/shard_map/back/pallas_call | solution.py:163
  267.8 4.4 weight_grad.8
  277.9 6.6 %collective-permute-start.21 = (bf16[576,1152]{1,0:T(8,128)(2,1)}, bf16[576,1152]{1,0:T(8,128)(2,1)}, u32[]{:S(2)}, u32[]{:S(2)}) collective-permute-start(bf16[576,1152]{1,0:T(8,128)(2,1)} %get-tuple-element.198), channel_id=1, source_target_pairs={{0,4},{4,0},{8,12},{12,8},{16,20},{20,16},{24,28},{28,24},{1,5},{5... | collective-permute-start | bytes 3981320 | tf_op jit(solution)/shard_map/ppermute | solution.py:339
  295.5 31.1 %attend_back.2 = (bf16[8,576,128]{2,1,0:T(8,128)(2,1)}, bf16[2,8,1152,128]{3,2,1,0:T(8,128)(2,1)}) custom-call(bf16[576,3456]{1,0:T(8,128)(2,1)} %copy-done.16, bf16[576,2304]{1,0:T(8,128)(2,1)} %collective-permute-done.4.refs_1_, f32[1152,128]{1,0:T(8,128)} %broadcast_in_dim.37.refs_2_, bf16[576,1152]{1,0:T(8,128)(2,1)} %get-tuple-element.172.rows.refs_3_, ...), custom_call_target="tpu_custom_call" | custom-call | flops 1048576 | bytes 1048576 | tf_op jit(solution)/shard_map/attend_back/pallas_call | solution.py:528
  334.0 3.7 fusion.19
  337.7 39.2 %attend_back.3 = (bf16[576,1152]{1,0:T(8,128)(2,1)}, bf16[576,2304]{1,0:T(8,128)(2,1)}, bf16[576,2304]{1,0:T(8,128)(2,1)}) custom-call(bf16[576,3456]{1,0:T(8,128)(2,1)} %copy-done.16, bf16[576,2304]{1,0:T(8,128)(2,1)} %collective-permute-done.4.refs_1_, f32[1152,128]{1,0:T(8,128)} %broadcast_in_dim.37.refs_2_, ...), custom_call_target="tpu_custom_call" | custom-call | flops 1048576 | bytes 1048576 | tf_op jit(solution)/shard_map/attend_back/pallas_call | solution.py:528
  381.8 4.4 weight_grad.9
  386.4 4.3 fusion.18
  392.9 8.8 %weight_grad.10 = (bf16[1152,2304]{1,0:T(8,128)(2,1)}, bf16[576,2304]{1,0:T(8,128)(2,1)}, f32[1,2304]{1,0:T(1,128)}) custom-call(s32[1]{0:T(128)} %bitcast.other, bf16[576,1152]{1,0:T(8,128)(2,1)S(1)} %copy-done.3, bf16[576,2304]{1,0:T(8,128)(2,1)} %add_convert_fusion.1.grads), custom_call_target="tpu_custom_call" | custom-call | flops 1048576 | bytes 1048576 | tf_op jit(solution)/shard_map/weight_grad/pallas_call | solution.py:199
  407.4 4.5 collective-permute-done.26
  411.9 3.4 fusion.42
  415.4 3.5 collective-permute-start.32
  427.9 9.9 %back.7 = f32[576,1152]{1,0:T(8,128)S(1)} custom-call(bf16[576,3456]{1,0:T(8,128)(2,1)} %pad_maximum_fusion.grads, bf16[1152,3456]{1,0:T(8,128)(2,1)} %weight.7), custom_call_target="tpu_custom_call" | custom-call | flops 1048576 | bytes 1048576 | tf_op jit(solution)/shard_map/back/pallas_call | solution.py:163
  439.3 4.1 collective-permute-start.31
  448.8 8.6 %weight_grad.11 = (bf16[2304,1152]{1,0:T(8,128)(2,1)}, bf16[1152,1152]{1,0:T(8,128)(2,1)}, f32[1,1152]{1,0:T(1,128)}) custom-call(s32[1]{0:T(128)} %bitcast.other, bf16[576,2304]{1,0:T(8,128)(2,1)} %pad_maximum_fusion.2.rows, bf16[576,1152]{1,0:T(8,128)(2,1)S(1)} %get-tuple-element.415.grads), custom_call_target="tpu_custom_call" | custom-call | flops 1048576 | bytes 1048576 | tf_op jit(solution)/shard_map/weight_grad/pallas_call | solution.py:199
  470.5 3.9 split.4
  480.5 5.9 collective-permute-start.61
  492.3 18.5 %collective-permute-done.29 = bf16[288,2304]{1,0:T(8,128)(2,1)S(1)} collective-permute-done((bf16[288,2304]{1,0:T(8,128)(2,1)S(1)}, bf16[288,2304]{1,0:T(8,128)(2,1)S(1)}, u32[]{:S(2)}, u32[]{:S(2)}) %collective-permute-start.29) | collective-permute-done | bytes 1327136 | tf_op jit(solution)/shard_map/ppermute | solution.py:339
  514.1 3.8 collective-permute-done.38.refs_3_
  520.4 6.1 %fusion.6 = f32[2,288,2304]{2,1,0:T(8,128)S(1)} fusion(bf16[2,288,1152]{2,1,0:T(8,128)(2,1)S(1)} %pad_maximum_fusion.4, bf16[2304,1152]{1,0:T(8,128)(2,1)} %param.35), kind=kOutput, calls=%fused_computation.16 | convolution fusion | flops 3057647616 | bytes 11943936 | tf_op jit(solution)/shard_map/re,de->rd/dot_general | solution.py:88
  531.8 18.3 %collective-permute-start.60 = (bf16[36,4608]{1,0:T(8,128)(2,1)S(1)}, bf16[36,4608]{1,0:T(8,128)(2,1)S(1)}, u32[]{:S(2)}, u32[]{:S(2)}) collective-permute-start(bf16[36,4608]{1,0:T(8,128)(2,1)S(1)} %get-tuple-element.307), channel_id=1, source_target_pairs={{0,2},{1,3},{2,0},{3,1},{4,6},{5,7},{6,4},{7,5},{8,10},{9,11},{10,... | collective-permute-start | bytes 995336 | tf_op jit(solution)/shard_map/ppermute | solution.py:333
  554.8 3.8 collective-permute-start.58
  558.6 6.3 %collective-permute-done.60 = bf16[36,4608]{1,0:T(8,128)(2,1)S(1)} collective-permute-done((bf16[36,4608]{1,0:T(8,128)(2,1)S(1)}, bf16[36,4608]{1,0:T(8,128)(2,1)S(1)}, u32[]{:S(2)}, u32[]{:S(2)}) %collective-permute-start.60) | collective-permute-done | bytes 331808 | tf_op jit(solution)/shard_map/ppermute | solution.py:333
  564.9 3.1 collective-permute-start.55
  567.9 3.2 collective-permute-start.53
  571.1 3.8 collective-permute-start.54
  576.7 2.8 collective-permute-start.52
  579.5 6.8 %collective-permute-start.51 = (bf16[36,1152]{1,0:T(8,128)(2,1)S(1)}, bf16[36,1152]{1,0:T(8,128)(2,1)S(1)}, u32[]{:S(2)}, u32[]{:S(2)}) collective-permute-start(bf16[36,1152]{1,0:T(8,128)(2,1)S(1)} %get-tuple-element.289), channel_id=1, source_target_pairs={{0,2},{1,3},{2,0},{3,1},{4,6},{5,7},{6,4},{7,5},{8,10},{9,11},{10,... | collective-permute-start | bytes 248840 | tf_op jit(solution)/shard_map/ppermute | solution.py:333
  586.3 3.3 collective-permute-done.54
  591.0 3.8 collective-permute-done.51
  594.9 4.4 collective-permute-start.43
  607.3 3.3 collective-permute-done.44
  (446 shorter events, 180.6 us)
Async XLA Ops:
  21.2 17.9 %collective-permute-start.1 = (bf16[288,1152]{1,0:T(8,128)(2,1)S(1)}, bf16[288,1152]{1,0:T(8,128)(2,1)}, u32[]{:S(2)}, u32[]{:S(2)}) collective-permute-start(bf16[288,1152]{1,0:T(8,128)(2,1)S(1)} %get-tuple-element.169), channel_id=1, source_target_pairs={{0,1},{1,0},{2,5},{3,4},{4,3},{5,2},{6,7},{7,6},{8,9},{9,8},{10,13... | collective-permute-start | bytes 1990664 | tf_op jit(solution)/shard_map/ppermute | solution.py:120
  53.1 39.2 %collective-permute-start.4 = (bf16[576,2304]{1,0:T(8,128)(2,1)}, bf16[576,2304]{1,0:T(8,128)(2,1)}, u32[]{:S(2)}, u32[]{:S(2)}) collective-permute-start(bf16[576,2304]{1,0:T(8,128)(2,1)} %slice.279), channel_id=1, source_target_pairs={{0,4},{1,5},{2,6},{3,7},{4,0},{5,1},{6,2},{7,3},{8,12},{9,13},{10,... | collective-permute-start | bytes 7962632 | tf_op jit(solution)/shard_map/ppermute | solution.py:143
  73.8 18.3 %collective-permute-start.8 = (f32[32,128]{1,0:T(8,128)S(1)}, f32[32,128]{1,0:T(8,128)S(1)}, u32[]{:S(2)}, u32[]{:S(2)}) collective-permute-start(f32[32,128]{1,0:T(8,128)S(1)} %get-tuple-element.454), channel_id=1, source_target_pairs={{0,0},{1,1},{2,4},{3,5},{4,2},{5,3},{6,6},{7,7},{8,8},{9,9},{10,12... | collective-permute-start | bytes 49160 | tf_op jit(solution)/shard_map/ppermute | solution.py:120
  74.4 17.5 %collective-permute-start.9 = (f32[32,128]{1,0:T(8,128)S(1)}, f32[32,128]{1,0:T(8,128)S(1)}, u32[]{:S(2)}, u32[]{:S(2)}) collective-permute-start(f32[32,128]{1,0:T(8,128)S(1)} %get-tuple-element.455), channel_id=1, source_target_pairs={{0,1},{1,0},{2,5},{3,4},{4,3},{5,2},{6,7},{7,6},{8,9},{9,8},{10,13... | collective-permute-start | bytes 49160 | tf_op jit(solution)/shard_map/ppermute | solution.py:120
  80.0 78.2 %collective-permute-start.7 = (bf16[288,2304]{1,0:T(8,128)(2,1)}, bf16[288,2304]{1,0:T(8,128)(2,1)}, u32[]{:S(2)}, u32[]{:S(2)}) collective-permute-start(bf16[288,2304]{1,0:T(8,128)(2,1)} %get-tuple-element.422), channel_id=1, source_target_pairs={{0,1},{1,0},{2,5},{3,4},{4,3},{5,2},{6,7},{7,6},{8,9},{9,8},{10,13... | collective-permute-start | bytes 3981320 | tf_op jit(solution)/shard_map/ppermute | solution.py:120
  80.0 78.2 %collective-permute-start.6 = (bf16[288,2304]{1,0:T(8,128)(2,1)}, bf16[288,2304]{1,0:T(8,128)(2,1)}, u32[]{:S(2)}, u32[]{:S(2)}) collective-permute-start(bf16[288,2304]{1,0:T(8,128)(2,1)} %get-tuple-element.423), channel_id=1, source_target_pairs={{0,0},{1,1},{2,4},{3,5},{4,2},{5,3},{6,6},{7,7},{8,8},{9,9},{10,12... | collective-permute-start | bytes 3981320 | tf_op jit(solution)/shard_map/ppermute | solution.py:120
  187.7 19.2 %collective-permute-start.11 = (bf16[2304,1152]{1,0:T(8,128)(2,1)}, bf16[2304,1152]{1,0:T(8,128)(2,1)}, u32[]{:S(2)}, u32[]{:S(2)}) collective-permute-start(bf16[2304,1152]{1,0:T(8,128)(2,1)} %get-tuple-element.178), channel_id=1, source_target_pairs={{0,4},{4,0},{8,12},{12,8},{16,20},{20,16},{24,28},{28,24},{1,5},{5... | collective-permute-start | bytes 15925256 | tf_op jit(solution)/shard_map/ppermute | solution.py:339
  225.5 37.9 %collective-permute-start.12 = (bf16[576,4608]{1,0:T(8,128)(2,1)}, bf16[576,4608]{1,0:T(8,128)(2,1)}, u32[]{:S(2)}, u32[]{:S(2)}) collective-permute-start(bf16[576,4608]{1,0:T(8,128)(2,1)} %get-tuple-element.185), channel_id=1, source_target_pairs={{0,4},{4,0},{8,12},{12,8},{16,20},{20,16},{24,28},{28,24},{1,5},{5... | collective-permute-start | bytes 15925256 | tf_op jit(solution)/shard_map/ppermute | solution.py:339
  238.7 95.3 %collective-permute-start.20 = (bf16[1152,1152]{1,0:T(8,128)(2,1)}, bf16[1152,1152]{1,0:T(8,128)(2,1)}, u32[]{:S(2)}, u32[]{:S(2)}) collective-permute-start(bf16[1152,1152]{1,0:T(8,128)(2,1)} %fusion.5), channel_id=1, source_target_pairs={{0,8},{4,12},{8,0},{12,4},{16,24},{20,28},{24,16},{28,20},{1,9},{5... | collective-permute-start | bytes 7962632 | tf_op jit(solution)/shard_map/ppermute | solution.py:339
  277.9 53.9 %collective-permute-start.21 = (bf16[576,1152]{1,0:T(8,128)(2,1)}, bf16[576,1152]{1,0:T(8,128)(2,1)}, u32[]{:S(2)}, u32[]{:S(2)}) collective-permute-start(bf16[576,1152]{1,0:T(8,128)(2,1)} %get-tuple-element.198), channel_id=1, source_target_pairs={{0,4},{4,0},{8,12},{12,8},{16,20},{20,16},{24,28},{28,24},{1,5},{5... | collective-permute-start | bytes 3981320 | tf_op jit(solution)/shard_map/ppermute | solution.py:339
  285.2 41.4 %collective-permute-start.17 = (f32[2,4,64,1]{2,1,3,0:T(4,128)}, f32[2,4,64,1]{2,1,3,0:T(4,128)S(1)}, u32[]{:S(2)}, u32[]{:S(2)}) collective-permute-start(f32[2,4,64,1]{2,1,3,0:T(4,128)} %get-tuple-element.446), channel_id=1, source_target_pairs={{0,1},{1,2},{2,3},{4,5},{5,6},{6,7},{8,9},{9,10},{10,11},{12,13},{... | collective-permute-start | bytes 6152 | tf_op jit(solution)/shard_map/ppermute | solution.py:37
  287.6 39.0 %collective-permute-start.18 = (f32[2,4,64,1]{2,1,3,0:T(4,128)}, f32[2,4,64,1]{2,1,3,0:T(4,128)S(1)}, u32[]{:S(2)}, u32[]{:S(2)}) collective-permute-start(f32[2,4,64,1]{2,1,3,0:T(4,128)} %get-tuple-element.447), channel_id=1, source_target_pairs={{1,0},{2,1},{3,2},{5,4},{6,5},{7,6},{9,8},{10,9},{11,10},{13,12},{... | collective-permute-start | bytes 6152 | tf_op jit(solution)/shard_map/ppermute | solution.py:40
  291.5 94.9 %collective-permute-start.19 = (bf16[288,4608]{1,0:T(8,128)(2,1)}, bf16[288,4608]{1,0:T(8,128)(2,1)S(1)}, u32[]{:S(2)}, u32[]{:S(2)}) collective-permute-start(bf16[288,4608]{1,0:T(8,128)(2,1)} %fusion.4), channel_id=1, source_target_pairs={{0,16},{4,20},{8,24},{12,28},{16,0},{20,4},{24,8},{28,12},{1,17},{... | collective-permute-start | bytes 7962632 | tf_op jit(solution)/shard_map/ppermute | solution.py:339
  376.9 13.8 %collective-permute-start.22 = (bf16[576,2304]{1,0:T(8,128)(2,1)}, bf16[576,2304]{1,0:T(8,128)(2,1)S(1)}, u32[]{:S(2)}, u32[]{:S(2)}) collective-permute-start(bf16[576,2304]{1,0:T(8,128)(2,1)} %get-tuple-element.215), channel_id=1, source_target_pairs={{0,4},{1,5},{2,6},{3,7},{4,0},{5,1},{6,2},{7,3},{8,12},{9,13},{10,... | collective-permute-start | bytes 7962632 | tf_op jit(solution)/shard_map/ppermute | solution.py:143
  380.0 31.9 %collective-permute-start.26 = (bf16[576,1152]{1,0:T(8,128)(2,1)}, bf16[576,1152]{1,0:T(8,128)(2,1)}, u32[]{:S(2)}, u32[]{:S(2)}) collective-permute-start(bf16[576,1152]{1,0:T(8,128)(2,1)} %fusion.19), channel_id=1, source_target_pairs={{0,16},{4,20},{8,24},{12,28},{16,0},{20,4},{24,8},{28,12},{1,17},{... | collective-permute-start | bytes 3981320 | tf_op jit(solution)/shard_map/ppermute | solution.py:339
  386.2 32.6 %collective-permute-start.25 = (bf16[576,1152]{1,0:T(8,128)(2,1)}, bf16[576,1152]{1,0:T(8,128)(2,1)}, u32[]{:S(2)}, u32[]{:S(2)}) collective-permute-start(bf16[576,1152]{1,0:T(8,128)(2,1)} %get-tuple-element.211), channel_id=1, source_target_pairs={{0,4},{4,0},{8,12},{12,8},{16,20},{20,16},{24,28},{28,24},{1,5},{5... | collective-permute-start | bytes 3981320 | tf_op jit(solution)/shard_map/ppermute | solution.py:339
  401.6 37.6 %collective-permute-start.23 = (bf16[576,2304]{1,0:T(8,128)(2,1)}, bf16[576,2304]{1,0:T(8,128)(2,1)S(1)}, u32[]{:S(2)}, u32[]{:S(2)}) collective-permute-start(bf16[576,2304]{1,0:T(8,128)(2,1)} %get-tuple-element.218), channel_id=1, source_target_pairs={{0,4},{4,0},{8,12},{12,8},{16,20},{20,16},{24,28},{28,24},{1,5},{5... | collective-permute-start | bytes 7962632 | tf_op jit(solution)/shard_map/ppermute | solution.py:339
  404.2 18.0 %collective-permute-start.24 = (bf16[288,1152]{1,0:T(8,128)(2,1)}, bf16[288,1152]{1,0:T(8,128)(2,1)S(1)}, u32[]{:S(2)}, u32[]{:S(2)}) collective-permute-start(bf16[288,1152]{1,0:T(8,128)(2,1)} %fusion.26), channel_id=1, source_target_pairs={{0,8},{4,12},{8,0},{12,4},{16,24},{20,28},{24,16},{28,20},{1,9},{5... | collective-permute-start | bytes 1990664 | tf_op jit(solution)/shard_map/ppermute | solution.py:339
  405.9 64.1 %collective-permute-start.36 = (bf16[144,4608]{1,0:T(8,128)(2,1)}, bf16[144,4608]{1,0:T(8,128)(2,1)}, u32[]{:S(2)}, u32[]{:S(2)}) collective-permute-start(bf16[144,4608]{1,0:T(8,128)(2,1)} %fusion.18), channel_id=1, source_target_pairs={{0,8},{4,12},{8,0},{12,4},{16,24},{20,28},{24,16},{28,20},{1,9},{5... | collective-permute-start | bytes 3981320 | tf_op jit(solution)/shard_map/ppermute | solution.py:339
  415.4 51.9 %collective-permute-start.32 = (bf16[144,1152]{1,0:T(8,128)(2,1)}, bf16[144,1152]{1,0:T(8,128)(2,1)}, u32[]{:S(2)}, u32[]{:S(2)}) collective-permute-start(bf16[144,1152]{1,0:T(8,128)(2,1)} %get-tuple-element.223), channel_id=1, source_target_pairs={{0,3},{1,0},{2,1},{3,2},{4,7},{5,4},{6,5},{7,6},{8,11},{9,8},{10,9... | collective-permute-start | bytes 995336 | tf_op jit(solution)/shard_map/ppermute | solution.py:333
  418.8 38.6 %collective-permute-start.30 = (bf16[144,1152]{1,0:T(8,128)(2,1)S(1)}, bf16[144,1152]{1,0:T(8,128)(2,1)S(1)}, u32[]{:S(2)}, u32[]{:S(2)}) collective-permute-start(bf16[144,1152]{1,0:T(8,128)(2,1)S(1)} %get-tuple-element.238), channel_id=1, source_target_pairs={{0,1},{1,2},{2,3},{3,0},{4,5},{5,6},{6,7},{7,4},{8,9},{9,10},{10,1... | collective-permute-start | bytes 995336 | tf_op jit(solution)/shard_map/ppermute | solution.py:333
  422.2 52.3 %collective-permute-start.35 = (bf16[288,1152]{1,0:T(8,128)(2,1)}, bf16[288,1152]{1,0:T(8,128)(2,1)}, u32[]{:S(2)}, u32[]{:S(2)}) collective-permute-start(bf16[288,1152]{1,0:T(8,128)(2,1)} %fusion.25), channel_id=1, source_target_pairs={{0,16},{4,20},{8,24},{12,28},{16,0},{20,4},{24,8},{28,12},{1,17},{... | collective-permute-start | bytes 1990664 | tf_op jit(solution)/shard_map/ppermute | solution.py:339
  439.3 25.9 %collective-permute-start.31 = (bf16[144,1152]{1,0:T(8,128)(2,1)}, bf16[144,1152]{1,0:T(8,128)(2,1)}, u32[]{:S(2)}, u32[]{:S(2)}) collective-permute-start(bf16[144,1152]{1,0:T(8,128)(2,1)} %get-tuple-element.239), channel_id=1, source_target_pairs={{0,2},{1,3},{2,0},{3,1},{4,6},{5,7},{6,4},{7,5},{8,10},{9,11},{10,... | collective-permute-start | bytes 995336 | tf_op jit(solution)/shard_map/ppermute | solution.py:333
  457.4 29.8 %collective-permute-start.34 = (bf16[1152,1152]{1,0:T(8,128)(2,1)}, bf16[1152,1152]{1,0:T(8,128)(2,1)}, u32[]{:S(2)}, u32[]{:S(2)}) collective-permute-start(bf16[1152,1152]{1,0:T(8,128)(2,1)} %get-tuple-element.237), channel_id=1, source_target_pairs={{0,4},{4,0},{8,12},{12,8},{16,20},{20,16},{24,28},{28,24},{1,5},{5... | collective-permute-start | bytes 7962632 | tf_op jit(solution)/shard_map/ppermute | solution.py:339
  465.2 15.4 %collective-permute-start.27 = (bf16[288,1152]{1,0:T(8,128)(2,1)}, bf16[288,1152]{1,0:T(8,128)(2,1)S(1)}, u32[]{:S(2)}, u32[]{:S(2)}) collective-permute-start(bf16[288,1152]{1,0:T(8,128)(2,1)} %get-tuple-element.429), channel_id=1, source_target_pairs={{0,0},{1,1},{4,2},{5,3},{2,4},{3,5},{6,6},{7,7},{8,8},{9,9},{12,10... | collective-permute-start | bytes 1990664 | tf_op jit(solution)/shard_map/ppermute | solution.py:127
  467.2 19.3 %collective-permute-start.28 = (bf16[288,1152]{1,0:T(8,128)(2,1)}, bf16[288,1152]{1,0:T(8,128)(2,1)S(1)}, u32[]{:S(2)}, u32[]{:S(2)}) collective-permute-start(bf16[288,1152]{1,0:T(8,128)(2,1)} %get-tuple-element.430), channel_id=1, source_target_pairs={{1,0},{0,1},{5,2},{4,3},{3,4},{2,5},{7,6},{6,7},{9,8},{8,9},{13,10... | collective-permute-start | bytes 1990664 | tf_op jit(solution)/shard_map/ppermute | solution.py:127
  470.0 41.9 %collective-permute-start.39 = (bf16[144,1152]{1,0:T(8,128)(2,1)S(1)}, bf16[144,1152]{1,0:T(8,128)(2,1)S(1)}, u32[]{:S(2)}, u32[]{:S(2)}) collective-permute-start(bf16[144,1152]{1,0:T(8,128)(2,1)S(1)} %copy-done.35), channel_id=1, source_target_pairs={{0,16},{4,20},{8,24},{12,28},{16,0},{20,4},{24,8},{28,12},{1,17},{... | collective-permute-start | bytes 995336 | tf_op jit(solution)/shard_map/ppermute | solution.py:339
  474.5 17.4 %collective-permute-start.33 = (f32[256,128]{1,0:T(8,128)S(1)}, f32[256,128]{1,0:T(8,128)S(1)}, u32[]{:S(2)}, u32[]{:S(2)}) collective-permute-start(f32[256,128]{1,0:T(8,128)S(1)} %bitcast.565), channel_id=1, source_target_pairs={{0,4},{4,0},{8,12},{12,8},{16,20},{20,16},{24,28},{28,24},{1,5},{5... | collective-permute-start | bytes 393224 | tf_op jit(solution)/shard_map/ppermute | solution.py:339
  480.5 84.3 %collective-permute-start.61 = (bf16[36,4608]{1,0:T(8,128)(2,1)S(1)}, bf16[36,4608]{1,0:T(8,128)(2,1)}, u32[]{:S(2)}, u32[]{:S(2)}) collective-permute-start(bf16[36,4608]{1,0:T(8,128)(2,1)S(1)} %get-tuple-element.250), channel_id=1, source_target_pairs={{0,3},{1,0},{2,1},{3,2},{4,7},{5,4},{6,5},{7,6},{8,11},{9,8},{10,9... | collective-permute-start | bytes 995336 | tf_op jit(solution)/shard_map/ppermute | solution.py:333
  486.5 24.3 %collective-permute-start.29 = (bf16[288,2304]{1,0:T(8,128)(2,1)S(1)}, bf16[288,2304]{1,0:T(8,128)(2,1)S(1)}, u32[]{:S(2)}, u32[]{:S(2)}) collective-permute-start(bf16[288,2304]{1,0:T(8,128)(2,1)S(1)} %copy-done.32), channel_id=1, source_target_pairs={{0,8},{4,12},{8,0},{12,4},{16,24},{20,28},{24,16},{28,20},{1,9},{5... | collective-permute-start | bytes 3981320 | tf_op jit(solution)/shard_map/ppermute | solution.py:339
  487.2 30.7 %collective-permute-start.38 = (bf16[144,1152]{1,0:T(8,128)(2,1)}, bf16[144,1152]{1,0:T(8,128)(2,1)S(1)}, u32[]{:S(2)}, u32[]{:S(2)}) collective-permute-start(bf16[144,1152]{1,0:T(8,128)(2,1)} %fusion.37), channel_id=1, source_target_pairs={{0,8},{4,12},{8,0},{12,4},{16,24},{20,28},{24,16},{28,20},{1,9},{5... | collective-permute-start | bytes 995336 | tf_op jit(solution)/shard_map/ppermute | solution.py:339
  491.9 34.6 %collective-permute-start.37 = (bf16[576,1152]{1,0:T(8,128)(2,1)}, bf16[576,1152]{1,0:T(8,128)(2,1)S(1)}, u32[]{:S(2)}, u32[]{:S(2)}) collective-permute-start(bf16[576,1152]{1,0:T(8,128)(2,1)} %fusion.16), channel_id=1, source_target_pairs={{0,16},{4,20},{8,24},{12,28},{16,0},{20,4},{24,8},{28,12},{1,17},{... | collective-permute-start | bytes 3981320 | tf_op jit(solution)/shard_map/ppermute | solution.py:339
  510.8 44.0 %collective-permute-start.59 = (bf16[36,4608]{1,0:T(8,128)(2,1)S(1)}, bf16[36,4608]{1,0:T(8,128)(2,1)}, u32[]{:S(2)}, u32[]{:S(2)}) collective-permute-start(bf16[36,4608]{1,0:T(8,128)(2,1)S(1)} %get-tuple-element.306), channel_id=1, source_target_pairs={{0,1},{1,2},{2,3},{3,0},{4,5},{5,6},{6,7},{7,4},{8,9},{9,10},{10,1... | collective-permute-start | bytes 995336 | tf_op jit(solution)/shard_map/ppermute | solution.py:333
  511.9 19.8 %collective-permute-start.42 = (f32[128,128]{1,0:T(8,128)S(1)}, f32[128,128]{1,0:T(8,128)S(1)}, u32[]{:S(2)}, u32[]{:S(2)}) collective-permute-start(f32[128,128]{1,0:T(8,128)S(1)} %bitcast_add_fusion), channel_id=1, source_target_pairs={{0,16},{4,20},{8,24},{12,28},{16,0},{20,4},{24,8},{28,12},{1,17},{... | collective-permute-start | bytes 196616 | tf_op jit(solution)/shard_map/ppermute | solution.py:339
  517.9 32.2 %collective-permute-start.41 = (bf16[144,2304]{1,0:T(8,128)(2,1)}, bf16[144,2304]{1,0:T(8,128)(2,1)S(1)}, u32[]{:S(2)}, u32[]{:S(2)}) collective-permute-start(bf16[144,2304]{1,0:T(8,128)(2,1)} %fusion.24), channel_id=1, source_target_pairs={{0,16},{4,20},{8,24},{12,28},{16,0},{20,4},{24,8},{28,12},{1,17},{... | collective-permute-start | bytes 1990664 | tf_op jit(solution)/shard_map/ppermute | solution.py:339
  528.6 21.6 %collective-permute-start.40 = (bf16[288,1152]{1,0:T(8,128)(2,1)S(1)}, bf16[288,1152]{1,0:T(8,128)(2,1)S(1)}, u32[]{:S(2)}, u32[]{:S(2)}) collective-permute-start(bf16[288,1152]{1,0:T(8,128)(2,1)S(1)} %fusion.23), channel_id=1, source_target_pairs={{0,8},{4,12},{8,0},{12,4},{16,24},{20,28},{24,16},{28,20},{1,9},{5... | collective-permute-start | bytes 1990664 | tf_op jit(solution)/shard_map/ppermute | solution.py:339
  531.8 33.1 %collective-permute-start.60 = (bf16[36,4608]{1,0:T(8,128)(2,1)S(1)}, bf16[36,4608]{1,0:T(8,128)(2,1)S(1)}, u32[]{:S(2)}, u32[]{:S(2)}) collective-permute-start(bf16[36,4608]{1,0:T(8,128)(2,1)S(1)} %get-tuple-element.307), channel_id=1, source_target_pairs={{0,2},{1,3},{2,0},{3,1},{4,6},{5,7},{6,4},{7,5},{8,10},{9,11},{10,... | collective-permute-start | bytes 995336 | tf_op jit(solution)/shard_map/ppermute | solution.py:333
  550.1 17.8 %collective-permute-start.56 = (bf16[36,1152]{1,0:T(8,128)(2,1)S(1)}, bf16[36,1152]{1,0:T(8,128)(2,1)S(1)}, u32[]{:S(2)}, u32[]{:S(2)}) collective-permute-start(bf16[36,1152]{1,0:T(8,128)(2,1)S(1)} %get-tuple-element.300), channel_id=1, source_target_pairs={{0,1},{1,2},{2,3},{3,0},{4,5},{5,6},{6,7},{7,4},{8,9},{9,10},{10,1... | collective-permute-start | bytes 248840 | tf_op jit(solution)/shard_map/ppermute | solution.py:333
  550.2 20.9 %collective-permute-start.46 = (f32[64,128]{1,0:T(8,128)S(1)}, f32[64,128]{1,0:T(8,128)S(1)}, u32[]{:S(2)}, u32[]{:S(2)}) collective-permute-start(f32[64,128]{1,0:T(8,128)S(1)} %bitcast_add_fusion.1), channel_id=1, source_target_pairs={{0,8},{4,12},{8,0},{12,4},{16,24},{20,28},{24,16},{28,20},{1,9},{5... | collective-permute-start | bytes 98312 | tf_op jit(solution)/shard_map/ppermute | solution.py:339
  554.8 24.7 %collective-permute-start.58 = (bf16[36,1152]{1,0:T(8,128)(2,1)S(1)}, bf16[36,1152]{1,0:T(8,128)(2,1)S(1)}, u32[]{:S(2)}, u32[]{:S(2)}) collective-permute-start(bf16[36,1152]{1,0:T(8,128)(2,1)S(1)} %get-tuple-element.260), channel_id=1, source_target_pairs={{0,3},{1,0},{2,1},{3,2},{4,7},{5,4},{6,5},{7,6},{8,11},{9,8},{10,9... | collective-permute-start | bytes 248840 | tf_op jit(solution)/shard_map/ppermute | solution.py:333
  564.9 11.8 %collective-permute-start.57 = (bf16[36,1152]{1,0:T(8,128)(2,1)S(1)}, bf16[36,1152]{1,0:T(8,128)(2,1)S(1)}, u32[]{:S(2)}, u32[]{:S(2)}) collective-permute-start(bf16[36,1152]{1,0:T(8,128)(2,1)S(1)} %get-tuple-element.301), channel_id=1, source_target_pairs={{0,2},{1,3},{2,0},{3,1},{4,6},{5,7},{6,4},{7,5},{8,10},{9,11},{10,... | collective-permute-start | bytes 248840 | tf_op jit(solution)/shard_map/ppermute | solution.py:333
  564.9 26.1 %collective-permute-start.55 = (bf16[36,2304]{1,0:T(8,128)(2,1)S(1)}, bf16[36,2304]{1,0:T(8,128)(2,1)S(1)}, u32[]{:S(2)}, u32[]{:S(2)}) collective-permute-start(bf16[36,2304]{1,0:T(8,128)(2,1)S(1)} %get-tuple-element.272), channel_id=1, source_target_pairs={{0,3},{1,0},{2,1},{3,2},{4,7},{5,4},{6,5},{7,6},{8,11},{9,8},{10,9... | collective-permute-start | bytes 497672 | tf_op jit(solution)/shard_map/ppermute | solution.py:333
  571.1 18.5 %collective-permute-start.54 = (bf16[36,2304]{1,0:T(8,128)(2,1)S(1)}, bf16[36,2304]{1,0:T(8,128)(2,1)S(1)}, u32[]{:S(2)}, u32[]{:S(2)}) collective-permute-start(bf16[36,2304]{1,0:T(8,128)(2,1)S(1)} %get-tuple-element.295), channel_id=1, source_target_pairs={{0,2},{1,3},{2,0},{3,1},{4,6},{5,7},{6,4},{7,5},{8,10},{9,11},{10,... | collective-permute-start | bytes 497672 | tf_op jit(solution)/shard_map/ppermute | solution.py:333
  576.7 18.1 %collective-permute-start.52 = (bf16[36,1152]{1,0:T(8,128)(2,1)S(1)}, bf16[36,1152]{1,0:T(8,128)(2,1)S(1)}, u32[]{:S(2)}, u32[]{:S(2)}) collective-permute-start(bf16[36,1152]{1,0:T(8,128)(2,1)S(1)} %get-tuple-element.265), channel_id=1, source_target_pairs={{0,3},{1,0},{2,1},{3,2},{4,7},{5,4},{6,5},{7,6},{8,11},{9,8},{10,9... | collective-permute-start | bytes 248840 | tf_op jit(solution)/shard_map/ppermute | solution.py:333
  579.5 15.4 %collective-permute-start.51 = (bf16[36,1152]{1,0:T(8,128)(2,1)S(1)}, bf16[36,1152]{1,0:T(8,128)(2,1)S(1)}, u32[]{:S(2)}, u32[]{:S(2)}) collective-permute-start(bf16[36,1152]{1,0:T(8,128)(2,1)S(1)} %get-tuple-element.289), channel_id=1, source_target_pairs={{0,2},{1,3},{2,0},{3,1},{4,6},{5,7},{6,4},{7,5},{8,10},{9,11},{10,... | collective-permute-start | bytes 248840 | tf_op jit(solution)/shard_map/ppermute | solution.py:333
  589.6 13.5 %collective-permute-start.49 = (f32[16,128]{1,0:T(8,128)S(1)}, f32[16,128]{1,0:T(8,128)S(1)}, u32[]{:S(2)}, u32[]{:S(2)}) collective-permute-start(f32[16,128]{1,0:T(8,128)S(1)} %get-tuple-element.278), channel_id=1, source_target_pairs={{0,3},{1,0},{2,1},{3,2},{4,7},{5,4},{6,5},{7,6},{8,11},{9,8},{10,9... | collective-permute-start | bytes 24584 | tf_op jit(solution)/shard_map/ppermute | solution.py:333
  591.0 19.5 %collective-permute-start.45 = (bf16[72,1152]{1,0:T(8,128)(2,1)S(1)}, bf16[72,1152]{1,0:T(8,128)(2,1)S(1)}, u32[]{:S(2)}, u32[]{:S(2)}) collective-permute-start(bf16[72,1152]{1,0:T(8,128)(2,1)S(1)} %get-tuple-element.276), channel_id=1, source_target_pairs={{0,3},{1,0},{2,1},{3,2},{4,7},{5,4},{6,5},{7,6},{8,11},{9,8},{10,9... | collective-permute-start | bytes 497672 | tf_op jit(solution)/shard_map/ppermute | solution.py:333
  594.9 12.4 %collective-permute-start.43 = (bf16[72,1152]{1,0:T(8,128)(2,1)S(1)}, bf16[72,1152]{1,0:T(8,128)(2,1)S(1)}, u32[]{:S(2)}, u32[]{:S(2)}) collective-permute-start(bf16[72,1152]{1,0:T(8,128)(2,1)S(1)} %get-tuple-element.274), channel_id=1, source_target_pairs={{0,1},{1,2},{2,3},{3,0},{4,5},{5,6},{6,7},{7,4},{8,9},{9,10},{10,1... | collective-permute-start | bytes 497672 | tf_op jit(solution)/shard_map/ppermute | solution.py:333
  (86 other events, 1097.6 us)
